TPU v7x, 32 devices: a whole 2x2x4 slice. The times are simulated.
32 devices in a mesh: dp: 8 (over y, x, core), mp: 4 (over z).
Axes of the slice: x: 2, y: 2, z: 4, core: 2. Of those that a mesh axis runs over, the one named last changes fastest.
Arguments:
- hidden: bfloat16 [24576, 768], P('dp'), may hold values from -6 to 6
- timesteps: int32 [144], P('dp'), may hold values from 0 to 999
- cotangent: bfloat16 [24576, 768], P('dp'), may hold values from -6 to 6
- time_table: bfloat16 [1000, 768], replicated, may hold values from -3 to 3
- first_gain: float32 [768], replicated, may hold values from 0.25 to 1.75
- first_shift: float32 [768], replicated, may hold values from -1.5 to 1.5
- qkv_weight: bfloat16 [3, 768, 768], P(None, None, 'mp'), may hold values from -0.21875 to 0.21875
- out_weight: bfloat16 [768, 768], P('mp'), may hold values from -0.875 to 0.875
- out_bias: float32 [768], replicated, may hold values from -1.5 to 1.5
- second_gain: float32 [768], replicated, may hold values from 0.25 to 1.75
- second_shift: float32 [768], replicated, may hold values from -1.5 to 1.5
- up_weight: bfloat16 [768, 3072], P(None, 'mp'), may hold values from -0.21875 to 0.21875
- up_bias: float32 [3072], P('mp'), may hold values from -2.5 to 2.5
- down_weight: bfloat16 [3072, 768], P('mp'), may hold values from -0.15625 to 0.15625
- down_bias: float32 [768], replicated, may hold values from -1.5 to 1.5
Outputs:
- output: bfloat16 [24576, 768], P('dp')
- grad_hidden: bfloat16 [24576, 768], P('dp')
- grad_table: float32 [1000, 768], P(None, 'mp')
- grad_first_gain: float32 [768], replicated
- grad_first_shift: float32 [768], replicated
- grad_qkv_weight: float32 [3, 768, 768], P(None, 'dp', 'mp')
- grad_out_weight: float32 [768, 768], P('mp', 'dp')
- grad_out_bias: float32 [768], replicated
- grad_second_gain: float32 [768], replicated
- grad_second_shift: float32 [768], replicated
- grad_up_weight: float32 [768, 3072], P('dp', 'mp')
- grad_up_bias: float32 [3072], P('mp')
- grad_down_weight: float32 [3072, 768], P('mp', 'dp')
- grad_down_bias: float32 [768], replicated
All inputs are finite; a program needn't handle non-finite values.
Results may differ from a plain program's by a relative error of at most 0.02.
Values may be sent and summed in bfloat16 or wider, within the bound.
A program may use at most 192 MiB of HBM per device.

v0:
```python
from functools import partial

import jax
import jax.numpy as jnp
from jax import lax
from jax.sharding import PartitionSpec as P

HD = 64
LEN_A = 128
LEN_B = 256
BLOCK = 512


def layer_norm(rows_in, gain_vec, shift_vec):
    centre = jnp.mean(rows_in, axis=-1, keepdims=True)
    offset = rows_in - centre
    spread = jnp.mean(offset * offset, axis=-1, keepdims=True)
    return offset * lax.rsqrt(spread + 1e-05) * gain_vec + shift_vec


def block_scores(queries, key_rows, seg_len):
    scores = jnp.einsum(
        "qhd,khd->hqk", queries, key_rows, preferred_element_type=jnp.float32
    ) * HD ** (-0.5)
    segment = lax.broadcasted_iota(jnp.int32, (BLOCK,), 0) // seg_len
    same_row = segment[:, None] == segment[None, :]
    return jnp.where(same_row[None], scores, -1000000000.0)


def attend_block(queries, key_rows, value_rows, seg_len):
    scores = block_scores(queries, key_rows, seg_len)
    log_total = jax.nn.logsumexp(scores, axis=-1)
    attn_probs = jnp.exp(scores - log_total[..., None]).astype(jnp.bfloat16)
    context = jnp.einsum("hqk,khd->qhd", attn_probs, value_rows, preferred_element_type=jnp.float32)
    return (context, log_total)


def attend_pair(pieces):
    queries, key_rows, value_rows = pieces
    lead_out, lead_log = attend_block(queries[0], key_rows[0], value_rows[0], LEN_A)
    tail_out, tail_log = attend_block(queries[1], key_rows[1], value_rows[1], LEN_B)
    return (jnp.stack([lead_out, tail_out]), jnp.stack([lead_log, tail_log]))


def attend_back_block(queries, key_rows, value_rows, grad_out, log_total, seg_len):
    scores = block_scores(queries, key_rows, seg_len)
    attn_probs = jnp.exp(scores - log_total[..., None])
    grad_probs = jnp.einsum(
        "qhd,khd->hqk", grad_out, value_rows, preferred_element_type=jnp.float32
    )
    grad_values = jnp.einsum(
        "hqk,qhd->khd",
        attn_probs.astype(jnp.bfloat16),
        grad_out,
        preferred_element_type=jnp.float32,
    )
    inner_sum = jnp.sum(attn_probs * grad_probs, axis=-1, keepdims=True)
    grad_scores = (attn_probs * (grad_probs - inner_sum)).astype(jnp.bfloat16)
    scale = HD ** (-0.5)
    grad_queries = (
        jnp.einsum("hqk,khd->qhd", grad_scores, key_rows, preferred_element_type=jnp.float32)
        * scale
    )
    grad_keys = (
        jnp.einsum("hqk,qhd->khd", grad_scores, queries, preferred_element_type=jnp.float32) * scale
    )
    return (grad_queries, grad_keys, grad_values)


def attend_back_pair(pieces):
    queries, key_rows, value_rows, grad_out, log_total = pieces
    lead = attend_back_block(
        queries[0], key_rows[0], value_rows[0], grad_out[0], log_total[0], LEN_A
    )
    tail = attend_back_block(
        queries[1], key_rows[1], value_rows[1], grad_out[1], log_total[1], LEN_B
    )
    return tuple((jnp.stack([lead[index], tail[index]]) for index in range(3)))


def local(
    hidden,
    timesteps,
    cotangent,
    time_table,
    first_gain,
    first_shift,
    qkv_weight,
    out_weight,
    out_bias,
    second_gain,
    second_shift,
    up_weight,
    up_bias,
    down_weight,
    down_bias,
):
    count = hidden.shape[0]
    width = hidden.shape[1]
    local_width = qkv_weight.shape[2]
    local_heads = local_width // HD
    pairs_dev = count // (2 * BLOCK)
    row_count = timesteps.shape[0]
    members = lax.axis_size("mp")
    row_emb = (
        jnp.take(time_table, timesteps, axis=0).astype(jnp.float32).reshape(pairs_dev, 6, width)
    )
    lead_emb = jnp.broadcast_to(row_emb[:, :4, None, :], (pairs_dev, 4, LEN_A, width)).reshape(
        pairs_dev, BLOCK, width
    )
    tail_emb = jnp.broadcast_to(row_emb[:, 4:, None, :], (pairs_dev, 2, LEN_B, width)).reshape(
        pairs_dev, BLOCK, width
    )
    stream_in = jnp.concatenate([lead_emb, tail_emb], axis=1).reshape(count, width) + hidden.astype(
        jnp.float32
    )

    def front(stream_rows):
        normed = layer_norm(stream_rows, first_gain, first_shift).astype(jnp.bfloat16)
        proj = jnp.einsum(
            "td,cde->cte", normed, qkv_weight, preferred_element_type=jnp.float32
        ).astype(jnp.bfloat16)
        shaped = proj.reshape(3, pairs_dev, 2, BLOCK, local_heads, HD)
        context, log_total = lax.map(attend_pair, (shaped[0], shaped[1], shaped[2]))
        return (normed, shaped, context.reshape(count, local_width).astype(jnp.bfloat16), log_total)

    def mlp_front(normed_rows):
        pre_act = jnp.dot(normed_rows, up_weight, preferred_element_type=jnp.float32) + up_bias
        return (pre_act, jax.nn.gelu(pre_act, approximate=True).astype(jnp.bfloat16))

    normed, shaped, context, log_total = front(stream_in)
    attn_part = jnp.dot(context, out_weight, preferred_element_type=jnp.float32)
    attn_total = lax.psum(attn_part.astype(jnp.bfloat16), "mp").astype(jnp.float32)
    middle = stream_in + attn_total + out_bias
    normed_two = layer_norm(middle, second_gain, second_shift).astype(jnp.bfloat16)
    pre_act, activated = mlp_front(normed_two)
    mlp_part = jnp.dot(activated, down_weight, preferred_element_type=jnp.float32)
    result = middle + lax.psum(mlp_part.astype(jnp.bfloat16), "mp").astype(jnp.float32) + down_bias
    grad_top = cotangent.astype(jnp.float32)
    pre_act, activated = mlp_front(lax.optimization_barrier(normed_two))
    grad_down = jnp.einsum("tf,td->fd", activated, cotangent, preferred_element_type=jnp.float32)
    grad_down_bias = jnp.sum(grad_top, axis=0)
    grad_act = jnp.einsum("td,fd->tf", cotangent, down_weight, preferred_element_type=jnp.float32)
    slope_pull = jax.vjp(partial(jax.nn.gelu, approximate=True), pre_act)[1]
    grad_pre = slope_pull(grad_act)[0].astype(jnp.bfloat16)
    grad_up = jnp.einsum("td,tf->df", normed_two, grad_pre, preferred_element_type=jnp.float32)
    grad_up_bias = jnp.sum(grad_pre, axis=0, dtype=jnp.float32)
    norm_part = jnp.einsum("tf,df->td", grad_pre, up_weight, preferred_element_type=jnp.float32)
    norm_grad = lax.psum(norm_part.astype(jnp.bfloat16), "mp").astype(jnp.float32)
    second_pull = jax.vjp(layer_norm, middle, second_gain, second_shift)[1]
    grad_mid, grad_gain_two, grad_shift_two = second_pull(norm_grad)
    grad_mid = grad_mid + grad_top
    grad_mid_low = grad_mid.astype(jnp.bfloat16)
    grad_out_bias = jnp.sum(grad_mid, axis=0)
    normed, shaped, context, log_total = front(lax.optimization_barrier(stream_in))
    grad_out_w = jnp.einsum("te,td->ed", context, grad_mid_low, preferred_element_type=jnp.float32)
    grad_context = jnp.einsum(
        "td,ed->te", grad_mid_low, out_weight, preferred_element_type=jnp.float32
    ).astype(jnp.bfloat16)
    grad_context = grad_context.reshape(pairs_dev, 2, BLOCK, local_heads, HD)
    grad_query, grad_key, grad_value = lax.map(
        attend_back_pair, (shaped[0], shaped[1], shaped[2], grad_context, log_total)
    )
    grad_proj = (
        jnp.stack([grad_query, grad_key, grad_value])
        .reshape(3, count, local_width)
        .astype(jnp.bfloat16)
    )
    grad_qkv = jnp.einsum("td,cte->cde", normed, grad_proj, preferred_element_type=jnp.float32)
    first_part = jnp.einsum(
        "cte,cde->td", grad_proj, qkv_weight, preferred_element_type=jnp.float32
    )
    first_grad = lax.psum(first_part.astype(jnp.bfloat16), "mp").astype(jnp.float32)
    first_pull = jax.vjp(layer_norm, stream_in, first_gain, first_shift)[1]
    grad_in, grad_gain_one, grad_shift_one = first_pull(first_grad)
    grad_in = grad_in + grad_mid
    output = result.astype(jnp.bfloat16)
    columns = width // members
    own_cols = lax.dynamic_slice_in_dim(
        grad_in, lax.axis_index("mp") * columns, columns, 1
    ).reshape(pairs_dev, 2 * BLOCK, columns)
    lead_rows = jnp.sum(own_cols[:, :BLOCK].reshape(pairs_dev, 4, LEN_A, columns), axis=2)
    tail_rows = jnp.sum(own_cols[:, BLOCK:].reshape(pairs_dev, 2, LEN_B, columns), axis=2)
    row_grad = jnp.concatenate([lead_rows, tail_rows], axis=1).reshape(row_count, columns)
    chosen = (
        timesteps[:, None] == lax.broadcasted_iota(jnp.int32, (1, time_table.shape[0]), 1)
    ).astype(jnp.float32)
    table_grad = jnp.dot(
        chosen.T, row_grad, precision=lax.Precision.HIGHEST, preferred_element_type=jnp.float32
    )
    grad_qkv, grad_out_w, grad_up, grad_down = (
        lax.psum_scatter(grad_qkv, "dp", scatter_dimension=1, tiled=True),
        lax.psum_scatter(grad_out_w, "dp", scatter_dimension=1, tiled=True),
        lax.psum_scatter(grad_up, "dp", scatter_dimension=0, tiled=True),
        lax.psum_scatter(grad_down, "dp", scatter_dimension=1, tiled=True),
    )
    (
        table_grad,
        grad_gain_one,
        grad_shift_one,
        grad_out_bias,
        grad_gain_two,
        grad_shift_two,
        grad_up_bias,
        grad_down_bias,
    ) = lax.psum(
        (
            table_grad,
            grad_gain_one,
            grad_shift_one,
            grad_out_bias,
            grad_gain_two,
            grad_shift_two,
            grad_up_bias,
            grad_down_bias,
        ),
        "dp",
    )
    return (
        output,
        grad_in.astype(jnp.bfloat16),
        table_grad,
        grad_gain_one,
        grad_shift_one,
        grad_qkv,
        grad_out_w,
        grad_out_bias,
        grad_gain_two,
        grad_shift_two,
        grad_up,
        grad_up_bias,
        grad_down,
        grad_down_bias,
    )


def solution(mesh):
    return jax.shard_map(
        local,
        mesh=mesh,
        in_specs=(
            P("dp", None),
            P("dp"),
            P("dp", None),
            P(),
            P(),
            P(),
            P(None, None, "mp"),
            P("mp", None),
            P(),
            P(),
            P(),
            P(None, "mp"),
            P("mp"),
            P("mp", None),
            P(),
        ),
        out_specs=(
            P("dp", None),
            P("dp", None),
            P(None, "mp"),
            P(),
            P(),
            P(None, "dp", "mp"),
            P("mp", "dp"),
            P(),
            P(),
            P(),
            P("dp", "mp"),
            P("mp"),
            P("mp", "dp"),
            P(),
        ),
        check_vma=False,
    )
```

profile of v0, /device:TPU:0, one launch (start us, length us, event | category | flops | bytes accessed | tf_op | source)
XLA Modules:
  0.0 1124.5 jit_solution(4650453596753585933)
XLA Ops:
  9.9 2.5 broadcast_in_dim.229
  12.4 6.6 pad_maximum_fusion
  19.0 9.7 fusion.139
  28.8 4.9 multiply_reduce_fusion.4
  35.1 3.5 fusion.104
  40.8 3.5 squeeze.178
  44.3 4.0 squeeze.177
  51.1 31.3 %while.45 = (s32[]{:T(128)}, bf16[3,2,512,3,64]{2,4,3,1,0:T(8,128)(2,1)}, bf16[3,2,512,3,64]{2,1,0,4,3:T(2,128)(2,1)}, bf16[3,2,512,3,64]{2,1,0,4,3:T(2,128)(2,1...) while((s32[]{:T(128)}, bf16[3,2,512,3,64]{2,4,3,1,0:T(8,128)(2,1)}, ...), condition=%wide.region_7.8_spmd, body=%wide.region_2.7_spmd.sunk | while | flops 421284864 | bytes 25809020 | solution.py:124
  53.4 2.4 constant_dynamic-slice_fusion.12
  63.8 2.4 constant_dynamic-slice_fusion.12
  74.2 2.4 constant_dynamic-slice_fusion.12
  82.4 2.5 copy.92
  86.3 3.6 convolution_convert_fusion.2
  90.1 4.2 reduce_sum.301
  94.2 4.8 multiply_reduce_fusion.2
  99.1 5.1 add_convert_fusion
  104.2 2.9 fusion.142
  108.9 4.0 squeeze.181
  112.9 2.5 copy.93
  121.9 143.0 %all-reduce.7.cloned.1.call-done = bf16[3072,768]{1,0:T(8,128)(2,1)} async-done(((bf16[3072,768]{1,0:T(8,128)(2,1)}), bf16[3072,768]{1,0:T(8,128)(2,1)}) %all-reduce.7.cloned.1.call-update) | async-done | bytes 4718608 | tf_op jit(solution)/shard_map/psum | solution.py:133
  264.8 10.0 fusion.138
  274.9 4.9 multiply_reduce_fusion.3
  283.0 6.3 fusion.143
  289.4 12.0 %convert_reduce_fusion.3 = (f32[768]{0:T(1024)}, bf16[3072,768]{1,0:T(8,128)(2,1)S(1)}) fusion(f32[3072,768]{1,0:T(8,128)} %fusion.143, f32[768]{0:T(1024)S(1)} %copy-done.37, bf16[3072,768]{1,0:T(8,128)(2,1)S(1)} %bitcast.369, bf16[768,768]{1,0:T(8,128)(2,1)S(1)} %copy-done.33), kind=kOutput, calls=%fused_computation.213 | convolution fusion | flops 3678141696 | bytes 20060160 | tf_op jit(solution)/shard_map/td,fd->tf/dot_general | solution.py:143
  301.4 2.2 copy-done.39
  303.6 5.5 convolution_convert_fusion
  310.3 24.6 %while.46 = (s32[]{:T(128)}, bf16[3,2,512,3,64]{2,4,3,1,0:T(8,128)(2,1)}, f32[3,2,3,512]{3,2,1,0:T(4,128)S(1)}, bf16[3,2,512,3,64]{2,4,3,1,0:T(8,128)(2,1)}, bf1...) while((s32[]{:T(128)}, ...), condition=%wide.region_22.23_spmd, body=%wide.region_17.22_spmd.sunk | while | flops 421300224 | bytes 23522436 | solution.py:124
  315.7 1.9 fusion.210
  320.5 1.9 fusion.213
  323.9 1.9 fusion.210
  332.1 1.9 fusion.210
  334.9 3.5 copy.103
  338.4 3.9 convert_element_type.176
  342.3 137.8 %all-reduce.9.cloned.1.call-done = bf16[3072,768]{1,0:T(8,128)(2,1)} async-done(((bf16[3072,768]{1,0:T(8,128)(2,1)}), bf16[3072,768]{1,0:T(8,128)(2,1)}) %all-reduce.9.cloned.1.call-update) | async-done | bytes 4718608 | tf_op jit(solution)/shard_map/psum | solution.py:149
  480.2 8.4 convert_reduce_fusion.1
  488.6 8.3 fusion.102
  497.0 5.4 fusion.136
  502.4 3.3 convolution_convert_fusion.3
  506.5 2.9 fusion.118
  509.5 4.4 reshape.677
  517.3 43.6 %while.47 = (s32[]{:T(128)}, bf16[3,2,512,3,64]{2,4,3,1,0:T(8,128)(2,1)}, bf16[3,2,512,3,64]{2,4,3,1,0:T(8,128)(2,1)}, bf16[3,2,512,3,64]{2,4,3,1,0:T(8,128)(2,1...) while((s32[]{:T(128)}, ...), condition=%wide.region_26.27_spmd, body=%wide.region_23.26_spmd.sunk | while | flops 1024463872 | bytes 55389380 | solution.py:161
  561.0 3.5 copy.102
  564.5 3.6 stack.128
  568.0 3.5 copy.100
  571.6 3.9 stack.126
  575.5 2.3 copy.101
  577.8 3.3 stack.127
  584.4 5.2 fusion.115
  589.6 2.7 copy.115
  592.3 4.8 reshape.697
  597.3 12.6 %convolution_convert_fusion.1 = bf16[3072,768]{1,0:T(8,128)(2,1)} fusion(bf16[768,768]{1,0:T(8,128)(2,1)S(1)} %copy-done.34, bf16[3072,768]{1,0:T(8,128)(2,1)} %copy-done.7, bf16[768,768]{1,0:T(8,128)(2,1)S(1)} %copy-done.32, f32[768]{0:T(1024)S(1)} %copy-done.38), kind=kOutput, calls=%fused_computation.224 | convolution fusion | flops 7273709568 | bytes 11799552 | tf_op jit(solution)/shard_map/dot_general | solution.py:137
  609.8 8.2 bitcast_convert_fusion
  618.1 9.1 fusion.144
  627.6 11.5 %fusion.111 = f32[768,768]{0,1:T(8,128)} fusion(bf16[3072,768]{1,0:T(8,128)(2,1)} %param.23, f32[3072,768]{1,0:T(8,128)} %fusion.143, f32[768]{0:T(1024)S(1)} %copy-done.38), kind=kOutput, calls=%fused_computation.233 | convolution fusion | flops 3647471616 | bytes 16518144 | tf_op jit(solution)/shard_map/tf,td->fd/dot_general | solution.py:141
  642.8 321.4 %all-reduce.13.cloned.1.call-done = (bf16[3072,768]{1,0:T(8,128)(2,1)}, bf16[3072,768]{1,0:T(8,128)(2,1)}) async-done(((bf16[3072,768]{1,0:T(8,128)(2,1)}, bf16[3072,768]{1,0:T(8,128)(2,1)}), (bf16[3072,768]{1,0:T(8,128)(2,1)}, bf16[3072,768]{1,0:T(8,128)(2,1)})) %all-reduce.13.cloned.1.call-update) | async-done | bytes 9437200 | tf_op jit(solution)/shard_map/psum | solution.py:138
  964.2 8.4 convert_reduce_fusion
  972.7 10.3 fusion.103
  983.2 6.6 fusion.137
  989.8 3.2 constant_dynamic-slice_fusion.8
  994.8 8.6 add_convert_fusion.1
  1003.5 24.4 %all-reduce = (f32[768]{0:T(1024)}, f32[768]{0:T(1024)}, f32[768]{0:T(1024)}, f32[768]{0:T(1024)}, f32[768]{0:T(1024)}, /*index=5*/f32[768]{0:T(1024)}, f32[768]{0:T(1024)}) all-reduce(f32[768]{0:T(1024)S(1)} %get-tuple-element.458, f32[768]{0:T(1024)S(1)} %get-tuple-element.462, ...), channel_id=1, replica_groups=mesh['dp'=8,'mp'=4] {'dp'}, use_global_device_ids=true, to_apply=%region_34.35 | all-reduce | flops 5376 | bytes 43008 | tf_op jit(solution)/shard_map/psum | solution.py:206
  1027.9 27.8 %reduce-scatter.11.cloned.1.call-done = f32[768,96]{0,1:T(8,128)} async-done(((f32[768,768]{0,1:T(8,128)}), f32[768,96]{0,1:T(8,128)}) %reduce-scatter.11.cloned.1.call-update) | async-done | bytes 294928 | tf_op jit(solution)/shard_map/reduce_scatter | solution.py:195
  1055.7 59.4 %all-reduce.11.cloned.1.call-done = f32[1000,192]{0,1:T(8,128)} async-done(((f32[1000,192]{0,1:T(8,128)}), f32[1000,192]{0,1:T(8,128)}) %all-reduce.11.cloned.1.call-update) | async-done | bytes 768016 | tf_op jit(solution)/shard_map/psum | solution.py:206
  1115.1 2.1 copy.219
  (334 shorter events, 120.3 us)
Async XLA Ops:
  7.2 1.6 copy-start
  7.2 257.6 %all-reduce.7.cloned.1.call-start = ((), (), s32[]{:S(2)}) async-start(), calls=%async_computation.4 | async-start | bytes 9437184 | tf_op jit(solution)/shard_map/psum | solution.py:133
  19.0 14.8 %copy-start.35 = (bf16[3,768,192]{1,2,0:T(8,128)(2,1)S(1)}, bf16[3,768,192]{1,2,0:T(8,128)(2,1)}, u32[]{:S(2)}) copy-start(bf16[3,768,192]{1,2,0:T(8,128)(2,1)} %param.27) | copy-start | bytes 2654212
  28.7 5.0 copy-start.12
  28.7 6.4 copy-start.2
  28.8 6.4 copy-start.19
  28.8 6.4 copy-start.25
  33.7 4.9 copy-start.14
  33.8 4.9 copy-start.16
  82.4 3.9 copy-start.10
  90.0 390.2 %all-reduce.9.cloned.1.call-start = ((), (), s32[]{:S(2)}) async-start(), calls=%async_computation.5 | async-start | bytes 9437184 | tf_op jit(solution)/shard_map/psum | solution.py:149
  99.1 5.1 copy-start.36
  104.2 3.0 copy-start.6
  117.2 147.7 %copy-start.26 = (f32[768]{0:T(1024)S(1)}, f32[768]{0:T(1024)}, u32[]{:S(2)}) copy-start(f32[768]{0:T(1024)} %param.29) | copy-start | bytes 9220
  274.8 6.4 copy-start.3
  274.9 6.4 copy-start.18
  274.9 6.4 copy-start.27
  281.2 1.7 copy-start.31
  281.2 8.1 slice-start.11
  282.9 6.4 copy-start.7
  283.0 6.4 slice-start.12
  283.0 6.4 copy-start.33
  283.0 6.4 copy-start.37
  301.4 2.2 copy-start.39
  309.1 330.2 %reduce-scatter.15.cloned.1.call-start = ((), (), s32[]{:S(2)}) async-start(), calls=%async_computation.10 | async-start | bytes 884736
  480.2 8.4 copy-start.5
  480.2 16.8 %slice-start.3 = ((s8[9437184]{0:T(1024)(128)(4,1)}), s8[4194304]{0:T(1024)(128)(4,1)S(1)}, s32[]{:S(2)}) async-start(s8[9437184]{0:T(1024)(128)(4,1)} %bitcast.355), calls=%async_computation.15 | async-start | bytes 8388608
  480.2 16.8 %slice-start.4 = ((s8[9437184]{0:T(1024)(128)(4,1)}), s8[4194304]{0:T(1024)(128)(4,1)S(1)}, s32[]{:S(2)}) async-start(s8[9437184]{0:T(1024)(128)(4,1)} %bitcast.355), calls=%async_computation.16 | async-start | bytes 8388608
  480.2 16.8 %slice-start.13 = ((s8[4718592]{0:T(1024)(128)(4,1)}), s8[4194304]{0:T(1024)(128)(4,1)S(1)}, s32[]{:S(2)}) async-start(s8[4718592]{0:T(1024)(128)(4,1)} %bitcast.370), calls=%async_computation.25 | async-start | bytes 8388608
  488.6 8.4 slice-start.5
  488.6 8.4 slice-start.14
  502.4 4.0 copy-start.4
  502.4 4.0 copy-start.9
  509.4 131.4 %reduce-scatter.13.cloned.1.call-start = ((), (), s32[]{:S(2)}) async-start(), calls=%async_computation.9 | async-start | bytes 2211840
  564.5 11.0 copy-start.8
  582.6 1.8 copy-start.11
  592.3 4.9 copy-start.32
  592.3 4.9 copy-start.34
  592.3 4.9 copy-start.38
  597.2 367.0 %all-reduce.13.cloned.1.call-start = ((), (), s32[]{:S(2)}) async-start(), calls=%async_computation.11 | async-start | bytes 18874368 | tf_op jit(solution)/shard_map/psum | solution.py:138
  618.1 409.8 %reduce-scatter.9.cloned.1.call-start = ((), (), s32[]{:S(2)}) async-start(), calls=%async_computation.7 | async-start | bytes 2654208 | tf_op jit(solution)/shard_map/reduce_scatter | solution.py:194
  627.3 428.4 %reduce-scatter.11.cloned.1.call-start = ((), (), s32[]{:S(2)}) async-start(), calls=%async_computation.8 | async-start | bytes 2654208 | tf_op jit(solution)/shard_map/reduce_scatter | solution.py:195
  627.6 345.1 %copy-start.15 = (f32[3072]{0:T(1024)S(1)}, f32[3072]{0:T(1024)}, u32[]{:S(2)}) copy-start(f32[3072]{0:T(1024)} %copy-done.14) | copy-start | bytes 36868
  627.6 345.1 %copy-start.17 = (f32[3072]{0:T(1024)S(1)}, f32[3072]{0:T(1024)}, u32[]{:S(2)}) copy-start(f32[3072]{0:T(1024)} %copy-done.16) | copy-start | bytes 36868
  639.2 325.0 %copy-start.13 = (f32[3072]{0:T(1024)S(1)}, f32[3072]{0:T(1024)}, u32[]{:S(2)}) copy-start(f32[3072]{0:T(1024)} %copy-done.12) | copy-start | bytes 36868
  639.2 325.0 %copy-start.20 = (f32[768]{0:T(1024)S(1)}, f32[768]{0:T(1024)}, u32[]{:S(2)}) copy-start(f32[768]{0:T(1024)} %param.25) | copy-start | bytes 9220
  639.2 475.9 %all-reduce.11.cloned.1.call-start = ((), (), s32[]{:S(2)}) async-start(), calls=%async_computation.6 | async-start | bytes 1572864 | tf_op jit(solution)/shard_map/psum | solution.py:206
  964.2 18.9 %slice-start = ((s8[9437184]{0:T(1024)(128)(4,1)}), s8[4194304]{0:T(1024)(128)(4,1)S(1)}, s32[]{:S(2)}) async-start(s8[9437184]{0:T(1024)(128)(4,1)} %bitcast.353), calls=%async_computation.12 | async-start | bytes 8388608
  964.2 18.9 %slice-start.1 = ((s8[9437184]{0:T(1024)(128)(4,1)}), s8[4194304]{0:T(1024)(128)(4,1)S(1)}, s32[]{:S(2)}) async-start(s8[9437184]{0:T(1024)(128)(4,1)} %bitcast.353), calls=%async_computation.13 | async-start | bytes 8388608
  964.2 18.9 %slice-start.6 = ((s8[9437184]{0:T(1024)(128)(4,1)}), s8[4194304]{0:T(1024)(128)(4,1)S(1)}, s32[]{:S(2)}) async-start(s8[9437184]{0:T(1024)(128)(4,1)} %bitcast.357), calls=%async_computation.18 | async-start | bytes 8388608
  964.2 18.9 %slice-start.7 = ((s8[9437184]{0:T(1024)(128)(4,1)}), s8[4194304]{0:T(1024)(128)(4,1)S(1)}, s32[]{:S(2)}) async-start(s8[9437184]{0:T(1024)(128)(4,1)} %bitcast.357), calls=%async_computation.19 | async-start | bytes 8388608
  964.2 18.9 %slice-start.9 = ((s8[4718592]{0:T(1024)(128)(4,1)}), s8[4194304]{0:T(1024)(128)(4,1)S(1)}, s32[]{:S(2)}) async-start(s8[4718592]{0:T(1024)(128)(4,1)} %bitcast.359), calls=%async_computation.21 | async-start | bytes 8388608
  972.7 10.4 slice-start.2
  972.7 10.4 slice-start.8
  972.7 10.4 slice-start.10
  989.8 3.5 copy-start.30
  993.0 1.8 copy-start.28
  994.8 8.7 copy-start.21
  994.8 8.7 copy-start.22
  994.8 8.7 copy-start.23
  994.8 8.7 copy-start.24
  994.8 8.7 copy-start.29
  994.8 122.4 %copy-start.1 = (bf16[1000,768]{1,0:T(8,128)(2,1)S(1)}, bf16[1000,768]{1,0:T(8,128)(2,1)}, u32[]{:S(2)}) copy-start(bf16[1000,768]{1,0:T(8,128)(2,1)} %param.24) | copy-start | bytes 4608004
Sparse Core Ops, SparseCore 0:
  90.1 174.6 all-reduce.6
  309.2 170.9 all-reduce.8
  509.6 33.9 reduce-scatter.14
  597.3 39.1 reduce-scatter.12
  639.5 324.6 all-reduce.12
  968.0 41.3 reduce-scatter.8
  1013.2 42.3 reduce-scatter.10
  1059.4 55.6 all-reduce.10
where the time goes:
time: 1130 us; the launch traced here: 1120 us
  waiting for transfers between devices  690 us (61%)
  matrix products  141 us (12%)
  other arithmetic  139 us (12%)
  local copies, waits for them, and re-layouts  114 us (10%)
  blocking collectives  24.4 us (2%)
  between operations  15.4 us (1%)
    psum x1, waiting for transfers between devices, local(): lax.psum(mlp_part.astype(jnp.bfloat16), 'mp').astype(jnp.float32)  321 us
    psum x1, waiting for transfers between devices, local(): lax.psum(attn_part.astype(jnp.bfloat16), 'mp').astype(jnp.float32)  143 us
    psum x1, waiting for transfers between devices, local(): lax.psum(norm_part.astype(jnp.bfloat16), 'mp').astype(jnp.float32)  138 us
    psum x1, waiting for transfers between devices, local(): lax.psum((table_grad, grad_gain_one, grad_shift_one, grad_out_bias, grad_...  59.4 us
    reduce_sum x4, other arithmetic, layer_norm(): return offset * lax.rsqrt(spread + 1e-05) * gain_vec + shift_vec  35.5 us
    reduce_scatter x1, waiting for transfers between devices, local(): lax.psum_scatter(grad_down, 'dp', scatter_dimension=1, tiled=True)  27.8 us
    psum x1, blocking collectives, local(): lax.psum((table_grad, grad_gain_one, grad_shift_one, grad_out_bias, grad_...  24.4 us
    reduce_sum x3, other arithmetic, layer_norm(): centre = jnp.mean(rows_in, axis=-1, keepdims=True)  23.9 us
  transfers between devices with their start and end apart: 8, of which 5 were waited for; matrix products, arithmetic and copies ran while one was open for 21% of the time, Pallas kernels for 0%

commit v1 on v0

v1 whole, which is shorter than its diff:
```python
from functools import partial

import jax
import jax.numpy as jnp
from jax import lax
from jax.experimental import pallas as pl
from jax.experimental.pallas import tpu as pltpu
from jax.sharding import PartitionSpec as P

F32 = jnp.float32
BF16 = jnp.bfloat16
HD = 64
LEN_A = 128
LEN_B = 256
BLOCK = 512
WIN = 256
TILE = 512
EPS = 1e-05
GELU_C = 0.7978845608028654
GELU_A = 0.044715


def mm(a, b):
    return lax.dot_general(a, b, (((1,), (0,)), ((), ())), preferred_element_type=F32)


def mm_nt(a, b):
    return lax.dot_general(a, b, (((1,), (1,)), ((), ())), preferred_element_type=F32)


def mm_tn(a, b):
    return lax.dot_general(a, b, (((0,), (0,)), ((), ())), preferred_element_type=F32)


def norm_stats(rows):
    centre = jnp.mean(rows, axis=-1, keepdims=True)
    offset = rows - centre
    spread = jnp.mean(offset * offset, axis=-1, keepdims=True)
    inv = lax.rsqrt(spread + EPS)
    return offset * inv, inv


def norm_back(grad, gain, hat, inv):
    dhat = grad * gain
    first = jnp.mean(dhat, axis=-1, keepdims=True)
    second = jnp.mean(dhat * hat, axis=-1, keepdims=True)
    return inv * (dhat - first - hat * second)


def stream_tile(hidden_ref, emb_ref, tile):
    parts = []
    for unit in range(TILE // LEN_A):
        row = emb_ref[pl.ds(tile * (TILE // LEN_A) + unit, 1), :]
        parts.append(hidden_ref[unit * LEN_A : (unit + 1) * LEN_A, :].astype(F32) + row)
    return jnp.concatenate(parts, axis=0)


def attn_fwd_kernel(
    meta, hidden_ref, emb_ref, gain_ref, shift_ref, wqkv_ref, wo_ref, ob_ref,
    qkv_ref, probs_ref, ctx_ref, mid_ref, same_ref, ctx_acc,
):
    tile = pl.program_id(0)
    half = meta[0]
    stream = stream_tile(hidden_ref, emb_ref, tile)
    hat, _ = norm_stats(stream)
    normed = (hat * gain_ref[...] + shift_ref[...]).astype(BF16)
    mid_ref[...] = stream + ob_ref[...]
    for part in range(3):
        qkv_ref[part] = mm_nt(normed, wqkv_ref[part]).astype(BF16)
    lane = lax.broadcasted_iota(jnp.int32, (WIN, 2 * HD), 1)
    low = lane < HD
    row_i = lax.broadcasted_iota(jnp.int32, (WIN, WIN), 0)
    col_i = lax.broadcasted_iota(jnp.int32, (WIN, WIN), 1)
    same_half = (row_i < LEN_A) == (col_i < LEN_A)
    scale = HD ** (-0.5)
    pairs = qkv_ref.shape[2] // (2 * HD)
    for win in range(TILE // WIN):
        spot = (half * (3 * TILE // WIN) + tile * (TILE // WIN) + win) % 4
        same_ref[...] = jnp.where(same_half, 0.0, jnp.where(spot < 2, -1e9, 0.0))
        rows = slice(win * WIN, (win + 1) * WIN)
        for pair in range(pairs):
            cols = slice(pair * 2 * HD, (pair + 1) * 2 * HD)
            q2 = qkv_ref[0, rows, cols] * jnp.asarray(scale, BF16)
            k2 = qkv_ref[1, rows, cols]
            v2 = qkv_ref[2, rows, cols]
            outs = []
            for j in range(2):
                q1 = jnp.where(low == (j == 0), q2, jnp.zeros_like(q2))
                scores = mm_nt(q1, k2) + same_ref[...]
                top = jnp.max(scores, axis=-1, keepdims=True)
                expo = jnp.exp(scores - top)
                total = jnp.sum(expo, axis=-1, keepdims=True)
                probs = (expo * (1.0 / total)).astype(BF16)
                probs_ref[2 * pair + j, win] = probs
                outs.append(mm(probs, v2))
            ctx_acc[rows, cols] = jnp.where(low, outs[0], outs[1]).astype(BF16)
    ctx_ref[...] = ctx_acc[...]
    mid_ref[...] += mm(ctx_acc[...], wo_ref[...])


def mlp_kernel(
    meta, mid_ref, gy_ref, wu_ref, bu_ref, wd_ref, gain_ref, shift_ref, db_ref,
    out_ref, gmid_ref, gw_ref, vec_ref, gbu_ref,
    acc_u, acc_d, n2_ref, n2t_ref, gyt_ref, mlp_ref, dn_ref,
):
    tile = pl.program_id(0)
    last = pl.num_programs(0) - 1
    pair = meta[1]
    ff = wu_ref.shape[2]

    @pl.when(tile == 0)
    def _():
        acc_u[...] = jnp.zeros_like(acc_u)
        acc_d[...] = jnp.zeros_like(acc_d)
        vec_ref[...] = jnp.zeros_like(vec_ref)
        gbu_ref[...] = jnp.zeros_like(gbu_ref)

    hat, inv = norm_stats(mid_ref[...])
    normed = (hat * gain_ref[...] + shift_ref[...]).astype(BF16)
    n2_ref[...] = normed
    n2t_ref[...] = normed.T
    gyt_ref[...] = gy_ref[...].T
    mlp_ref[...] = mid_ref[...] + db_ref[...]
    dn_ref[...] = jnp.zeros_like(dn_ref)

    def step(turn, own):
        group = lax.rem(2 * pair + turn, 4)
        pre = mm(n2_ref[...], wu_ref[group]) + bu_ref[group, 0:1]
        grad_act = mm_nt(gy_ref[...], wd_ref[group])
        square = pre * pre
        bend = jnp.tanh(pre * (GELU_C + (GELU_C * GELU_A) * square))
        half_in = 0.5 * pre
        up = 1.0 + bend
        act = (half_in * up).astype(BF16)
        slope = 0.5 * up + half_in * (1.0 - bend * bend) * (GELU_C + (3.0 * GELU_C * GELU_A) * square)
        grad_f = grad_act * slope
        grad_pre = grad_f.astype(BF16)
        mlp_ref[...] += mm(act, wd_ref[group])
        dn_ref[...] += mm_nt(grad_pre, wu_ref[group])
        if own:
            acc_u[turn] += mm(n2t_ref[...], grad_pre)
            acc_d[turn] += mm(gyt_ref[...], act)
            gbu_ref[turn, 0:1] += jnp.sum(grad_pre.astype(F32), axis=0, keepdims=True)

    lax.fori_loop(0, 2, lambda turn, c: (step(turn, True), c)[1], 0)
    lax.fori_loop(2, 4, lambda turn, c: (step(turn, False), c)[1], 0)

    out_ref[...] = mlp_ref[...].astype(BF16)
    hat, inv = norm_stats(mid_ref[...])
    top = gy_ref[...].astype(F32)
    dn = dn_ref[...]
    vec_ref[0:1] += jnp.sum(dn * hat, axis=0, keepdims=True)
    vec_ref[1:2] += jnp.sum(dn, axis=0, keepdims=True)
    gmid = top + norm_back(dn, gain_ref[...], hat, inv)
    vec_ref[2:3] += jnp.sum(gmid, axis=0, keepdims=True)
    vec_ref[3:4] += jnp.sum(top, axis=0, keepdims=True)
    gmid_ref[...] = gmid

    @pl.when(tile == last)
    def _():
        gw_ref[:, :, 0:ff] = acc_u[...].astype(BF16)
        gw_ref[:, :, ff : 2 * ff] = acc_d[...].astype(BF16)


def attn_bwd_kernel(
    meta, hidden_ref, emb_ref, gain_ref, shift_ref, wqkv_ref, wo_ref,
    qkv_ref, probs_ref, ctx_ref, gmid_ref,
    gh_ref, gw_ref, vec_ref, usum_ref,
    acc, gp_ref, gc_ref, n1t_ref, gmt_ref,
):
    tile = pl.program_id(0)
    last = pl.num_programs(0) - 1
    pair_id = meta[1]
    width = wo_ref.shape[1]
    part_w = width // 2

    @pl.when(tile == 0)
    def _():
        acc[...] = jnp.zeros_like(acc)
        vec_ref[...] = jnp.zeros_like(vec_ref)
        usum_ref[...] = jnp.zeros_like(usum_ref)

    own = pl.ds(pl.multiple_of(pair_id * part_w, 128), part_w)
    stream = stream_tile(hidden_ref, emb_ref, tile)
    hat, inv = norm_stats(stream)
    n1t_ref[...] = (hat * gain_ref[...] + shift_ref[...]).astype(BF16).T
    gm_low = gmid_ref[...].astype(BF16)
    gmt_ref[...] = gm_low.T
    gc_ref[...] = mm_nt(gm_low, wo_ref[...]).astype(BF16)
    acc[3] += mm(gmt_ref[...], ctx_ref[:, own])
    lane = lax.broadcasted_iota(jnp.int32, (WIN, 2 * HD), 1)
    low = lane < HD
    scale = HD ** (-0.5)
    pairs = width // (2 * HD)
    for win in range(TILE // WIN):
        rows = slice(win * WIN, (win + 1) * WIN)
        for pair in range(pairs):
            cols = slice(pair * 2 * HD, (pair + 1) * 2 * HD)
            q2 = qkv_ref[0, rows, cols]
            k2 = qkv_ref[1, rows, cols]
            v2 = qkv_ref[2, rows, cols]
            gc2 = gc_ref[rows, cols]
            dq, dk, dv = [], [], []
            for j in range(2):
                gc1 = jnp.where(low == (j == 0), gc2, jnp.zeros_like(gc2))
                probs_low = probs_ref[2 * pair + j, win]
                probs = probs_low.astype(F32)
                dprob = mm_nt(gc1, v2)
                mix = probs * dprob
                total = jnp.sum(mix, axis=-1, keepdims=True)
                grad_s = (mix - probs * total).astype(BF16)
                dv.append(mm_tn(probs_low, gc2))
                dk.append(mm_tn(grad_s, q2))
                dq.append(mm(grad_s, k2))
            gp_ref[0, rows, cols] = (jnp.where(low, dq[0], dq[1]) * scale).astype(BF16)
            gp_ref[1, rows, cols] = (jnp.where(low, dk[0], dk[1]) * scale).astype(BF16)
            gp_ref[2, rows, cols] = jnp.where(low, dv[0], dv[1]).astype(BF16)
    grad_n = mm(gp_ref[0], wqkv_ref[0])
    for part in range(1, 3):
        grad_n = grad_n + mm(gp_ref[part], wqkv_ref[part])
    for part in range(3):
        acc[part] += mm(n1t_ref[...], gp_ref[part, :, own])
    stream = stream_tile(hidden_ref, emb_ref, tile)
    hat, inv = norm_stats(stream)
    vec_ref[0:1] += jnp.sum(grad_n * hat, axis=0, keepdims=True)
    vec_ref[1:2] += jnp.sum(grad_n, axis=0, keepdims=True)
    grad_in = gmid_ref[...] + norm_back(grad_n, gain_ref[...], hat, inv)
    gh_ref[...] = grad_in.astype(BF16)
    for unit in range(TILE // LEN_A):
        usum_ref[pl.ds(tile * (TILE // LEN_A) + unit, 1), :] = jnp.sum(
            grad_in[unit * LEN_A : (unit + 1) * LEN_A], axis=0, keepdims=True
        )

    @pl.when(tile == last)
    def _():
        piece = part_w // 2
        for group in range(2):
            for part in range(4):
                gw_ref[group, :, part * piece : (part + 1) * piece] = acc[
                    part, :, group * piece : (group + 1) * piece
                ].astype(BF16)


def whole(shape):
    zeros = (0,) * len(shape)
    return pl.BlockSpec(shape, lambda i, meta: zeros, pipeline_mode=pl.Buffered(1))


def held(shape):
    zeros = (0,) * len(shape)
    return pl.BlockSpec(shape, lambda i, meta: zeros)


LIMIT = 62 * 1024 * 1024


def attn_fwd(meta, hidden, emb, gain, shift, wqkv, wo, ob):
    count, width = hidden.shape[0] // 2, hidden.shape[1]
    steps = count // TILE
    heads = width // HD
    tok = pl.BlockSpec((TILE, width), lambda i, meta: (i, 0))
    return pl.pallas_call(
        attn_fwd_kernel,
        name="attn_fwd",
        grid_spec=pltpu.PrefetchScalarGridSpec(
            num_scalar_prefetch=1,
            grid=(steps,),
            in_specs=[
                pl.BlockSpec((TILE, width), lambda i, meta: (meta[0] * steps + i, 0)),
                whole(emb.shape), whole((1, width)), whole((1, width)),
                whole(wqkv.shape), whole(wo.shape), whole((1, width)),
            ],
            out_specs=[
                pl.BlockSpec((3, TILE, width), lambda i, meta: (0, i, 0)),
                pl.BlockSpec((heads, TILE // WIN, WIN, WIN), lambda i, meta: (0, i, 0, 0)),
                tok,
                tok,
            ],
            scratch_shapes=[pltpu.VMEM((WIN, WIN), F32), pltpu.VMEM((TILE, width), BF16)],
        ),
        out_shape=[
            jax.ShapeDtypeStruct((3, count, width), BF16),
            jax.ShapeDtypeStruct((heads, count // WIN, WIN, WIN), BF16),
            jax.ShapeDtypeStruct((count, width), BF16),
            jax.ShapeDtypeStruct((count, width), F32),
        ],
        compiler_params=pltpu.CompilerParams(vmem_limit_bytes=LIMIT),
        cost_estimate=pl.CostEstimate(flops=12_000_000_000, bytes_accessed=30_000_000, transcendentals=5_000_000),
    )(meta, hidden, emb, gain, shift, wqkv, wo, ob)


def mlp(meta, mid, gy, wu, bu, wd, gain, shift, db):
    count, width = mid.shape
    steps = count // TILE
    ff = wu.shape[2]
    tok = pl.BlockSpec((TILE, width), lambda i, meta: (i, 0))
    return pl.pallas_call(
        mlp_kernel,
        name="mlp_both",
        grid_spec=pltpu.PrefetchScalarGridSpec(
            num_scalar_prefetch=1,
            grid=(steps,),
            in_specs=[
                tok,
                pl.BlockSpec((TILE, width), lambda i, meta: (meta[0] * steps + i, 0)),
                whole(wu.shape), whole(bu.shape), whole(wd.shape),
                whole((1, width)), whole((1, width)), whole((1, width)),
            ],
            out_specs=[tok, tok, whole((2, width, 2 * ff)), held((8, width)), held((2, 8, ff))],
            scratch_shapes=[
                pltpu.VMEM((2, width, ff), F32), pltpu.VMEM((2, width, ff), F32),
                pltpu.VMEM((TILE, width), BF16), pltpu.VMEM((width, TILE), BF16),
                pltpu.VMEM((width, TILE), BF16),
                pltpu.VMEM((TILE, width), F32), pltpu.VMEM((TILE, width), F32),
            ],
        ),
        out_shape=[
            jax.ShapeDtypeStruct((count, width), BF16),
            jax.ShapeDtypeStruct((count, width), F32),
            jax.ShapeDtypeStruct((2, width, 2 * ff), BF16),
            jax.ShapeDtypeStruct((8, width), F32),
            jax.ShapeDtypeStruct((2, 8, ff), F32),
        ],
        compiler_params=pltpu.CompilerParams(vmem_limit_bytes=LIMIT),
        cost_estimate=pl.CostEstimate(flops=36_000_000_000, bytes_accessed=30_000_000, transcendentals=5_000_000),
    )(meta, mid, gy, wu, bu, wd, gain, shift, db)


def attn_bwd(meta, hidden, emb, gain, shift, wqkv, wo, qkv, probs, ctx, gmid):
    count, width = gmid.shape
    steps = count // TILE
    heads = width // HD
    tok = pl.BlockSpec((TILE, width), lambda i, meta: (i, 0))
    return pl.pallas_call(
        attn_bwd_kernel,
        name="attn_bwd",
        grid_spec=pltpu.PrefetchScalarGridSpec(
            num_scalar_prefetch=1,
            grid=(steps,),
            in_specs=[
                pl.BlockSpec((TILE, width), lambda i, meta: (meta[0] * steps + i, 0)),
                whole(emb.shape), whole((1, width)), whole((1, width)),
                whole(wqkv.shape), whole(wo.shape),
                pl.BlockSpec((3, TILE, width), lambda i, meta: (0, i, 0)),
                pl.BlockSpec((heads, TILE // WIN, WIN, WIN), lambda i, meta: (0, i, 0, 0)),
                tok, tok,
            ],
            out_specs=[tok, whole((2, width, width)), held((8, width)), held(emb.shape)],
            scratch_shapes=[
                pltpu.VMEM((4, width, width // 2), F32),
                pltpu.VMEM((3, TILE, width), BF16), pltpu.VMEM((TILE, width), BF16),
                pltpu.VMEM((width, TILE), BF16), pltpu.VMEM((width, TILE), BF16),
            ],
        ),
        out_shape=[
            jax.ShapeDtypeStruct((count, width), BF16),
            jax.ShapeDtypeStruct((2, width, width), BF16),
            jax.ShapeDtypeStruct((8, width), F32),
            jax.ShapeDtypeStruct(emb.shape, F32),
        ],
        compiler_params=pltpu.CompilerParams(vmem_limit_bytes=LIMIT),
        cost_estimate=pl.CostEstimate(flops=20_000_000_000, bytes_accessed=40_000_000, transcendentals=0),
    )(meta, hidden, emb, gain, shift, wqkv, wo, qkv, probs, ctx, gmid)
ARRAYS = 4


def gather_kernel(
    wqkv, wo, wu, wd, bu, wqkv_f, wo_f, wu_f, wd_f, bu_f,
    hold_qkv, hold_wo, hold_wu, hold_wd, hold_bu,
    loc_sem, z_send, z_recv, b_send, b_recv, n_send, n_recv,
):
    place = lax.axis_index("dp")
    member = lax.axis_index("mp")
    base = place - lax.rem(place, 8)
    spot = place - base
    bit0 = lax.rem(spot, 2)
    bit1 = lax.rem(spot // 2, 2)
    bit2 = spot // 4

    def flip(where, bit, size):
        return where + size - 2 * size * bit

    near = {
        "core": {"dp": flip(place, bit0, 1), "mp": member},
        "x": {"dp": flip(place, bit1, 2), "mp": member},
        "y": {"dp": flip(place, bit2, 4), "mp": member},
    }
    mine = spot
    from_x = flip(spot, bit1, 2)
    from_y = flip(spot, bit2, 4)
    from_d = flip(from_x, bit2, 4)

    def peer(turn):
        return {"dp": place, "mp": lax.rem(member + turn, 4)}

    barrier = pltpu.get_barrier_semaphore()
    for target in (peer(1), peer(2), peer(3), near["core"], near["x"], near["y"]):
        pl.semaphore_signal(barrier, inc=1, device_id=target, device_id_type=pl.DeviceIdType.MESH)
    pl.semaphore_wait(barrier, 6)

    rows_a = wo.shape[0]
    step_a = rows_a // 8
    step_m = wu.shape[1 - 1] // 8

    def full_at(array, shard, piece):
        if array == 0:
            return wqkv_f.at[:, pl.ds(shard * rows_a + piece * step_a, step_a), :]
        if array == 1:
            return wo_f.at[pl.ds(shard * rows_a + piece * step_a, step_a), :]
        full = wu_f if array == 2 else wd_f
        return full.at[shard, pl.ds(piece * step_m, step_m), :]

    def own_at(array, piece):
        if array == 0:
            return wqkv.at[:, pl.ds(piece * step_a, step_a), :]
        if array == 1:
            return wo.at[pl.ds(piece * step_a, step_a), :]
        return (wu if array == 2 else wd).at[pl.ds(piece * step_m, step_m), :]

    sends = []
    z_recvs, n_recvs = {}, {}
    for array in range(ARRAYS):
        for turn in (2, 1, 3):
            copy = pltpu.make_async_remote_copy(
                src_ref=own_at(array, spot),
                dst_ref=full_at(array, member, spot),
                send_sem=z_send.at[array, turn - 1],
                recv_sem=z_recv.at[array, turn - 1],
                device_id=peer(turn),
                device_id_type=pl.DeviceIdType.MESH,
            )
            copy.start()
            sends.append(copy)
            z_recvs[array, turn] = copy
        if array == 0:
            for turn in (1, 2, 3):
                copy = pltpu.make_async_remote_copy(
                    src_ref=bu, dst_ref=bu_f.at[member],
                    send_sem=b_send.at[turn - 1], recv_sem=b_recv.at[turn - 1],
                    device_id=peer(turn), device_id_type=pl.DeviceIdType.MESH,
                )
                copy.start()
                sends.append(copy)
                n_recvs["bias", turn] = copy

    own_full = (
        (wqkv, hold_qkv, wqkv_f.at[:, pl.ds(member * rows_a, rows_a), :]),
        (wo, hold_wo, wo_f.at[pl.ds(member * rows_a, rows_a), :]),
        (wu, hold_wu, wu_f.at[member]),
        (wd, hold_wd, wd_f.at[member]),
        (bu, hold_bu, bu_f.at[member]),
    )
    into = [pltpu.make_async_copy(src, hold, loc_sem.at[n]) for n, (src, hold, _) in enumerate(own_full)]
    for copy in into:
        copy.start()
    outof = []
    for n, (_, hold, dst) in enumerate(own_full):
        into[n].wait()
        copy = pltpu.make_async_copy(hold, dst, loc_sem.at[5 + n])
        copy.start()
        outof.append(copy)

    def push(array, turn, kind, piece, target):
        shard = lax.rem(member + 4 - turn, 4)
        copy = pltpu.make_async_remote_copy(
            src_ref=full_at(array, shard, piece),
            dst_ref=full_at(array, shard, piece),
            send_sem=n_send.at[array, turn - 1, kind],
            recv_sem=n_recv.at[array, turn - 1, kind],
            device_id=near[target],
            device_id_type=pl.DeviceIdType.MESH,
        )
        copy.start()
        sends.append(copy)
        n_recvs[array, turn, kind] = copy

    order = (1, 3, 2)

    def stage_z(array):
        for turn in order:
            z_recvs[array, turn].wait_recv()
            push(array, turn, 0, mine, "x")
            push(array, turn, 1, mine, "y")
            push(array, turn, 3, mine, "core")

    def stage_near(array):
        for turn in order:
            n_recvs[array, turn, 0].wait_recv()
            if (array + turn) % 2 == 0:
                push(array, turn, 2, from_x, "y")
            push(array, turn, 4, from_x, "core")
            n_recvs[array, turn, 1].wait_recv()
            if (array + turn) % 2 == 1:
                push(array, turn, 2, from_y, "x")
            push(array, turn, 5, from_y, "core")

    def stage_far(array):
        for turn in order:
            n_recvs[array, turn, 2].wait_recv()
            push(array, turn, 6, from_d, "core")

    for step in range(ARRAYS + 2):
        if step < ARRAYS:
            stage_z(step)
        if 0 <= step - 1 < ARRAYS:
            stage_near(step - 1)
        if 0 <= step - 2 < ARRAYS:
            stage_far(step - 2)
    for array in range(ARRAYS):
        for turn in order:
            for kind in range(3, 7):
                n_recvs[array, turn, kind].wait_recv()
    for turn in (1, 2, 3):
        n_recvs["bias", turn].wait_recv()
    for copy in sends:
        copy.wait_send()
    for copy in outof:
        copy.wait()


def gather_weights(wqkv, wo, wu, wd, bu):
    anywhere = pl.BlockSpec(memory_space=pl.ANY)
    rows, width = wo.shape
    ff = wu.shape[1]
    return pl.pallas_call(
        gather_kernel,
        name="gather_weights",
        in_specs=[anywhere] * 5,
        out_specs=[anywhere] * 5,
        out_shape=[
            jax.ShapeDtypeStruct((3, 4 * rows, width), BF16),
            jax.ShapeDtypeStruct((4 * rows, width), BF16),
            jax.ShapeDtypeStruct((4, width, ff), BF16),
            jax.ShapeDtypeStruct((4, ff, width), BF16),
            jax.ShapeDtypeStruct((4,) + bu.shape, F32),
        ],
        scratch_shapes=[
            pltpu.VMEM(wqkv.shape, BF16), pltpu.VMEM(wo.shape, BF16),
            pltpu.VMEM(wu.shape, BF16), pltpu.VMEM(wd.shape, BF16), pltpu.VMEM(bu.shape, F32),
            pltpu.SemaphoreType.DMA((10,)),
            pltpu.SemaphoreType.DMA((ARRAYS, 3)), pltpu.SemaphoreType.DMA((ARRAYS, 3)),
            pltpu.SemaphoreType.DMA((3,)), pltpu.SemaphoreType.DMA((3,)),
            pltpu.SemaphoreType.DMA((ARRAYS, 3, 7)), pltpu.SemaphoreType.DMA((ARRAYS, 3, 7)),
        ],
        compiler_params=pltpu.CompilerParams(
            collective_id=1, has_side_effects=True, vmem_limit_bytes=LIMIT
        ),
    )(wqkv, wo, wu, wd, bu)
def local(
    hidden, timesteps, cotangent, time_table, first_gain, first_shift, qkv_weight, out_weight,
    out_bias, second_gain, second_shift, up_weight, up_bias, down_weight, down_bias,
):
    count, width = hidden.shape
    steps = time_table.shape[0]
    local_ff = up_weight.shape[1]
    member = lax.axis_index("mp")
    half = lax.rem(member, 2)
    pair = member // 2
    meta = jnp.stack([half, pair]).astype(jnp.int32)
    units = count // (2 * LEN_A)
    unit = half * units + jnp.arange(units, dtype=jnp.int32)
    within = unit % 8
    row_of = unit // 8 * 6 + jnp.where(within < 4, within, 4 + (within - 4) // 2)
    unit_step = jnp.take(timesteps, row_of)
    emb = jnp.take(time_table, unit_step, axis=0).astype(F32)
    emb = jnp.concatenate([emb, jnp.zeros((16 - units, width), F32)], axis=0)

    def row(v):
        return v.reshape(1, -1)

    wqkv_f, wo_f, wu_f, wd_f, bu_f = gather_weights(
        jnp.swapaxes(qkv_weight, 1, 2),
        out_weight,
        up_weight,
        down_weight,
        jnp.broadcast_to(row(up_bias), (8, local_ff)),
    )
    qkv, probs, ctx, mid = attn_fwd(
        meta, hidden, emb, row(first_gain), row(first_shift), wqkv_f, wo_f, row(out_bias)
    )
    out_own, gmid, gw_mlp, vec_mlp, gbu = mlp(
        meta, mid, cotangent, wu_f, bu_f, wd_f, row(second_gain), row(second_shift), row(down_bias)
    )
    swap = [(0, 1), (1, 0), (2, 3), (3, 2)]
    out_other = lax.ppermute(out_own, "mp", swap)
    gh_own, gw_attn, vec_attn, usum = attn_bwd(
        meta, hidden, emb, row(first_gain), row(first_shift), wqkv_f, wo_f, qkv, probs, ctx, gmid
    )
    gh_other = lax.ppermute(gh_own, "mp", swap)

    def join(own, other):
        first = jnp.where(half == 0, own, other)
        second = jnp.where(half == 0, other, own)
        return jnp.concatenate([first, second], axis=0)

    output = join(out_own, out_other)
    grad_hidden = join(gh_own, gh_other)

    def spread(grads):
        mine = lax.psum_scatter(grads, "dp", scatter_dimension=1, tiled=True)
        keep = jnp.where(half == 0, mine[0], mine[1]).astype(F32)
        give = jnp.where(half == 0, mine[1], mine[0])
        return keep + lax.ppermute(give, "mp", swap).astype(F32)

    g_mlp = spread(gw_mlp)
    g_attn = spread(gw_attn)
    grad_up = g_mlp[:, :local_ff]
    grad_down = g_mlp[:, local_ff:].T
    head_w = qkv_weight.shape[2]
    grad_qkv = jnp.stack([g_attn[:, c * head_w : (c + 1) * head_w] for c in range(3)])
    grad_out = g_attn[:, 3 * head_w :].T

    chosen = (unit_step[:, None] == lax.broadcasted_iota(jnp.int32, (1, steps), 1)).astype(F32)
    part_w = width // 2
    sums = lax.dynamic_slice_in_dim(usum[:units], pair * part_w, part_w, 1)
    table = jnp.dot(chosen.T, sums, precision=lax.Precision.HIGHEST, preferred_element_type=F32)
    left, right = table[:, : part_w // 2], table[:, part_w // 2 :]
    table = jnp.where(half == 0, left, right) + lax.ppermute(
        jnp.where(half == 0, right, left), "mp", swap
    )
    table = lax.psum(table, "dp")

    slots = jnp.where(
        (jnp.arange(4) // 2 == pair)[:, None], jnp.concatenate([gbu[:, 0], gbu[:, 0]], axis=0), 0.0
    )
    small = jnp.concatenate([0.5 * vec_attn[:2], 0.5 * vec_mlp[:4], slots], axis=0)
    small = lax.psum(small, ("dp", "mp"))
    grad_up_bias = lax.dynamic_slice_in_dim(small[6:], member, 1, 0)[0]
    return (
        output, grad_hidden, table, small[0], small[1], grad_qkv, grad_out, small[4],
        small[2], small[3], grad_up, grad_up_bias, grad_down, small[5],
    )


def solution(mesh):
    return jax.shard_map(
        local,
        mesh=mesh,
        in_specs=(
            P("dp", None), P("dp"), P("dp", None), P(), P(), P(), P(None, None, "mp"),
            P("mp", None), P(), P(), P(), P(None, "mp"), P("mp"), P("mp", None), P(),
        ),
        out_specs=(
            P("dp", None), P("dp", None), P(None, "mp"), P(), P(), P(None, "dp", "mp"),
            P("mp", "dp"), P(), P(), P(), P("dp", "mp"), P("mp"), P("mp", "dp"), P(),
        ),
        check_vma=False,
    )
```

time: 1130 us -> 438 us (0.39)
  waiting for transfers between devices: 690 us -> 38.4 us
  Pallas kernels: 0 us -> 200 us
  matrix products: 141 us -> 1.83 us
  other arithmetic: 139 us -> 21 us
  blocking collectives: 24.4 us -> 123 us
  local copies, waits for them, and re-layouts: 114 us -> 19.3 us
  starting transfers between devices: 0.58 us -> 12.6 us
    psum x4 -> x1, waiting for transfers between devices: 662 us -> 0.01 us  [local(): table = lax.psum(table, 'dp')]
    pallas_call x0 -> x4, Pallas kernels: none -> 200 us  [the longest x1 66.1 us: gather_weights(): pl.pallas_call(gather_kernel, name='gather_weights', in_specs=[anywhere]...]
    dot_general x65 -> x1, matrix products: 132 us -> 1.83 us  [local(): jnp.dot(chosen.T, sums, precision=lax.Precision.HIGHEST, preferred_elemen...]
    psum x1, blocking collectives: 24.4 us -> 123 us  [local(): small = lax.psum(small, ('dp', 'mp'))]
    reduce_sum x25 -> x0, other arithmetic: 88.3 us -> none  [the longest x4 35.5 us: layer_norm(): return offset * lax.rsqrt(spread + 1e-05) * gain_vec + shift_vec]
    convert_element_type x13 -> x0, other arithmetic: 28.4 us -> none  [the longest x1 8.64 us: local(): output = result.astype(jnp.bfloat16)]
    another operation x12 -> x0, local copies, waits for them, and re-layouts: 25.9 us -> none
    ppermute x0 -> x5, waiting for transfers between devices: none -> 23.9 us  [the longest x1 18.3 us: local(): lax.ppermute(jnp.where(half == 0, right, left), 'mp', swap)]
  transfers between devices with their start and end apart: 8 -> 8, of which waited for: 5 -> 3; matrix products, arithmetic and copies ran while one was open for 21% -> 5% of each run, Pallas kernels for 0% -> 0%
where the time goes in v1:
time: 438 us; the launch traced here: 431 us
  Pallas kernels  200 us (46%)
  blocking collectives  123 us (28%)
  waiting for transfers between devices  38.4 us (9%)
  other arithmetic  21 us (5%)
  local copies, waits for them, and re-layouts  19.3 us (4%)
  between operations  14.4 us (3%)
  starting transfers between devices  12.6 us (3%)
    psum x1, blocking collectives, local(): small = lax.psum(small, ('dp', 'mp'))  123 us
    pallas_call x1, Pallas kernels, gather_weights(): pl.pallas_call(gather_kernel, name='gather_weights', in_specs=[anywhere]...  66.1 us
    pallas_call x1, Pallas kernels, mlp(): pl.pallas_call(mlp_kernel, name='mlp_both', grid_spec=pltpu.PrefetchScala...  56.8 us
    pallas_call x1, Pallas kernels, attn_bwd(): pl.pallas_call(attn_bwd_kernel, name='attn_bwd', grid_spec=pltpu.Prefetch...  50.4 us
    pallas_call x1, Pallas kernels, attn_fwd(): pl.pallas_call(attn_fwd_kernel, name='attn_fwd', grid_spec=pltpu.Prefetch...  27.1 us
    ppermute x1, waiting for transfers between devices, local(): lax.ppermute(jnp.where(half == 0, right, left), 'mp', swap)  18.3 us
    reduce_scatter x2, waiting for transfers between devices, spread(): mine = lax.psum_scatter(grads, 'dp', scatter_dimension=1, tiled=True)  13.1 us
  transfers between devices with their start and end apart: 8, of which 3 were waited for; matrix products, arithmetic and copies ran while one was open for 5% of the time, Pallas kernels for 0%

profile of v1, /device:TPU:0, one launch (start us, length us, event | category | flops | bytes accessed | tf_op | source)
XLA Modules:
  0.0 431.0 jit_solution(3128233680444511588)
XLA Ops:
  7.2 0.0 copy-start
  7.2 0.0 all-reduce.3.cloned.1.call-start
  7.3 1.4 gather_fusion
  8.8 1.3 reshape.260.gain_ref
  10.1 1.3 reshape.261.shift_ref
  11.3 1.3 reshape.262.ob_ref
  12.6 1.3 reshape.263.gain_ref
  13.9 1.3 reshape.264.shift_ref
  15.1 1.3 reshape.265.db_ref
  16.4 0.0 copy-done
  16.4 0.6 gather_fusion.1
  17.0 0.1 broadcast_select_fusion.4
  17.1 0.6 pad_convert_fusion.emb_ref
  17.7 0.7 pad_add_fusion.meta
  18.4 1.3 broadcast_in_dim.34.bu
  19.7 66.1 %gather_weights.1 = (bf16[3,768,768]{2,1,0:T(8,128)(2,1)}, bf16[768,768]{1,0:T(8,128)(2,1)}, bf16[4,768,768]{2,1,0:T(8,128)(2,1)}, bf16[4,768,768]{2,1,0:T(8,128)(2,1)}, f32[4,8,768]{2,1,0:T(8,128)}) custom-call(bf16[3,192,768]{2,1,0:T(8,128)(2,1)} %bitcast.35, bf16[192,768]{1,0:T(8,128)(2,1)} %wo.1, bf16[768,768]{1,0:T(8,128)(2,1)} %wu.1, ...), custom_call_target="tpu_custom_call" | custom-call | tf_op jit(solution)/shard_map/gather_weights/pallas_call | solution.py:525
  85.7 27.1 %attn_fwd.1 = (bf16[3,1536,768]{2,1,0:T(8,128)(2,1)}, bf16[12,6,256,256]{3,2,1,0:T(8,128)(2,1)}, bf16[1536,768]{1,0:T(8,128)(2,1)}, f32[1536,768]{1,0:T(8,128)}) custom-call(s32[2]{0:T(128)} %pad_add_fusion.meta, bf16[3072,768]{1,0:T(8,128)(2,1)} %hidden_ref.3, f32[16,768]{1,0:T(8,128)} %pad_convert_fusion.emb_ref, f32[1,768]{1,0:T(1,128)} %reshape.260.gain_ref, ...), custom_call_target="tpu_custom_call" | custom-call | flops 12000000000 | bytes 30000000 | tf_op jit(solution)/shard_map/attn_fwd/pallas_call | solution.py:262
  112.8 56.8 %mlp_both.1 = (bf16[1536,768]{1,0:T(8,128)(2,1)}, f32[1536,768]{1,0:T(8,128)}, bf16[2,768,1536]{2,1,0:T(8,128)(2,1)}, f32[8,768]{1,0:T(8,128)}, f32[2,8,768]{2,1,0:T(8,128)}) custom-call(s32[2]{0:T(128)} %pad_add_fusion.meta, f32[1536,768]{1,0:T(8,128)} %get-tuple-element.34.mid_ref, bf16[3072,768]{1,0:T(8,128)(2,1)} %gy_ref.1, ...), custom_call_target="tpu_custom_call" | custom-call | flops 35999997952 | bytes 30000000 | tf_op jit(solution)/shard_map/mlp_both/pallas_call | solution.py:297
  169.5 50.4 %attn_bwd.1 = (bf16[1536,768]{1,0:T(8,128)(2,1)}, bf16[2,768,768]{2,1,0:T(8,128)(2,1)}, f32[8,768]{1,0:T(8,128)}, f32[16,768]{1,0:T(8,128)}) custom-call(s32[2]{0:T(128)} %pad_add_fusion.meta, bf16[3072,768]{1,0:T(8,128)(2,1)} %hidden_ref.3, f32[16,768]{1,0:T(8,128)} %pad_convert_fusion.emb_ref, f32[1,768]{1,0:T(1,128)} %reshape.260.gain_ref, ...), custom_call_target="tpu_custom_call" | custom-call | flops 20000000000 | bytes 40000000 | tf_op jit(solution)/shard_map/attn_bwd/pallas_call | solution.py:334
  219.9 1.8 fusion
  221.7 0.3 slice_select_fusion
  222.1 0.3 copy.33
  222.4 6.7 %collective-permute-start.2 = (f32[1000,192]{0,1:T(8,128)S(1)}, f32[1000,192]{0,1:T(8,128)}, u32[]{:S(2)}, u32[]{:S(2)}) collective-permute-start(f32[1000,192]{0,1:T(8,128)S(1)} %copy.33), channel_id=1, source_target_pairs={{0,1},{1,0},{2,3},{3,2},{4,5},{5,4},{6,7},{7,6},{8,9},{9,8},{10,11... | collective-permute-start | bytes 2304008 | tf_op jit(solution)/shard_map/ppermute | solution.py:618
  229.1 18.3 %collective-permute-done.2 = f32[1000,192]{0,1:T(8,128)} collective-permute-done((f32[1000,192]{0,1:T(8,128)S(1)}, f32[1000,192]{0,1:T(8,128)}, u32[]{:S(2)}, u32[]{:S(2)}) %collective-permute-start.2) | collective-permute-done | bytes 768032 | tf_op jit(solution)/shard_map/ppermute | solution.py:618
  247.5 1.5 copy.34
  249.0 1.3 select_add_fusion
  250.3 0.0 all-reduce.3.cloned.1.call-update
  250.3 0.0 reduce-scatter.3.cloned.1.call-start
  250.3 0.7 reduce-scatter.3.cloned.1.call-update
  251.0 0.0 reduce-scatter.5.cloned.1.call-start
  251.1 0.0 copy-start.3
  251.1 0.0 copy-start.6
  251.1 0.7 reduce-scatter.5.cloned.1.call-update
  251.8 1.8 collective-permute-start.1
  253.6 0.0 copy-done.3
  253.6 0.9 collective-permute-start
  254.5 0.8 slice.79
  255.3 0.1 maximum_select_fusion
  255.4 0.7 slice_multiply_fusion.1
  256.1 0.0 copy-done.6
  256.2 123.2 %psum.15 = f32[10,768]{1,0:T(8,128)S(1)} all-reduce(f32[10,768]{1,0:T(8,128)S(1)} %pad_maximum_fusion.3), channel_id=1, replica_groups=mesh['dp'=8,'mp'=4] {'dp','mp'}, use_global_device_ids=true, to_apply=%region_1.2 | all-reduce | flops 7680 | bytes 61440 | tf_op jit(solution)/shard_map/psum | solution.py:627
  379.4 0.6 dynamic-slice_reduce_fusion
  380.0 0.6 slice_reduce_fusion
  380.6 2.7 copy.35
  383.4 0.0 collective-permute-done.1
  383.4 2.7 broadcast_select_fusion.1
  386.1 2.5 pad_maximum_fusion.1
  388.6 0.0 collective-permute-done
  388.6 0.1 copy-done.4
  388.7 3.7 broadcast_select_fusion.3
  392.4 1.0 select_bitcast_fusion.1
  393.4 1.5 collective-permute-start.3
  394.9 4.2 pad_maximum_fusion
  399.1 0.0 collective-permute-done.3
  399.1 0.1 convert_add_fusion.1
  399.1 13.1 %reduce-scatter.5.cloned.1.call-done = bf16[2,96,1536]{2,1,0:T(8,128)(2,1)} async-done(((bf16[2,768,1536]{2,1,0:T(8,128)(2,1)}), bf16[2,96,1536]{2,1,0:T(8,128)(2,1)}) %reduce-scatter.5.cloned.1.call-update) | async-done | bytes 589840 | tf_op jit(solution)/shard_map/reduce_scatter | solution.py:600
  412.2 1.1 select_bitcast_fusion
  413.4 1.5 collective-permute-start.4
  414.9 0.1 slice_bitcast_fusion.1
  415.0 0.7 copy.36
  415.8 0.7 pad_maximum_fusion.2
  416.5 5.6 %collective-permute-done.4 = bf16[96,1536]{1,0:T(8,128)(2,1)} collective-permute-done((bf16[96,1536]{1,0:T(8,128)(2,1)S(1)}, bf16[96,1536]{1,0:T(8,128)(2,1)}, u32[]{:S(2)}, u32[]{:S(2)}) %collective-permute-start.4) | collective-permute-done | bytes 294944 | tf_op jit(solution)/shard_map/ppermute | solution.py:603
  422.1 1.1 convert_add_fusion
  423.2 0.9 slice_bitcast_fusion
  (19 shorter events, 0.2 us)
Async XLA Ops:
  7.2 9.2 %copy-start = (bf16[1000,768]{1,0:T(8,128)(2,1)S(1)}, bf16[1000,768]{1,0:T(8,128)(2,1)}, u32[]{:S(2)}) copy-start(bf16[1000,768]{1,0:T(8,128)(2,1)} %param.18) | copy-start | bytes 4608004
  7.2 373.4 %all-reduce.3.cloned.1.call-start = ((), (), s32[]{:S(2)}) async-start(), calls=%async_computation.2 | async-start | bytes 2048000 | tf_op jit(solution)/shard_map/psum | solution.py:621
  222.4 25.1 %collective-permute-start.2 = (f32[1000,192]{0,1:T(8,128)S(1)}, f32[1000,192]{0,1:T(8,128)}, u32[]{:S(2)}, u32[]{:S(2)}) collective-permute-start(f32[1000,192]{0,1:T(8,128)S(1)} %copy.33), channel_id=1, source_target_pairs={{0,1},{1,0},{2,3},{3,2},{4,5},{5,4},{6,7},{7,6},{8,9},{9,8},{10,11... | collective-permute-start | bytes 2304008 | tf_op jit(solution)/shard_map/ppermute | solution.py:618
  250.3 142.1 %reduce-scatter.3.cloned.1.call-start = ((), (), s32[]{:S(2)}) async-start(), calls=%async_computation.3 | async-start | bytes 2654208 | tf_op jit(solution)/shard_map/reduce_scatter | solution.py:600
  251.0 161.2 %reduce-scatter.5.cloned.1.call-start = ((), (), s32[]{:S(2)}) async-start(), calls=%async_computation.4 | async-start | bytes 5308416 | tf_op jit(solution)/shard_map/reduce_scatter | solution.py:600
  251.1 2.5 copy-start.3
  251.1 5.0 %copy-start.6 = (f32[8,768]{1,0:T(8,128)S(1)}, f32[8,768]{1,0:T(8,128)}, u32[]{:S(2)}) copy-start(f32[8,768]{1,0:T(8,128)} %get-tuple-element.46) | copy-start | bytes 73732
  251.8 131.6 %collective-permute-start.1 = (bf16[1536,768]{1,0:T(8,128)(2,1)}, bf16[1536,768]{1,0:T(8,128)(2,1)}, u32[]{:S(2)}, u32[]{:S(2)}) collective-permute-start(bf16[1536,768]{1,0:T(8,128)(2,1)} %get-tuple-element.43), channel_id=1, source_target_pairs={{0,1},{1,0},{2,3},{3,2},{4,5},{5,4},{6,7},{7,6},{8,9},{9,8},{10,11... | collective-permute-start | bytes 7077896 | tf_op jit(solution)/shard_map/ppermute | solution.py:589
  253.6 135.0 %collective-permute-start = (bf16[1536,768]{1,0:T(8,128)(2,1)S(1)}, bf16[1536,768]{1,0:T(8,128)(2,1)}, u32[]{:S(2)}, u32[]{:S(2)}) collective-permute-start(bf16[1536,768]{1,0:T(8,128)(2,1)S(1)} %copy-done.3), channel_id=1, source_target_pairs={{0,1},{1,0},{2,3},{3,2},{4,5},{5,4},{6,7},{7,6},{8,9},{9,8},{10,11... | collective-permute-start | bytes 7077896 | tf_op jit(solution)/shard_map/ppermute | solution.py:585
  386.1 2.6 copy-start.4
  393.4 5.7 %collective-permute-start.3 = (bf16[96,768]{1,0:T(8,128)(2,1)S(1)}, bf16[96,768]{1,0:T(8,128)(2,1)S(1)}, u32[]{:S(2)}, u32[]{:S(2)}) collective-permute-start(bf16[96,768]{1,0:T(8,128)(2,1)S(1)} %select_bitcast_fusion.1), channel_id=1, source_target_pairs={{0,1},{1,0},{2,3},{3,2},{4,5},{5,4},{6,7},{7,6},{8,9},{9,8},{10,11... | collective-permute-start | bytes 442376 | tf_op jit(solution)/shard_map/ppermute | solution.py:603
  394.9 4.2 copy-start.5
  399.1 24.9 %copy-start.1 = (bf16[1000,768]{1,0:T(8,128)(2,1)S(1)}, bf16[1000,768]{1,0:T(8,128)(2,1)}, u32[]{:S(2)}) copy-start(bf16[1000,768]{1,0:T(8,128)(2,1)} %param.18) | copy-start | bytes 4608004
  412.2 9.9 %copy-start.2 = (bf16[2,96,1536]{2,1,0:T(8,128)(2,1)S(1)}, bf16[2,96,1536]{2,1,0:T(8,128)(2,1)}, u32[]{:S(2)}) copy-start(bf16[2,96,1536]{2,1,0:T(8,128)(2,1)} %reduce-scatter.5.cloned.1.call-done) | copy-start | bytes 1769476
  413.4 8.7 %collective-permute-start.4 = (bf16[96,1536]{1,0:T(8,128)(2,1)S(1)}, bf16[96,1536]{1,0:T(8,128)(2,1)}, u32[]{:S(2)}, u32[]{:S(2)}) collective-permute-start(bf16[96,1536]{1,0:T(8,128)(2,1)S(1)} %select_bitcast_fusion), channel_id=1, source_target_pairs={{0,1},{1,0},{2,3},{3,2},{4,5},{5,4},{6,7},{7,6},{8,9},{9,8},{10,11... | collective-permute-start | bytes 884744 | tf_op jit(solution)/shard_map/ppermute | solution.py:603
Sparse Core Ops, SparseCore 0:
  250.4 59.5 all-reduce.2
  313.4 41.5 reduce-scatter.2
  358.4 53.7 reduce-scatter.4

commit v2 on v1

--- a/solution.py
+++ b/solution.py
@@ -15,6 +15,7 @@
 BLOCK = 512
 WIN = 256
 TILE = 512
+GROUP = 8
 EPS = 1e-05
 GELU_C = 0.7978845608028654
 GELU_A = 0.044715
@@ -98,15 +99,54 @@
     mid_ref[...] += mm(ctx_acc[...], wo_ref[...])
 
 
+def line_up(n):
+    place = lax.axis_index("dp")
+    spot = lax.rem(place, GROUP)
+    return place - spot, spot
+
+
+def ahead(ref, rows, dst, send, recv, target):
+    return pltpu.make_async_remote_copy(
+        src_ref=ref.at[rows] if rows is not None else ref,
+        dst_ref=dst.at[rows] if rows is not None else dst,
+        send_sem=send, recv_sem=recv, device_id=target, device_id_type=pl.DeviceIdType.MESH,
+    )
+
+
+def mate_of(member):
+    return {"dp": lax.axis_index("dp"), "mp": member + 1 - 2 * lax.rem(member, 2)}
+
+
+def greet(targets):
+    barrier = pltpu.get_barrier_semaphore()
+    for target in targets:
+        pl.semaphore_signal(barrier, inc=1, device_id=target, device_id_type=pl.DeviceIdType.MESH)
+    pl.semaphore_wait(barrier, len(targets))
+
+
 def mlp_kernel(
-    meta, mid_ref, gy_ref, wu_ref, bu_ref, wd_ref, gain_ref, shift_ref, db_ref,
+    mid_ref, gy_ref, wu_ref, bu_ref, wd_ref, gain_ref, shift_ref, db_ref,
     out_ref, gmid_ref, gw_ref, vec_ref, gbu_ref,
-    acc_u, acc_d, n2_ref, n2t_ref, gyt_ref, mlp_ref, dn_ref,
+    acc_u, acc_d, n2_ref, n2t_ref, gyt_ref, mlp_ref, dn_ref, stage, loc_sem, send_sem, recv_sem,
 ):
     tile = pl.program_id(0)
-    last = pl.num_programs(0) - 1
-    pair = meta[1]
+    steps = pl.num_programs(0)
+    last = steps - 1
+    member = lax.axis_index("mp")
+    half = lax.rem(member, 2)
+    pair = member // 2
+    mate = mate_of(member)
     ff = wu_ref.shape[2]
+    total = out_ref.shape[0] // (2 * TILE)
+
+    def rows_of(t):
+        return pl.ds(pl.multiple_of((half * total + t) * TILE, TILE), TILE)
+
+    def local_copy(t):
+        return pltpu.make_async_copy(stage.at[lax.rem(t, 2)], out_ref.at[rows_of(t)], loc_sem.at[t])
+
+    def remote_copy(t):
+        return ahead(out_ref, rows_of(t), out_ref, send_sem.at[t], recv_sem.at[t], mate)
 
     @pl.when(tile == 0)
     def _():
@@ -114,6 +154,12 @@
         acc_d[...] = jnp.zeros_like(acc_d)
         vec_ref[...] = jnp.zeros_like(vec_ref)
         gbu_ref[...] = jnp.zeros_like(gbu_ref)
+        greet([mate])
+
+    @pl.when(tile > 0)
+    def _():
+        local_copy(tile - 1).wait()
+        remote_copy(tile - 1).start()
 
     hat, inv = norm_stats(mid_ref[...])
     normed = (hat * gain_ref[...] + shift_ref[...]).astype(BF16)
@@ -145,7 +191,7 @@
     lax.fori_loop(0, 2, lambda turn, c: (step(turn, True), c)[1], 0)
     lax.fori_loop(2, 4, lambda turn, c: (step(turn, False), c)[1], 0)
 
-    out_ref[...] = mlp_ref[...].astype(BF16)
+    stage[lax.rem(tile, 2)] = mlp_ref[...].astype(BF16)
     hat, inv = norm_stats(mid_ref[...])
     top = gy_ref[...].astype(F32)
     dn = dn_ref[...]
@@ -155,30 +201,130 @@
     vec_ref[2:3] += jnp.sum(gmid, axis=0, keepdims=True)
     vec_ref[3:4] += jnp.sum(top, axis=0, keepdims=True)
     gmid_ref[...] = gmid
+    local_copy(tile).start()
 
     @pl.when(tile == last)
     def _():
         gw_ref[:, :, 0:ff] = acc_u[...].astype(BF16)
         gw_ref[:, :, ff : 2 * ff] = acc_d[...].astype(BF16)
+        local_copy(tile).wait()
+        for t in range(total - 1):
+            remote_copy(t).wait_send()
+            remote_copy(t).wait_recv()
 
 
 def attn_bwd_kernel(
-    meta, hidden_ref, emb_ref, gain_ref, shift_ref, wqkv_ref, wo_ref,
-    qkv_ref, probs_ref, ctx_ref, gmid_ref,
-    gh_ref, gw_ref, vec_ref, usum_ref,
-    acc, gp_ref, gc_ref, n1t_ref, gmt_ref,
+    hidden_ref, emb_ref, gain_ref, shift_ref, wqkv_ref, wo_ref,
+    qkv_ref, probs_ref, ctx_ref, gmid_ref, gwm_ref, vecm_ref, gbu_ref, out_in,
+    out_ref, gh_ref, gm_ref, ga_ref, vec_out, u_out,
+    acc, gp_ref, gc_ref, n1t_ref, gmt_ref, vec_ref, usum_ref, stage,
+    m_own, m_core, m_sum, m_chip, m_give, m_got,
+    a_src, a_core, a_sum, a_chip, a_give, a_got,
+    s_src, s_rcv, v_src, v_rcv, u_give, u_got,
+    own_sem, out_send, out_recv, loc_sem, gh_send, gh_recv,
+    core_send, core_recv, chip_send, chip_recv, give_send, give_recv,
+    s_send, s_recv, v_send, v_recv, u_send, u_recv,
 ):
     tile = pl.program_id(0)
     last = pl.num_programs(0) - 1
-    pair_id = meta[1]
+    member = lax.axis_index("mp")
+    half = lax.rem(member, 2)
+    pair_id = member // 2
     width = wo_ref.shape[1]
     part_w = width // 2
+    piece = part_w // 2
+    share = width // GROUP
+    total = out_ref.shape[0] // (2 * TILE)
+    base, spot = line_up(0)
+    core = lax.rem(spot, 2)
+    chip = spot // 2
+    bit_x = lax.rem(chip, 2)
+    bit_y = chip // 2
+    mate = mate_of(member)
+    flips = (
+        chip + 1 - 2 * bit_x,
+        chip + 2 - 4 * bit_y,
+        3 - chip,
+    )
+
+    def device(where):
+        return {"dp": base + where, "mp": member}
+
+    sibling = device(spot + 1 - 2 * core)
+    others = [device(lax.rem(spot + turn, GROUP)) for turn in range(1, GROUP)]
+    line = [{"dp": base + spot, "mp": lax.rem(member + turn, 4)} for turn in range(1, 4)]
+
+    def rows_of(t):
+        return pl.ds(pl.multiple_of((half * total + t) * TILE, TILE), TILE)
+
+    def share_of(where):
+        return pl.ds(pl.multiple_of(where * share, 32), share)
+
+    def out_copy(t):
+        return ahead(out_ref, rows_of(t), out_ref, out_send, out_recv, mate)
+
+    def gh_local(t):
+        return pltpu.make_async_copy(stage.at[lax.rem(t, 2)], gh_ref.at[rows_of(t)], loc_sem.at[t])
+
+    def gh_copy(t):
+        return ahead(gh_ref, rows_of(t), gh_ref, gh_send.at[t], gh_recv.at[t], mate)
+
+    def own_copy(k):
+        return pltpu.make_async_copy(gwm_ref.at[:, share_of(2 * k + core), :], m_own.at[k], own_sem.at[k])
+
+    def core_copy(kind, k):
+        src, dst = ((gwm_ref, m_core), (a_src, a_core))[kind]
+        return pltpu.make_async_remote_copy(
+            src_ref=src.at[:, share_of(2 * k + 1 - core), :], dst_ref=dst.at[k],
+            send_sem=core_send.at[kind, k], recv_sem=core_recv.at[kind, k],
+            device_id=sibling, device_id_type=pl.DeviceIdType.MESH,
+        )
+
+    def chip_copy(kind, r):
+        src, dst = ((m_sum, m_chip), (a_sum, a_chip))[kind]
+        return pltpu.make_async_remote_copy(
+            src_ref=src.at[flips[r]], dst_ref=dst.at[r],
+            send_sem=chip_send.at[kind, r], recv_sem=chip_recv.at[kind, r],
+            device_id=device(2 * flips[r] + core), device_id_type=pl.DeviceIdType.MESH,
+        )
+
+    def give_copy(kind):
+        src, dst = ((m_give, m_got), (a_give, a_got))[kind]
+        return ahead(src, None, dst, give_send.at[kind], give_recv.at[kind], mate)
+
+    def small_copy(n):
+        return pltpu.make_async_remote_copy(
+            src_ref=s_src, dst_ref=s_rcv.at[spot],
+            send_sem=s_send.at[n], recv_sem=s_recv.at[n],
+            device_id=others[n], device_id_type=pl.DeviceIdType.MESH,
+        )
+
+    def line_copy(n):
+        return pltpu.make_async_remote_copy(
+            src_ref=v_src, dst_ref=v_rcv.at[member],
+            send_sem=v_send.at[n], recv_sem=v_recv.at[n],
+            device_id=line[n], device_id_type=pl.DeviceIdType.MESH,
+        )
+
+    def u_copy():
+        return ahead(u_give, None, u_got, u_send, u_recv, mate)
 
     @pl.when(tile == 0)
     def _():
         acc[...] = jnp.zeros_like(acc)
         vec_ref[...] = jnp.zeros_like(vec_ref)
         usum_ref[...] = jnp.zeros_like(usum_ref)
+        greet(others + line)
+        out_copy(total - 1).start()
+        for k in range(4):
+            core_copy(0, k).start()
+        for k in range(4):
+            own_copy(k).start()
+
+    @pl.when(tile > 0)
+    def _():
+        gh_local(tile - 1).wait()
+        gh_copy(tile - 1).start()
 
     own = pl.ds(pl.multiple_of(pair_id * part_w, 128), part_w)
     stream = stream_tile(hidden_ref, emb_ref, tile)
@@ -207,38 +353,181 @@
                 probs = probs_low.astype(F32)
                 dprob = mm_nt(gc1, v2)
                 mix = probs * dprob
-                total = jnp.sum(mix, axis=-1, keepdims=True)
-                grad_s = (mix - probs * total).astype(BF16)
+                total_row = jnp.sum(mix, axis=-1, keepdims=True)
+                grad_s = (mix - probs * total_row).astype(BF16)
                 dv.append(mm_tn(probs_low, gc2))
                 dk.append(mm_tn(grad_s, q2))
                 dq.append(mm(grad_s, k2))
             gp_ref[0, rows, cols] = (jnp.where(low, dq[0], dq[1]) * scale).astype(BF16)
             gp_ref[1, rows, cols] = (jnp.where(low, dk[0], dk[1]) * scale).astype(BF16)
             gp_ref[2, rows, cols] = jnp.where(low, dv[0], dv[1]).astype(BF16)
+
+    @pl.when(tile == 0)
+    def _():
+        for k in range(4):
+            own_copy(k).wait()
+            core_copy(0, k).wait_recv()
+            m_sum[k] = (m_own[k].astype(F32) + m_core[k].astype(F32)).astype(BF16)
+
     grad_n = mm(gp_ref[0], wqkv_ref[0])
     for part in range(1, 3):
         grad_n = grad_n + mm(gp_ref[part], wqkv_ref[part])
     for part in range(3):
         acc[part] += mm(n1t_ref[...], gp_ref[part, :, own])
+
+    @pl.when(tile == 0)
+    def _():
+        for r in range(3):
+            chip_copy(0, r).start()
+
     stream = stream_tile(hidden_ref, emb_ref, tile)
     hat, inv = norm_stats(stream)
     vec_ref[0:1] += jnp.sum(grad_n * hat, axis=0, keepdims=True)
     vec_ref[1:2] += jnp.sum(grad_n, axis=0, keepdims=True)
     grad_in = gmid_ref[...] + norm_back(grad_n, gain_ref[...], hat, inv)
-    gh_ref[...] = grad_in.astype(BF16)
+    stage[lax.rem(tile, 2)] = grad_in.astype(BF16)
     for unit in range(TILE // LEN_A):
         usum_ref[pl.ds(tile * (TILE // LEN_A) + unit, 1), :] = jnp.sum(
             grad_in[unit * LEN_A : (unit + 1) * LEN_A], axis=0, keepdims=True
         )
+    gh_local(tile).start()
 
     @pl.when(tile == last)
     def _():
-        piece = part_w // 2
+        units = usum_ref.shape[0]
         for group in range(2):
             for part in range(4):
-                gw_ref[group, :, part * piece : (part + 1) * piece] = acc[
+                a_src[group, :, part * piece : (part + 1) * piece] = acc[
                     part, :, group * piece : (group + 1) * piece
                 ].astype(BF16)
+        s_src[0:units, :] = usum_ref[:, own]
+        for left in range(2):
+            cols = slice(left * part_w, (left + 1) * part_w)
+            at = units + 8 * left
+            s_src[at : at + 2, :] = vec_ref[0:2, cols]
+            s_src[at + 2 : at + 6, :] = vecm_ref[0:4, cols]
+            s_src[at + 6 : at + 7, :] = gbu_ref[0, 0:1, cols]
+            s_src[at + 7 : at + 8, :] = gbu_ref[1, 0:1, cols]
+        gh_local(tile).wait()
+        gh_copy(tile).start()
+        for k in range(4):
+            core_copy(1, k).start()
+        s_rcv[spot] = s_src[...]
+        for n in range(GROUP - 1):
+            small_copy(n).start()
+        for r in range(3):
+            chip_copy(0, r).wait_recv()
+        kept_m = m_sum[chip, half].astype(F32)
+        give_m = m_sum[chip, 1 - half].astype(F32)
+        for r in range(3):
+            kept_m = kept_m + m_chip[r, half].astype(F32)
+            give_m = give_m + m_chip[r, 1 - half].astype(F32)
+        m_give[...] = give_m.astype(BF16)
+        gm_ref[...] = kept_m
+        for k in range(4):
+            core_copy(1, k).wait_recv()
+            a_sum[k] = (
+                a_src[:, share_of(2 * k + core), :].astype(F32) + a_core[k].astype(F32)
+            ).astype(BF16)
+        give_copy(0).start()
+        for n in range(GROUP - 1):
+            small_copy(n).wait_recv()
+        for r in range(3):
+            chip_copy(1, r).start()
+        v_sum = s_rcv[0, units : units + 16, :]
+        for n in range(1, GROUP):
+            v_sum = v_sum + s_rcv[n, units : units + 16, :]
+        v_src[...] = v_sum
+        v_rcv[member] = v_sum
+        for n in range(GROUP):
+            whole_u = s_rcv[n, 0:units, :]
+            left, right = whole_u[:, :piece], whole_u[:, piece:]
+            u_give[n] = jnp.where(half == 0, right, left)
+            u_out[0, n] = jnp.where(half == 0, left, right)
+        for n in range(3):
+            line_copy(n).start()
+        u_copy().start()
+        give_copy(0).wait_recv()
+        gm_ref[...] += m_got[...].astype(F32)
+        for n in range(3):
+            line_copy(n).wait_recv()
+        every = 0.5 * ((v_rcv[0] + v_rcv[1]) + (v_rcv[2] + v_rcv[3]))
+        other = member + 1 - 2 * half
+        mine = v_rcv[member] + v_rcv[other]
+        for left in range(2):
+            cols = slice(left * part_w, (left + 1) * part_w)
+            at = 8 * left
+            vec_out[0:6, cols] = every[at : at + 6]
+            vec_out[6:7, cols] = jnp.where(half == 0, mine[at + 6 : at + 7], mine[at + 7 : at + 8])
+        u_copy().wait_recv()
+        u_out[1] = u_got[...]
+        for r in range(3):
+            chip_copy(1, r).wait_recv()
+        kept_a = a_sum[chip, half].astype(F32)
+        give_a = a_sum[chip, 1 - half].astype(F32)
+        for r in range(3):
+            kept_a = kept_a + a_chip[r, half].astype(F32)
+            give_a = give_a + a_chip[r, 1 - half].astype(F32)
+        a_give[...] = give_a.astype(BF16)
+        ga_ref[...] = kept_a
+        give_copy(1).start()
+        give_copy(1).wait_recv()
+        ga_ref[...] += a_got[...].astype(F32)
+        out_copy(total - 1).wait_recv()
+        out_copy(total - 1).wait_send()
+        for t in range(total):
+            gh_copy(t).wait_recv()
+            gh_copy(t).wait_send()
+        for kind in range(2):
+            for k in range(4):
+                core_copy(kind, k).wait_send()
+            for r in range(3):
+                chip_copy(kind, r).wait_send()
+            give_copy(kind).wait_send()
+        for n in range(GROUP - 1):
+            small_copy(n).wait_send()
+        for n in range(3):
+            line_copy(n).wait_send()
+        u_copy().wait_send()
+
+
+def finish_kernel(
+    out_in, gh_in, gm_ref, ga_ref, vec_ref, u_ref, ts_ref,
+    out_ref, gh_ref, table_ref, g1_ref, s1_ref, qkv_ref, wo_ref, ob_ref,
+    g2_ref, s2_ref, up_ref, ub_ref, down_ref, db_ref,
+):
+    out_ref[...] = out_in[...]
+    gh_ref[...] = gh_in[...]
+
+    @pl.when(pl.program_id(0) == 0)
+    def _():
+        ff = up_ref.shape[1]
+        piece = qkv_ref.shape[2]
+        up_ref[...] = gm_ref[:, 0:ff]
+        down_ref[...] = gm_ref[:, ff : 2 * ff].T
+        for part in range(3):
+            qkv_ref[part] = ga_ref[:, part * piece : (part + 1) * piece]
+        wo_ref[...] = ga_ref[:, 3 * piece : 4 * piece].T
+        for n, ref in enumerate((g1_ref, s1_ref, g2_ref, s2_ref, ob_ref, db_ref, ub_ref)):
+            ref[...] = vec_ref[n]
+        member = lax.axis_index("mp")
+        half = lax.rem(member, 2)
+        steps = table_ref.shape[0]
+        at = lax.broadcasted_iota(jnp.int32, (16, steps), 1)
+        table = jnp.zeros(table_ref.shape, F32)
+        picks, parts = [], [[], [], []]
+        for n in range(GROUP):
+            for side in range(2):
+                picks.append((ts_ref[n, 16 * side : 16 * side + 16, 0:1] == at).astype(F32))
+                value = jnp.where(half == side, u_ref[0, n], u_ref[1, n])
+                parts[0].append(value)
+        pick = jnp.concatenate(picks, axis=0).astype(BF16)
+        rest = jnp.concatenate(parts[0], axis=0)
+        for _ in range(3):
+            low = rest.astype(BF16)
+            table = table + mm_tn(pick, low)
+            rest = rest - low.astype(F32)
+        table_ref[...] = table
 
 
 def whole(shape):
@@ -289,85 +578,150 @@
     )(meta, hidden, emb, gain, shift, wqkv, wo, ob)
 
 
-def mlp(meta, mid, gy, wu, bu, wd, gain, shift, db):
+def half_map(steps):
+    return lambda i: (lax.rem(lax.axis_index("mp"), 2) * steps + i, 0)
+
+
+def fixed(shape):
+    zeros = (0,) * len(shape)
+    return pl.BlockSpec(shape, lambda i: zeros, pipeline_mode=pl.Buffered(1))
+
+
+def mlp(mid, gy, wu, bu, wd, gain, shift, db):
     count, width = mid.shape
     steps = count // TILE
     ff = wu.shape[2]
-    tok = pl.BlockSpec((TILE, width), lambda i, meta: (i, 0))
+    tok = pl.BlockSpec((TILE, width), lambda i: (i, 0))
+    dma = pltpu.SemaphoreType.DMA
     return pl.pallas_call(
         mlp_kernel,
         name="mlp_both",
-        grid_spec=pltpu.PrefetchScalarGridSpec(
-            num_scalar_prefetch=1,
-            grid=(steps,),
-            in_specs=[
-                tok,
-                pl.BlockSpec((TILE, width), lambda i, meta: (meta[0] * steps + i, 0)),
-                whole(wu.shape), whole(bu.shape), whole(wd.shape),
-                whole((1, width)), whole((1, width)), whole((1, width)),
-            ],
-            out_specs=[tok, tok, whole((2, width, 2 * ff)), held((8, width)), held((2, 8, ff))],
-            scratch_shapes=[
-                pltpu.VMEM((2, width, ff), F32), pltpu.VMEM((2, width, ff), F32),
-                pltpu.VMEM((TILE, width), BF16), pltpu.VMEM((width, TILE), BF16),
-                pltpu.VMEM((width, TILE), BF16),
-                pltpu.VMEM((TILE, width), F32), pltpu.VMEM((TILE, width), F32),
-            ],
-        ),
+        grid=(steps,),
+        in_specs=[
+            tok,
+            pl.BlockSpec((TILE, width), half_map(steps)),
+            fixed(wu.shape), fixed(bu.shape), fixed(wd.shape),
+            fixed((1, width)), fixed((1, width)), fixed((1, width)),
+        ],
+        out_specs=[
+            pl.BlockSpec(memory_space=pl.ANY), tok, fixed((2, width, 2 * ff)),
+            fixed((8, width)), fixed((2, 8, ff)),
+        ],
+        scratch_shapes=[
+            pltpu.VMEM((2, width, ff), F32), pltpu.VMEM((2, width, ff), F32),
+            pltpu.VMEM((TILE, width), BF16), pltpu.VMEM((width, TILE), BF16),
+            pltpu.VMEM((width, TILE), BF16),
+            pltpu.VMEM((TILE, width), F32), pltpu.VMEM((TILE, width), F32),
+            pltpu.VMEM((2, TILE, width), BF16), dma((steps,)), dma((steps,)), dma((steps,)),
+        ],
         out_shape=[
-            jax.ShapeDtypeStruct((count, width), BF16),
+            jax.ShapeDtypeStruct((2 * count, width), BF16),
             jax.ShapeDtypeStruct((count, width), F32),
             jax.ShapeDtypeStruct((2, width, 2 * ff), BF16),
             jax.ShapeDtypeStruct((8, width), F32),
             jax.ShapeDtypeStruct((2, 8, ff), F32),
         ],
-        compiler_params=pltpu.CompilerParams(vmem_limit_bytes=LIMIT),
+        compiler_params=pltpu.CompilerParams(
+            collective_id=2, has_side_effects=True, vmem_limit_bytes=LIMIT
+        ),
         cost_estimate=pl.CostEstimate(flops=36_000_000_000, bytes_accessed=30_000_000, transcendentals=5_000_000),
-    )(meta, mid, gy, wu, bu, wd, gain, shift, db)
-
-
-def attn_bwd(meta, hidden, emb, gain, shift, wqkv, wo, qkv, probs, ctx, gmid):
+    )(mid, gy, wu, bu, wd, gain, shift, db)
+
+
+def attn_bwd(hidden, emb, gain, shift, wqkv, wo, qkv, probs, ctx, gmid, gwm, vecm, gbu, out):
     count, width = gmid.shape
     steps = count // TILE
     heads = width // HD
-    tok = pl.BlockSpec((TILE, width), lambda i, meta: (i, 0))
+    share = width // GROUP
+    wide = gwm.shape[2]
+    units = emb.shape[0]
+    piece = width // 4
+    tok = pl.BlockSpec((TILE, width), lambda i: (i, 0))
+    anywhere = pl.BlockSpec(memory_space=pl.ANY)
+    dma = pltpu.SemaphoreType.DMA
     return pl.pallas_call(
         attn_bwd_kernel,
         name="attn_bwd",
-        grid_spec=pltpu.PrefetchScalarGridSpec(
-            num_scalar_prefetch=1,
-            grid=(steps,),
-            in_specs=[
-                pl.BlockSpec((TILE, width), lambda i, meta: (meta[0] * steps + i, 0)),
-                whole(emb.shape), whole((1, width)), whole((1, width)),
-                whole(wqkv.shape), whole(wo.shape),
-                pl.BlockSpec((3, TILE, width), lambda i, meta: (0, i, 0)),
-                pl.BlockSpec((heads, TILE // WIN, WIN, WIN), lambda i, meta: (0, i, 0, 0)),
-                tok, tok,
-            ],
-            out_specs=[tok, whole((2, width, width)), held((8, width)), held(emb.shape)],
-            scratch_shapes=[
-                pltpu.VMEM((4, width, width // 2), F32),
-                pltpu.VMEM((3, TILE, width), BF16), pltpu.VMEM((TILE, width), BF16),
-                pltpu.VMEM((width, TILE), BF16), pltpu.VMEM((width, TILE), BF16),
-            ],
+        grid=(steps,),
+        in_specs=[
+            pl.BlockSpec((TILE, width), half_map(steps)),
+            fixed(emb.shape), fixed((1, width)), fixed((1, width)),
+            fixed(wqkv.shape), fixed(wo.shape),
+            pl.BlockSpec((3, TILE, width), lambda i: (0, i, 0)),
+            pl.BlockSpec((heads, TILE // WIN, WIN, WIN), lambda i: (0, i, 0, 0)),
+            tok, tok, anywhere, fixed(vecm.shape), fixed(gbu.shape), anywhere,
+        ],
+        out_specs=[
+            anywhere, anywhere, fixed((share, wide)), fixed((share, width)),
+            fixed((8, width)), fixed((2, GROUP, units, piece)),
+        ],
+        scratch_shapes=[
+            pltpu.VMEM((4, width, width // 2), F32),
+            pltpu.VMEM((3, TILE, width), BF16), pltpu.VMEM((TILE, width), BF16),
+            pltpu.VMEM((width, TILE), BF16), pltpu.VMEM((width, TILE), BF16),
+            pltpu.VMEM((8, width), F32), pltpu.VMEM((units, width), F32),
+            pltpu.VMEM((2, TILE, width), BF16),
+            pltpu.VMEM((4, 2, share, wide), BF16), pltpu.VMEM((4, 2, share, wide), BF16),
+            pltpu.VMEM((4, 2, share, wide), BF16), pltpu.VMEM((3, 2, share, wide), BF16),
+            pltpu.VMEM((share, wide), BF16), pltpu.VMEM((share, wide), BF16),
+            pltpu.VMEM((2, width, width), BF16), pltpu.VMEM((4, 2, share, width), BF16),
+            pltpu.VMEM((4, 2, share, width), BF16), pltpu.VMEM((3, 2, share, width), BF16),
+            pltpu.VMEM((share, width), BF16), pltpu.VMEM((share, width), BF16),
+            pltpu.VMEM((units + 16, width // 2), F32), pltpu.VMEM((GROUP, units + 16, width // 2), F32),
+            pltpu.VMEM((16, width // 2), F32), pltpu.VMEM((4, 16, width // 2), F32),
+            pltpu.VMEM((GROUP, units, piece), F32), pltpu.VMEM((GROUP, units, piece), F32),
+            dma((4,)), dma(()), dma(()), dma((steps,)), dma((steps,)), dma((steps,)),
+            dma((2, 4)), dma((2, 4)), dma((2, 3)), dma((2, 3)), dma((2,)), dma((2,)),
+            dma((GROUP - 1,)), dma((GROUP - 1,)), dma((3,)), dma((3,)), dma(()), dma(()),
+        ],
+        out_shape=[
+            jax.ShapeDtypeStruct((2 * count, width), BF16),
+            jax.ShapeDtypeStruct((2 * count, width), BF16),
+            jax.ShapeDtypeStruct((share, wide), F32),
+            jax.ShapeDtypeStruct((share, width), F32),
+            jax.ShapeDtypeStruct((8, width), F32),
+            jax.ShapeDtypeStruct((2, GROUP, units, piece), F32),
+        ],
+        input_output_aliases={13: 0},
+        compiler_params=pltpu.CompilerParams(
+            collective_id=3, has_side_effects=True, vmem_limit_bytes=LIMIT
         ),
-        out_shape=[
-            jax.ShapeDtypeStruct((count, width), BF16),
-            jax.ShapeDtypeStruct((2, width, width), BF16),
-            jax.ShapeDtypeStruct((8, width), F32),
-            jax.ShapeDtypeStruct(emb.shape, F32),
-        ],
+        cost_estimate=pl.CostEstimate(flops=20_000_000_000, bytes_accessed=40_000_000, transcendentals=0),
+    )(hidden, emb, gain, shift, wqkv, wo, qkv, probs, ctx, gmid, gwm, vecm, gbu, out)
+
+
+def finish(out, gh, gm, ga, vec, u, ts, steps):
+    count, width = out.shape
+    share = gm.shape[0]
+    ff = gm.shape[1] // 2
+    piece = width // 4
+    tok = pl.BlockSpec((2 * TILE, width), lambda i: (i, 0))
+    line = jax.ShapeDtypeStruct((width,), F32)
+    shapes = [
+        jax.ShapeDtypeStruct((steps, piece), F32), line, line,
+        jax.ShapeDtypeStruct((3, share, piece), F32), jax.ShapeDtypeStruct((piece, share), F32),
+        line, line, line,
+        jax.ShapeDtypeStruct((share, ff), F32), line, jax.ShapeDtypeStruct((ff, share), F32), line,
+    ]
+    return pl.pallas_call(
+        finish_kernel,
+        name="finish",
+        grid=(count // (2 * TILE),),
+        in_specs=[tok, tok] + [fixed(x.shape) for x in (gm, ga, vec, u, ts)],
+        out_specs=[tok, tok] + [fixed(x.shape) for x in shapes],
+        out_shape=[jax.ShapeDtypeStruct(out.shape, BF16), jax.ShapeDtypeStruct(gh.shape, BF16)] + shapes,
         compiler_params=pltpu.CompilerParams(vmem_limit_bytes=LIMIT),
-        cost_estimate=pl.CostEstimate(flops=20_000_000_000, bytes_accessed=40_000_000, transcendentals=0),
-    )(meta, hidden, emb, gain, shift, wqkv, wo, qkv, probs, ctx, gmid)
+        cost_estimate=pl.CostEstimate(flops=1_000_000, bytes_accessed=20_000_000, transcendentals=0),
+    )(out, gh, gm, ga, vec, u, ts)
+
+
 ARRAYS = 4
 
 
 def gather_kernel(
-    wqkv, wo, wu, wd, bu, wqkv_f, wo_f, wu_f, wd_f, bu_f,
-    hold_qkv, hold_wo, hold_wu, hold_wd, hold_bu,
-    loc_sem, z_send, z_recv, b_send, b_recv, n_send, n_recv,
+    wqkv, wo, wu, wd, bu, ts, wqkv_f, wo_f, wu_f, wd_f, bu_f, ts_f,
+    hold_qkv, hold_wo, hold_wu, hold_wd, hold_bu, hold_ts,
+    loc_sem, z_send, z_recv, b_send, b_recv, n_send, n_recv, t_send, t_recv,
 ):
     place = lax.axis_index("dp")
     member = lax.axis_index("mp")
@@ -393,10 +747,8 @@
     def peer(turn):
         return {"dp": place, "mp": lax.rem(member + turn, 4)}
 
-    barrier = pltpu.get_barrier_semaphore()
-    for target in (peer(1), peer(2), peer(3), near["core"], near["x"], near["y"]):
-        pl.semaphore_signal(barrier, inc=1, device_id=target, device_id_type=pl.DeviceIdType.MESH)
-    pl.semaphore_wait(barrier, 6)
+    others = [{"dp": base + lax.rem(spot + turn, 8), "mp": member} for turn in range(1, 8)]
+    greet([peer(1), peer(2), peer(3)] + others)
 
     rows_a = wo.shape[0]
     step_a = rows_a // 8
@@ -442,6 +794,15 @@
                 copy.start()
                 sends.append(copy)
                 n_recvs["bias", turn] = copy
+            for n in range(7):
+                copy = pltpu.make_async_remote_copy(
+                    src_ref=ts, dst_ref=ts_f.at[spot],
+                    send_sem=t_send.at[n], recv_sem=t_recv.at[n],
+                    device_id=others[n], device_id_type=pl.DeviceIdType.MESH,
+                )
+                copy.start()
+                sends.append(copy)
+                n_recvs["step", n] = copy
 
     own_full = (
         (wqkv, hold_qkv, wqkv_f.at[:, pl.ds(member * rows_a, rows_a), :]),
@@ -449,6 +810,7 @@
         (wu, hold_wu, wu_f.at[member]),
         (wd, hold_wd, wd_f.at[member]),
         (bu, hold_bu, bu_f.at[member]),
+        (ts, hold_ts, ts_f.at[spot]),
     )
     into = [pltpu.make_async_copy(src, hold, loc_sem.at[n]) for n, (src, hold, _) in enumerate(own_full)]
     for copy in into:
@@ -456,7 +818,7 @@
     outof = []
     for n, (_, hold, dst) in enumerate(own_full):
         into[n].wait()
-        copy = pltpu.make_async_copy(hold, dst, loc_sem.at[5 + n])
+        copy = pltpu.make_async_copy(hold, dst, loc_sem.at[6 + n])
         copy.start()
         outof.append(copy)
 
@@ -512,40 +874,47 @@
                 n_recvs[array, turn, kind].wait_recv()
     for turn in (1, 2, 3):
         n_recvs["bias", turn].wait_recv()
+    for n in range(7):
+        n_recvs["step", n].wait_recv()
     for copy in sends:
         copy.wait_send()
     for copy in outof:
         copy.wait()
 
 
-def gather_weights(wqkv, wo, wu, wd, bu):
+def gather_weights(wqkv, wo, wu, wd, bu, ts):
     anywhere = pl.BlockSpec(memory_space=pl.ANY)
     rows, width = wo.shape
     ff = wu.shape[1]
     return pl.pallas_call(
         gather_kernel,
         name="gather_weights",
-        in_specs=[anywhere] * 5,
-        out_specs=[anywhere] * 5,
+        in_specs=[anywhere] * 6,
+        out_specs=[anywhere] * 6,
         out_shape=[
             jax.ShapeDtypeStruct((3, 4 * rows, width), BF16),
             jax.ShapeDtypeStruct((4 * rows, width), BF16),
             jax.ShapeDtypeStruct((4, width, ff), BF16),
             jax.ShapeDtypeStruct((4, ff, width), BF16),
             jax.ShapeDtypeStruct((4,) + bu.shape, F32),
+            jax.ShapeDtypeStruct((GROUP,) + ts.shape, jnp.int32),
         ],
         scratch_shapes=[
             pltpu.VMEM(wqkv.shape, BF16), pltpu.VMEM(wo.shape, BF16),
             pltpu.VMEM(wu.shape, BF16), pltpu.VMEM(wd.shape, BF16), pltpu.VMEM(bu.shape, F32),
-            pltpu.SemaphoreType.DMA((10,)),
+            pltpu.VMEM(ts.shape, jnp.int32),
+            pltpu.SemaphoreType.DMA((12,)),
             pltpu.SemaphoreType.DMA((ARRAYS, 3)), pltpu.SemaphoreType.DMA((ARRAYS, 3)),
             pltpu.SemaphoreType.DMA((3,)), pltpu.SemaphoreType.DMA((3,)),
             pltpu.SemaphoreType.DMA((ARRAYS, 3, 7)), pltpu.SemaphoreType.DMA((ARRAYS, 3, 7)),
+            pltpu.SemaphoreType.DMA((7,)), pltpu.SemaphoreType.DMA((7,)),
         ],
         compiler_params=pltpu.CompilerParams(
             collective_id=1, has_side_effects=True, vmem_limit_bytes=LIMIT
         ),
-    )(wqkv, wo, wu, wd, bu)
+    )(wqkv, wo, wu, wd, bu, ts)
+
+
 def local(
     hidden, timesteps, cotangent, time_table, first_gain, first_shift, qkv_weight, out_weight,
     out_bias, second_gain, second_shift, up_weight, up_bias, down_weight, down_bias,
@@ -555,81 +924,51 @@
     local_ff = up_weight.shape[1]
     member = lax.axis_index("mp")
     half = lax.rem(member, 2)
-    pair = member // 2
-    meta = jnp.stack([half, pair]).astype(jnp.int32)
-    units = count // (2 * LEN_A)
-    unit = half * units + jnp.arange(units, dtype=jnp.int32)
+    meta = jnp.stack([half, member // 2]).astype(jnp.int32)
+    units = count // LEN_A
+    unit = jnp.arange(units, dtype=jnp.int32)
     within = unit % 8
     row_of = unit // 8 * 6 + jnp.where(within < 4, within, 4 + (within - 4) // 2)
-    unit_step = jnp.take(timesteps, row_of)
-    emb = jnp.take(time_table, unit_step, axis=0).astype(F32)
-    emb = jnp.concatenate([emb, jnp.zeros((16 - units, width), F32)], axis=0)
+    unit_step = jnp.pad(
+        jnp.take(timesteps, row_of).reshape(2, units // 2), ((0, 0), (0, 16 - units // 2)), constant_values=-1
+    )
+    emb = jnp.take(time_table, jnp.maximum(unit_step[half], 0), axis=0).astype(F32)
+    stamps = jnp.broadcast_to(unit_step.reshape(32, 1), (32, 128))
 
     def row(v):
         return v.reshape(1, -1)
 
-    wqkv_f, wo_f, wu_f, wd_f, bu_f = gather_weights(
+    wqkv_f, wo_f, wu_f, wd_f, bu_f, ts_f = gather_weights(
         jnp.swapaxes(qkv_weight, 1, 2),
         out_weight,
         up_weight,
         down_weight,
         jnp.broadcast_to(row(up_bias), (8, local_ff)),
+        stamps,
     )
     qkv, probs, ctx, mid = attn_fwd(
         meta, hidden, emb, row(first_gain), row(first_shift), wqkv_f, wo_f, row(out_bias)
     )
-    out_own, gmid, gw_mlp, vec_mlp, gbu = mlp(
-        meta, mid, cotangent, wu_f, bu_f, wd_f, row(second_gain), row(second_shift), row(down_bias)
+    output, gmid, gw_mlp, vec_mlp, gbu = mlp(
+        mid, cotangent, wu_f, bu_f, wd_f, row(second_gain), row(second_shift), row(down_bias)
     )
-    swap = [(0, 1), (1, 0), (2, 3), (3, 2)]
-    out_other = lax.ppermute(out_own, "mp", swap)
-    gh_own, gw_attn, vec_attn, usum = attn_bwd(
-        meta, hidden, emb, row(first_gain), row(first_shift), wqkv_f, wo_f, qkv, probs, ctx, gmid
+    output, grad_hidden, g_mlp, g_attn, vecs, sums = attn_bwd(
+        hidden, emb, row(first_gain), row(first_shift), wqkv_f, wo_f, qkv, probs, ctx, gmid,
+        gw_mlp, vec_mlp, gbu, output,
     )
-    gh_other = lax.ppermute(gh_own, "mp", swap)
-
-    def join(own, other):
-        first = jnp.where(half == 0, own, other)
-        second = jnp.where(half == 0, other, own)
-        return jnp.concatenate([first, second], axis=0)
-
-    output = join(out_own, out_other)
-    grad_hidden = join(gh_own, gh_other)
-
-    def spread(grads):
-        mine = lax.psum_scatter(grads, "dp", scatter_dimension=1, tiled=True)
-        keep = jnp.where(half == 0, mine[0], mine[1]).astype(F32)
-        give = jnp.where(half == 0, mine[1], mine[0])
-        return keep + lax.ppermute(give, "mp", swap).astype(F32)
-
-    g_mlp = spread(gw_mlp)
-    g_attn = spread(gw_attn)
-    grad_up = g_mlp[:, :local_ff]
-    grad_down = g_mlp[:, local_ff:].T
-    head_w = qkv_weight.shape[2]
-    grad_qkv = jnp.stack([g_attn[:, c * head_w : (c + 1) * head_w] for c in range(3)])
-    grad_out = g_attn[:, 3 * head_w :].T
-
-    chosen = (unit_step[:, None] == lax.broadcasted_iota(jnp.int32, (1, steps), 1)).astype(F32)
-    part_w = width // 2
-    sums = lax.dynamic_slice_in_dim(usum[:units], pair * part_w, part_w, 1)
-    table = jnp.dot(chosen.T, sums, precision=lax.Precision.HIGHEST, preferred_element_type=F32)
-    left, right = table[:, : part_w // 2], table[:, part_w // 2 :]
-    table = jnp.where(half == 0, left, right) + lax.ppermute(
-        jnp.where(half == 0, right, left), "mp", swap
-    )
-    table = lax.psum(table, "dp")
-
-    slots = jnp.where(
-        (jnp.arange(4) // 2 == pair)[:, None], jnp.concatenate([gbu[:, 0], gbu[:, 0]], axis=0), 0.0
-    )
-    small = jnp.concatenate([0.5 * vec_attn[:2], 0.5 * vec_mlp[:4], slots], axis=0)
-    small = lax.psum(small, ("dp", "mp"))
-    grad_up_bias = lax.dynamic_slice_in_dim(small[6:], member, 1, 0)[0]
-    return (
-        output, grad_hidden, table, small[0], small[1], grad_qkv, grad_out, small[4],
-        small[2], small[3], grad_up, grad_up_bias, grad_down, small[5],
-    )
+    outs = list(finish(output, grad_hidden, g_mlp, g_attn, vecs, sums, ts_f, steps))
+    groups = lax.axis_size("dp") // GROUP
+    if groups > 1:
+        spots = [[g * GROUP + n for n in range(GROUP)] for g in range(groups)]
+        split = {5: 1, 6: 1, 10: 0, 12: 1}
+        for n in range(2, len(outs)):
+            value = outs[n] * (1.0 / GROUP)
+            if n in split:
+                value = lax.all_gather(value, "dp", axis_index_groups=spots, axis=split[n], tiled=True)
+                outs[n] = lax.psum_scatter(value, "dp", scatter_dimension=split[n], tiled=True)
+            else:
+                outs[n] = lax.psum(value, "dp")
+    return tuple(outs)
 
 
 def solution(mesh):

time: 438 us -> 287 us (0.66); the launches traced: 431 us -> 286 us
  blocking collectives: 123 us -> 0 us
  Pallas kernels: 200 us -> 268 us
  waiting for transfers between devices: 38.4 us -> 0 us
  other arithmetic: 21 us -> 1.37 us
  between operations: 14.4 us -> 0.75 us
  starting transfers between devices: 12.6 us -> 0 us
    psum x1 -> x0, blocking collectives: 123 us -> none  [local(): small = lax.psum(small, ('dp', 'mp'))]
    pallas_call x2 -> x3, Pallas kernels: 107 us -> 174 us  [the longest x1 96.1 us: attn_bwd(): pl.pallas_call(attn_bwd_kernel, name='attn_bwd', grid=(steps,), in_specs=...]
    ppermute x5 -> x0, waiting for transfers between devices: 23.9 us -> none  [the longest x1 18.3 us: local(): lax.ppermute(jnp.where(half == 0, right, left), 'mp', swap)]
    reduce_scatter x2 -> x0, waiting for transfers between devices: 13.1 us -> none  [spread(): mine = lax.psum_scatter(grads, 'dp', scatter_dimension=1, tiled=True)]
    ppermute x5 -> x0, starting transfers between devices: 12.5 us -> none  [the longest x1 6.75 us: local(): lax.ppermute(jnp.where(half == 0, right, left), 'mp', swap)]
    select_n x9 -> x2, other arithmetic: 9.05 us -> 0.05 us  [local(): jnp.take(timesteps, row_of).reshape(2, units // 2)]
    concatenate x4 -> x0, other arithmetic: 7.34 us -> none  [the longest x2 6.69 us: join(): return jnp.concatenate([first, second], axis=0)]
  transfers between devices with their start and end apart: 8 -> 0, of which waited for: 3 -> 0; matrix products, arithmetic and copies ran while one was open for 5% -> 0% of each run, Pallas kernels for 0% -> 0%
where the time goes in v2:
time: 287 us; the launch traced here: 286 us
  Pallas kernels  268 us (93%)
  local copies, waits for them, and re-layouts  16 us (6%)
    pallas_call x1, Pallas kernels, attn_bwd(): pl.pallas_call(attn_bwd_kernel, name='attn_bwd', grid=(steps,), in_specs=...  96.1 us
    pallas_call x1, Pallas kernels, mlp(): pl.pallas_call(mlp_kernel, name='mlp_both', grid=(steps,), in_specs=[tok,...  67.5 us
    pallas_call x1, Pallas kernels, gather_weights(): pl.pallas_call(gather_kernel, name='gather_weights', in_specs=[anywhere]...  67.4 us
    pallas_call x1, Pallas kernels, attn_fwd(): pl.pallas_call(attn_fwd_kernel, name='attn_fwd', grid_spec=pltpu.Prefetch...  27.1 us
    pallas_call x1, Pallas kernels, finish(): pl.pallas_call(finish_kernel, name='finish', grid=(count // (2 * TILE),),...  9.97 us
    reshape x6, local copies, waits for them, and re-layouts, row(): return v.reshape(1, -1)  7.6 us

profile of v2, /device:TPU:0, one launch (start us, length us, event | category | flops | bytes accessed | tf_op | source)
XLA Modules:
  0.0 286.2 jit_solution(12002329833595351564)
XLA Ops:
  0.6 0.0 copy-start
  0.7 0.6 pad_add_fusion.meta
  1.3 1.3 reshape.210.gain_ref
  2.6 1.3 reshape.211.shift_ref
  3.8 1.3 reshape.212.ob_ref
  5.1 1.3 reshape.213.gain_ref
  6.4 1.3 reshape.214.shift_ref
  7.6 1.3 reshape.215.db_ref
  8.9 1.4 gather_fusion
  10.2 0.1 gather.11
  10.4 0.1 broadcast_in_dim.27
  10.5 0.7 broadcast_in_dim.28.ts
  11.2 0.0 copy-done
  11.2 0.6 gather_fusion.1
  11.8 0.7 select_convert_fusion.emb_ref
  12.5 1.3 broadcast_in_dim.26.bu
  13.8 67.4 %gather_weights.1 = (bf16[3,768,768]{2,1,0:T(8,128)(2,1)}, bf16[768,768]{1,0:T(8,128)(2,1)}, bf16[4,768,768]{2,1,0:T(8,128)(2,1)}, bf16[4,768,768]{2,1,0:T(8,128...) custom-call(bf16[3,192,768]{2,1,0:T(8,128)(2,1)} %bitcast.9, bf16[192,768]{1,0:T(8,128)(2,1)} %wo.1, ...), custom_call_target="tpu_custom_call" | custom-call | tf_op jit(solution)/shard_map/gather_weights/pallas_call | solution.py:889
  81.2 27.1 %attn_fwd.1 = (bf16[3,1536,768]{2,1,0:T(8,128)(2,1)}, bf16[12,6,256,256]{3,2,1,0:T(8,128)(2,1)}, bf16[1536,768]{1,0:T(8,128)(2,1)}, f32[1536,768]{1,0:T(8,128)}) custom-call(s32[2]{0:T(128)} %pad_add_fusion.meta, bf16[3072,768]{1,0:T(8,128)(2,1)} %hidden_ref.3, f32[16,768]{1,0:T(8,128)} %select_convert_fusion.emb_ref, f32[1,768]{1,0:T(1,128)} %reshape.210.gain_ref, ...), custom_call_target="tpu_custom_call" | custom-call | flops 12000000000 | bytes 30000000 | tf_op jit(solution)/shard_map/attn_fwd/pallas_call | solution.py:551
  108.3 67.5 %mlp_both.1 = (bf16[3072,768]{1,0:T(8,128)(2,1)}, f32[1536,768]{1,0:T(8,128)}, bf16[2,768,1536]{2,1,0:T(8,128)(2,1)}, f32[8,768]{1,0:T(8,128)}, f32[2,8,768]{2,1,0:T(8,128)}) custom-call(f32[1536,768]{1,0:T(8,128)} %get-tuple-element.40.mid_ref, bf16[3072,768]{1,0:T(8,128)(2,1)} %gy_ref.1, bf16[4,768,768]{2,1,0:T(8,128)(2,1)} %get-tuple-element.41.wu_ref, ...), custom_call_target="tpu_custom_call" | custom-call | flops 35999997952 | bytes 30000000 | tf_op jit(solution)/shard_map/mlp_both/pallas_call | solution.py:596
  175.8 96.1 %attn_bwd.1 = (bf16[3072,768]{1,0:T(8,128)(2,1)}, bf16[3072,768]{1,0:T(8,128)(2,1)}, f32[96,1536]{1,0:T(8,128)}, f32[96,768]{1,0:T(8,128)}, f32[8,768]{1,0:T(8,128)}, /*index=5*/f32[2,8,16,192]{3,2,1,0:T(8,128)}) custom-call(bf16[3072,768]{1,0:T(8,128)(2,1)} %hidden_ref.3, f32[16,768]{1,0:T(8,128)} %select_convert_fusion.emb_ref, ...), custom_call_target="tpu_custom_call", output_to_operand_aliasing={{0}: (13, {})} | custom-call | flops 20000000000 | bytes 40000000 | tf_op jit(solution)/shard_map/attn_bwd/pallas_call | solution.py:642
  271.9 0.0 copy-start.1
  271.9 10.0 %finish.1 = (bf16[3072,768]{1,0:T(8,128)(2,1)}, bf16[3072,768]{1,0:T(8,128)(2,1)}, f32[1000,192]{1,0:T(8,128)}, f32[768]{0:T(1024)}, f32[768]{0:T(1024)}, /*inde...) custom-call(bf16[3072,768]{1,0:T(8,128)(2,1)} %get-tuple-element.49., ...), custom_call_target="tpu_custom_call" | custom-call | flops 1000000 | bytes 20000000 | tf_op jit(solution)/shard_map/finish/pallas_call | solution.py:706
  281.9 1.9 copy.33
  283.8 2.4 copy.32
  286.2 0.0 copy-done.1
  (7 shorter events, 0.1 us)
Async XLA Ops:
  0.6 10.5 %copy-start = (bf16[1000,768]{1,0:T(8,128)(2,1)S(1)}, bf16[1000,768]{1,0:T(8,128)(2,1)}, u32[]{:S(2)}) copy-start(bf16[1000,768]{1,0:T(8,128)(2,1)} %param.18) | copy-start | bytes 4608004
  271.9 14.3 %copy-start.1 = (bf16[1000,768]{1,0:T(8,128)(2,1)S(1)}, bf16[1000,768]{1,0:T(8,128)(2,1)}, u32[]{:S(2)}) copy-start(bf16[1000,768]{1,0:T(8,128)(2,1)} %param.18) | copy-start | bytes 4608004

commit v3 on v2

--- a/solution.py
+++ b/solution.py
@@ -56,18 +56,212 @@
     return jnp.concatenate(parts, axis=0)
 
 
+def line_up():
+    place = lax.axis_index("dp")
+    spot = lax.rem(place, GROUP)
+    return place - spot, spot
+
+
+def ahead(ref, rows, dst, send, recv, target):
+    return pltpu.make_async_remote_copy(
+        src_ref=ref.at[rows] if rows is not None else ref,
+        dst_ref=dst.at[rows] if rows is not None else dst,
+        send_sem=send, recv_sem=recv, device_id=target, device_id_type=pl.DeviceIdType.MESH,
+    )
+
+
+def mate_of(member):
+    return {"dp": lax.axis_index("dp"), "mp": member + 1 - 2 * lax.rem(member, 2)}
+
+
+def greet(targets):
+    barrier = pltpu.get_barrier_semaphore()
+    for target in targets:
+        pl.semaphore_signal(barrier, inc=1, device_id=target, device_id_type=pl.DeviceIdType.MESH)
+    pl.semaphore_wait(barrier, len(targets))
+
+
 def attn_fwd_kernel(
-    meta, hidden_ref, emb_ref, gain_ref, shift_ref, wqkv_ref, wo_ref, ob_ref,
-    qkv_ref, probs_ref, ctx_ref, mid_ref, same_ref, ctx_acc,
+    hidden_ref, emb_ref, gain_ref, shift_ref, ob_ref, bias_ref, ts_ref, wqkv, wo, wu, wd,
+    wqkv_f, wo_f, wu_f, wd_f, bu_f, ts_f, qkv_ref, probs_ref, ctx_ref, mid_ref,
+    same_ref, ctx_acc, wqkv_v, wo_v, norm_v, hold_wu, hold_wd, hold_bu, hold_ts,
+    loc_sem, load_sem, z_send, z_recv, b_send, b_recv, n_send, n_recv, t_send, t_recv,
 ):
     tile = pl.program_id(0)
-    half = meta[0]
+    steps = pl.num_programs(0)
+    last = steps - 1
+    member = lax.axis_index("mp")
+    half = lax.rem(member, 2)
+    place = lax.axis_index("dp")
+    base, spot = line_up()
+    bit0 = lax.rem(spot, 2)
+    bit1 = lax.rem(spot // 2, 2)
+    bit2 = spot // 4
+
+    def flip(where, bit, size):
+        return where + size - 2 * size * bit
+
+    near = {
+        "core": {"dp": flip(place, bit0, 1), "mp": member},
+        "x": {"dp": flip(place, bit1, 2), "mp": member},
+        "y": {"dp": flip(place, bit2, 4), "mp": member},
+    }
+    from_x = flip(spot, bit1, 2)
+    from_y = flip(spot, bit2, 4)
+    from_d = flip(from_x, bit2, 4)
+    others = [{"dp": base + lax.rem(spot + turn, GROUP), "mp": member} for turn in range(1, GROUP)]
+
+    def peer(turn):
+        return {"dp": place, "mp": lax.rem(member + turn, 4)}
+
+    rows_a = wo.shape[0]
+    step_a = rows_a // GROUP
+    step_m = wu.shape[0] // GROUP
+
+    def full_at(array, shard, piece):
+        if array == 0:
+            return wqkv_f.at[:, pl.ds(shard * rows_a + piece * step_a, step_a), :]
+        if array == 1:
+            return wo_f.at[pl.ds(shard * rows_a + piece * step_a, step_a), :]
+        full = wu_f if array == 2 else wd_f
+        return full.at[shard, pl.ds(piece * step_m, step_m), :]
+
+    def own_at(array, piece):
+        if array == 0:
+            return wqkv.at[:, pl.ds(piece * step_a, step_a), :]
+        if array == 1:
+            return wo.at[pl.ds(piece * step_a, step_a), :]
+        return (wu if array == 2 else wd).at[pl.ds(piece * step_m, step_m), :]
+
+    def remote(src, dst, send, recv, target):
+        return pltpu.make_async_remote_copy(
+            src_ref=src, dst_ref=dst, send_sem=send, recv_sem=recv,
+            device_id=target, device_id_type=pl.DeviceIdType.MESH,
+        )
+
+    def z_copy(array, turn):
+        return remote(
+            own_at(array, spot), full_at(array, member, spot),
+            z_send.at[array, turn - 1], z_recv.at[array, turn - 1], peer(turn),
+        )
+
+    def bias_copy(turn):
+        return remote(hold_bu, bu_f.at[member], b_send.at[turn - 1], b_recv.at[turn - 1], peer(turn))
+
+    def stamp_copy(n):
+        return remote(ts_ref, ts_f.at[spot], t_send.at[n], t_recv.at[n], others[n])
+
+    def push(array, turn, kind):
+        shard = lax.rem(member + 4 - turn, 4)
+        by_x = (array + turn) % 2 == 0
+        piece = (spot, spot, from_x if by_x else from_y, spot, from_x, from_y, from_d)[kind]
+        target = ("x", "y", "y" if by_x else "x", "core", "core", "core", "core")[kind]
+        return remote(
+            full_at(array, shard, piece), full_at(array, shard, piece),
+            n_send.at[array, turn - 1, kind], n_recv.at[array, turn - 1, kind], near[target],
+        )
+
+    order = (1, 3, 2)
+
+    def stage_z(array):
+        for turn in order:
+            z_copy(array, turn).wait_recv()
+            for kind in (0, 1, 3):
+                push(array, turn, kind).start()
+
+    def stage_near(array):
+        for turn in order:
+            push(array, turn, 0).wait_recv()
+            if (array + turn) % 2 == 0:
+                push(array, turn, 2).start()
+            push(array, turn, 4).start()
+            push(array, turn, 1).wait_recv()
+            if (array + turn) % 2 == 1:
+                push(array, turn, 2).start()
+            push(array, turn, 5).start()
+
+    def stage_far(array):
+        for turn in order:
+            push(array, turn, 2).wait_recv()
+            push(array, turn, 6).start()
+
+    def settle(array):
+        for turn in order:
+            for kind in range(3, 7):
+                push(array, turn, kind).wait_recv()
+
+    own_rows = pl.ds(pl.multiple_of(member * rows_a, 64), rows_a)
+    own_parts = (
+        (wqkv, wqkv_v.at[:, own_rows, :], wqkv_f.at[:, own_rows, :]),
+        (wo, wo_v.at[own_rows, :], wo_f.at[own_rows, :]),
+        (wu, hold_wu, wu_f.at[member]),
+        (wd, hold_wd, wd_f.at[member]),
+        (ts_ref, hold_ts, ts_f.at[spot]),
+    )
+
+    def into(n):
+        return pltpu.make_async_copy(own_parts[n][0], own_parts[n][1], loc_sem.at[n])
+
+    def outof(n):
+        return pltpu.make_async_copy(own_parts[n][1], own_parts[n][2], loc_sem.at[8 + n])
+
+    def bias_out():
+        return pltpu.make_async_copy(hold_bu, bu_f.at[member], loc_sem.at[15])
+
+    def load(array):
+        src, dst = ((wqkv_f, wqkv_v), (wo_f, wo_v))[array]
+        return pltpu.make_async_copy(src, dst, load_sem.at[array])
+
+    @pl.when(tile == 0)
+    def _():
+        hold_bu[...] = jnp.broadcast_to(bias_ref[...], hold_bu.shape)
+        greet([peer(1), peer(2), peer(3)] + others)
+        for array in range(4):
+            for turn in (2, 1, 3):
+                z_copy(array, turn).start()
+        for n in range(5):
+            into(n).start()
+        for n in range(GROUP - 1):
+            stamp_copy(n).start()
+        for n in range(5):
+            into(n).wait()
+            outof(n).start()
+
     stream = stream_tile(hidden_ref, emb_ref, tile)
     hat, _ = norm_stats(stream)
-    normed = (hat * gain_ref[...] + shift_ref[...]).astype(BF16)
+    norm_v[...] = (hat * gain_ref[...] + shift_ref[...]).astype(BF16)
     mid_ref[...] = stream + ob_ref[...]
+
+    @pl.when(tile == 0)
+    def _():
+        bias_out().start()
+        for turn in (1, 2, 3):
+            bias_copy(turn).start()
+        stage_z(0)
+        stage_z(1)
+        stage_near(0)
+        stage_far(0)
+        settle(0)
+        outof(0).wait()
+        load(0).start()
+        load(0).wait()
+
+    @pl.when(tile == 1)
+    def _():
+        stage_z(3)
+
     for part in range(3):
-        qkv_ref[part] = mm_nt(normed, wqkv_ref[part]).astype(BF16)
+        qkv_ref[part] = mm_nt(norm_v[...], wqkv_v[part]).astype(BF16)
+
+    @pl.when(tile == 0)
+    def _():
+        stage_near(1)
+        stage_z(2)
+        stage_far(1)
+        settle(1)
+        outof(1).wait()
+        load(1).start()
+
     lane = lax.broadcasted_iota(jnp.int32, (WIN, 2 * HD), 1)
     low = lane < HD
     row_i = lax.broadcasted_iota(jnp.int32, (WIN, WIN), 0)
@@ -76,8 +270,8 @@
     scale = HD ** (-0.5)
     pairs = qkv_ref.shape[2] // (2 * HD)
     for win in range(TILE // WIN):
-        spot = (half * (3 * TILE // WIN) + tile * (TILE // WIN) + win) % 4
-        same_ref[...] = jnp.where(same_half, 0.0, jnp.where(spot < 2, -1e9, 0.0))
+        at = ((half * steps + tile) * (TILE // WIN) + win) % 4
+        same_ref[...] = jnp.where(same_half, 0.0, jnp.where(at < 2, -1e9, 0.0))
         rows = slice(win * WIN, (win + 1) * WIN)
         for pair in range(pairs):
             cols = slice(pair * 2 * HD, (pair + 1) * 2 * HD)
@@ -95,33 +289,46 @@
                 probs_ref[2 * pair + j, win] = probs
                 outs.append(mm(probs, v2))
             ctx_acc[rows, cols] = jnp.where(low, outs[0], outs[1]).astype(BF16)
+        if win == 0:
+
+            @pl.when(tile == last)
+            def _():
+                stage_near(3)
+
+    @pl.when(tile == 0)
+    def _():
+        load(1).wait()
+
+    @pl.when(tile == 1)
+    def _():
+        stage_near(2)
+
+    @pl.when(tile == last)
+    def _():
+        stage_far(2)
+
     ctx_ref[...] = ctx_acc[...]
-    mid_ref[...] += mm(ctx_acc[...], wo_ref[...])
-
-
-def line_up(n):
-    place = lax.axis_index("dp")
-    spot = lax.rem(place, GROUP)
-    return place - spot, spot
-
-
-def ahead(ref, rows, dst, send, recv, target):
-    return pltpu.make_async_remote_copy(
-        src_ref=ref.at[rows] if rows is not None else ref,
-        dst_ref=dst.at[rows] if rows is not None else dst,
-        send_sem=send, recv_sem=recv, device_id=target, device_id_type=pl.DeviceIdType.MESH,
-    )
-
-
-def mate_of(member):
-    return {"dp": lax.axis_index("dp"), "mp": member + 1 - 2 * lax.rem(member, 2)}
-
-
-def greet(targets):
-    barrier = pltpu.get_barrier_semaphore()
-    for target in targets:
-        pl.semaphore_signal(barrier, inc=1, device_id=target, device_id_type=pl.DeviceIdType.MESH)
-    pl.semaphore_wait(barrier, len(targets))
+    mid_ref[...] += mm(ctx_acc[...], wo_v[...])
+
+    @pl.when(tile == last)
+    def _():
+        stage_far(3)
+        settle(2)
+        settle(3)
+        for n in range(GROUP - 1):
+            stamp_copy(n).wait_recv()
+            stamp_copy(n).wait_send()
+        for turn in (1, 2, 3):
+            bias_copy(turn).wait_recv()
+            bias_copy(turn).wait_send()
+        for array in range(4):
+            for turn in (1, 2, 3):
+                z_copy(array, turn).wait_send()
+                for kind in range(7):
+                    push(array, turn, kind).wait_send()
+        for n in range(2, 5):
+            outof(n).wait()
+        bias_out().wait()
 
 
 def mlp_kernel(
@@ -215,12 +422,12 @@
 
 def attn_bwd_kernel(
     hidden_ref, emb_ref, gain_ref, shift_ref, wqkv_ref, wo_ref,
-    qkv_ref, probs_ref, ctx_ref, gmid_ref, gwm_ref, vecm_ref, gbu_ref, out_in,
-    out_ref, gh_ref, gm_ref, ga_ref, vec_out, u_out,
+    qkv_ref, probs_ref, ctx_ref, gmid_ref, gwm_ref, vecm_ref, gbu_ref, ts_ref, out_in,
+    out_ref, gh_ref, gm_ref, ga_ref, vec_out, table_ref,
     acc, gp_ref, gc_ref, n1t_ref, gmt_ref, vec_ref, usum_ref, stage,
     m_own, m_core, m_sum, m_chip, m_give, m_got,
     a_src, a_core, a_sum, a_chip, a_give, a_got,
-    s_src, s_rcv, v_src, v_rcv, u_give, u_got,
+    s_src, s_rcv, v_src, v_rcv, u_give, u_got, u_mine,
     own_sem, out_send, out_recv, loc_sem, gh_send, gh_recv,
     core_send, core_recv, chip_send, chip_recv, give_send, give_recv,
     s_send, s_recv, v_send, v_recv, u_send, u_recv,
@@ -235,7 +442,7 @@
     piece = part_w // 2
     share = width // GROUP
     total = out_ref.shape[0] // (2 * TILE)
-    base, spot = line_up(0)
+    base, spot = line_up()
     core = lax.rem(spot, 2)
     chip = spot // 2
     bit_x = lax.rem(chip, 2)
@@ -443,7 +650,7 @@
             whole_u = s_rcv[n, 0:units, :]
             left, right = whole_u[:, :piece], whole_u[:, piece:]
             u_give[n] = jnp.where(half == 0, right, left)
-            u_out[0, n] = jnp.where(half == 0, left, right)
+            u_mine[n] = jnp.where(half == 0, left, right)
         for n in range(3):
             line_copy(n).start()
         u_copy().start()
@@ -460,7 +667,21 @@
             vec_out[0:6, cols] = every[at : at + 6]
             vec_out[6:7, cols] = jnp.where(half == 0, mine[at + 6 : at + 7], mine[at + 7 : at + 8])
         u_copy().wait_recv()
-        u_out[1] = u_got[...]
+        at = lax.broadcasted_iota(jnp.int32, (units, table_ref.shape[1]), 1)
+        picks, sums = [], []
+        for n in range(GROUP):
+            for side in range(2):
+                rows = slice(units * side, units * (side + 1))
+                picks.append((ts_ref[n, rows, 0:1] == at).astype(F32))
+                sums.append(jnp.where(half == side, u_mine[n], u_got[n]))
+        pick = jnp.concatenate(picks, axis=0).astype(BF16)
+        rest = jnp.concatenate(sums, axis=0)
+        table = jnp.zeros(table_ref.shape, F32)
+        for _ in range(3):
+            first = rest.astype(BF16)
+            table = table + mm_tn(first, pick)
+            rest = rest - first.astype(F32)
+        table_ref[...] = table
         for r in range(3):
             chip_copy(1, r).wait_recv()
         kept_a = a_sum[chip, half].astype(F32)
@@ -492,7 +713,7 @@
 
 
 def finish_kernel(
-    out_in, gh_in, gm_ref, ga_ref, vec_ref, u_ref, ts_ref,
+    out_in, gh_in, gm_ref, ga_ref, vec_ref, table_in,
     out_ref, gh_ref, table_ref, g1_ref, s1_ref, qkv_ref, wo_ref, ob_ref,
     g2_ref, s2_ref, up_ref, ub_ref, down_ref, db_ref,
 ):
@@ -503,88 +724,77 @@
     def _():
         ff = up_ref.shape[1]
         piece = qkv_ref.shape[2]
+        table_ref[...] = table_in[...]
         up_ref[...] = gm_ref[:, 0:ff]
-        down_ref[...] = gm_ref[:, ff : 2 * ff].T
+        down_ref[...] = gm_ref[:, ff : 2 * ff]
         for part in range(3):
             qkv_ref[part] = ga_ref[:, part * piece : (part + 1) * piece]
         wo_ref[...] = ga_ref[:, 3 * piece : 4 * piece].T
         for n, ref in enumerate((g1_ref, s1_ref, g2_ref, s2_ref, ob_ref, db_ref, ub_ref)):
             ref[...] = vec_ref[n]
-        member = lax.axis_index("mp")
-        half = lax.rem(member, 2)
-        steps = table_ref.shape[0]
-        at = lax.broadcasted_iota(jnp.int32, (16, steps), 1)
-        table = jnp.zeros(table_ref.shape, F32)
-        picks, parts = [], [[], [], []]
-        for n in range(GROUP):
-            for side in range(2):
-                picks.append((ts_ref[n, 16 * side : 16 * side + 16, 0:1] == at).astype(F32))
-                value = jnp.where(half == side, u_ref[0, n], u_ref[1, n])
-                parts[0].append(value)
-        pick = jnp.concatenate(picks, axis=0).astype(BF16)
-        rest = jnp.concatenate(parts[0], axis=0)
-        for _ in range(3):
-            low = rest.astype(BF16)
-            table = table + mm_tn(pick, low)
-            rest = rest - low.astype(F32)
-        table_ref[...] = table
-
-
-def whole(shape):
+
+
+LIMIT = 62 * 1024 * 1024
+
+
+def half_map(steps):
+    return lambda i: (lax.rem(lax.axis_index("mp"), 2) * steps + i, 0)
+
+
+def fixed(shape):
     zeros = (0,) * len(shape)
-    return pl.BlockSpec(shape, lambda i, meta: zeros, pipeline_mode=pl.Buffered(1))
-
-
-def held(shape):
-    zeros = (0,) * len(shape)
-    return pl.BlockSpec(shape, lambda i, meta: zeros)
-
-
-LIMIT = 62 * 1024 * 1024
-
-
-def attn_fwd(meta, hidden, emb, gain, shift, wqkv, wo, ob):
+    return pl.BlockSpec(shape, lambda i: zeros, pipeline_mode=pl.Buffered(1))
+
+
+def attn_fwd(hidden, emb, gain, shift, ob, bias, ts, wqkv, wo, wu, wd):
     count, width = hidden.shape[0] // 2, hidden.shape[1]
     steps = count // TILE
     heads = width // HD
-    tok = pl.BlockSpec((TILE, width), lambda i, meta: (i, 0))
+    rows = wo.shape[0]
+    ff = wu.shape[1]
+    tok = pl.BlockSpec((TILE, width), lambda i: (i, 0))
+    anywhere = pl.BlockSpec(memory_space=pl.ANY)
+    dma = pltpu.SemaphoreType.DMA
     return pl.pallas_call(
         attn_fwd_kernel,
         name="attn_fwd",
-        grid_spec=pltpu.PrefetchScalarGridSpec(
-            num_scalar_prefetch=1,
-            grid=(steps,),
-            in_specs=[
-                pl.BlockSpec((TILE, width), lambda i, meta: (meta[0] * steps + i, 0)),
-                whole(emb.shape), whole((1, width)), whole((1, width)),
-                whole(wqkv.shape), whole(wo.shape), whole((1, width)),
-            ],
-            out_specs=[
-                pl.BlockSpec((3, TILE, width), lambda i, meta: (0, i, 0)),
-                pl.BlockSpec((heads, TILE // WIN, WIN, WIN), lambda i, meta: (0, i, 0, 0)),
-                tok,
-                tok,
-            ],
-            scratch_shapes=[pltpu.VMEM((WIN, WIN), F32), pltpu.VMEM((TILE, width), BF16)],
-        ),
+        grid=(steps,),
+        in_specs=[
+            pl.BlockSpec((TILE, width), half_map(steps)),
+            fixed(emb.shape), fixed(gain.shape), fixed(shift.shape), fixed(ob.shape), fixed(bias.shape),
+        ] + [anywhere] * 5,
+        out_specs=[anywhere] * 6 + [
+            pl.BlockSpec((3, TILE, width), lambda i: (0, i, 0)),
+            pl.BlockSpec((heads, TILE // WIN, WIN, WIN), lambda i: (0, i, 0, 0)),
+            tok,
+            tok,
+        ],
         out_shape=[
+            jax.ShapeDtypeStruct((3, 4 * rows, width), BF16),
+            jax.ShapeDtypeStruct((4 * rows, width), BF16),
+            jax.ShapeDtypeStruct((4, width, ff), BF16),
+            jax.ShapeDtypeStruct((4, ff, width), BF16),
+            jax.ShapeDtypeStruct((4, 8, ff), F32),
+            jax.ShapeDtypeStruct((GROUP,) + ts.shape, jnp.int32),
             jax.ShapeDtypeStruct((3, count, width), BF16),
             jax.ShapeDtypeStruct((heads, count // WIN, WIN, WIN), BF16),
             jax.ShapeDtypeStruct((count, width), BF16),
             jax.ShapeDtypeStruct((count, width), F32),
         ],
-        compiler_params=pltpu.CompilerParams(vmem_limit_bytes=LIMIT),
+        scratch_shapes=[
+            pltpu.VMEM((WIN, WIN), F32), pltpu.VMEM((TILE, width), BF16),
+            pltpu.VMEM((3, 4 * rows, width), BF16), pltpu.VMEM((4 * rows, width), BF16),
+            pltpu.VMEM((TILE, width), BF16),
+            pltpu.VMEM(wu.shape, BF16), pltpu.VMEM(wd.shape, BF16),
+            pltpu.VMEM((8, ff), F32), pltpu.VMEM(ts.shape, jnp.int32),
+            dma((16,)), dma((2,)), dma((4, 3)), dma((4, 3)), dma((3,)), dma((3,)),
+            dma((4, 3, 7)), dma((4, 3, 7)), dma((GROUP - 1,)), dma((GROUP - 1,)),
+        ],
+        compiler_params=pltpu.CompilerParams(
+            collective_id=1, has_side_effects=True, vmem_limit_bytes=LIMIT
+        ),
         cost_estimate=pl.CostEstimate(flops=12_000_000_000, bytes_accessed=30_000_000, transcendentals=5_000_000),
-    )(meta, hidden, emb, gain, shift, wqkv, wo, ob)
-
-
-def half_map(steps):
-    return lambda i: (lax.rem(lax.axis_index("mp"), 2) * steps + i, 0)
-
-
-def fixed(shape):
-    zeros = (0,) * len(shape)
-    return pl.BlockSpec(shape, lambda i: zeros, pipeline_mode=pl.Buffered(1))
+    )(hidden, emb, gain, shift, ob, bias, ts, wqkv, wo, wu, wd)
 
 
 def mlp(mid, gy, wu, bu, wd, gain, shift, db):
@@ -601,7 +811,7 @@
             tok,
             pl.BlockSpec((TILE, width), half_map(steps)),
             fixed(wu.shape), fixed(bu.shape), fixed(wd.shape),
-            fixed((1, width)), fixed((1, width)), fixed((1, width)),
+            fixed(gain.shape), fixed(shift.shape), fixed(db.shape),
         ],
         out_specs=[
             pl.BlockSpec(memory_space=pl.ANY), tok, fixed((2, width, 2 * ff)),
@@ -628,7 +838,7 @@
     )(mid, gy, wu, bu, wd, gain, shift, db)
 
 
-def attn_bwd(hidden, emb, gain, shift, wqkv, wo, qkv, probs, ctx, gmid, gwm, vecm, gbu, out):
+def attn_bwd(hidden, emb, gain, shift, wqkv, wo, qkv, probs, ctx, gmid, gwm, vecm, gbu, ts, out, table_rows):
     count, width = gmid.shape
     steps = count // TILE
     heads = width // HD
@@ -645,15 +855,15 @@
         grid=(steps,),
         in_specs=[
             pl.BlockSpec((TILE, width), half_map(steps)),
-            fixed(emb.shape), fixed((1, width)), fixed((1, width)),
+            fixed(emb.shape), fixed(gain.shape), fixed(shift.shape),
             fixed(wqkv.shape), fixed(wo.shape),
             pl.BlockSpec((3, TILE, width), lambda i: (0, i, 0)),
             pl.BlockSpec((heads, TILE // WIN, WIN, WIN), lambda i: (0, i, 0, 0)),
-            tok, tok, anywhere, fixed(vecm.shape), fixed(gbu.shape), anywhere,
+            tok, tok, anywhere, fixed(vecm.shape), fixed(gbu.shape), fixed(ts.shape), anywhere,
         ],
         out_specs=[
             anywhere, anywhere, fixed((share, wide)), fixed((share, width)),
-            fixed((8, width)), fixed((2, GROUP, units, piece)),
+            fixed((8, width)), fixed((piece, table_rows)),
         ],
         scratch_shapes=[
             pltpu.VMEM((4, width, width // 2), F32),
@@ -670,6 +880,7 @@
             pltpu.VMEM((units + 16, width // 2), F32), pltpu.VMEM((GROUP, units + 16, width // 2), F32),
             pltpu.VMEM((16, width // 2), F32), pltpu.VMEM((4, 16, width // 2), F32),
             pltpu.VMEM((GROUP, units, piece), F32), pltpu.VMEM((GROUP, units, piece), F32),
+            pltpu.VMEM((GROUP, units, piece), F32),
             dma((4,)), dma(()), dma(()), dma((steps,)), dma((steps,)), dma((steps,)),
             dma((2, 4)), dma((2, 4)), dma((2, 3)), dma((2, 3)), dma((2,)), dma((2,)),
             dma((GROUP - 1,)), dma((GROUP - 1,)), dma((3,)), dma((3,)), dma(()), dma(()),
@@ -680,17 +891,17 @@
             jax.ShapeDtypeStruct((share, wide), F32),
             jax.ShapeDtypeStruct((share, width), F32),
             jax.ShapeDtypeStruct((8, width), F32),
-            jax.ShapeDtypeStruct((2, GROUP, units, piece), F32),
-        ],
-        input_output_aliases={13: 0},
+            jax.ShapeDtypeStruct((piece, table_rows), F32),
+        ],
+        input_output_aliases={14: 0},
         compiler_params=pltpu.CompilerParams(
             collective_id=3, has_side_effects=True, vmem_limit_bytes=LIMIT
         ),
         cost_estimate=pl.CostEstimate(flops=20_000_000_000, bytes_accessed=40_000_000, transcendentals=0),
-    )(hidden, emb, gain, shift, wqkv, wo, qkv, probs, ctx, gmid, gwm, vecm, gbu, out)
-
-
-def finish(out, gh, gm, ga, vec, u, ts, steps):
+    )(hidden, emb, gain, shift, wqkv, wo, qkv, probs, ctx, gmid, gwm, vecm, gbu, ts, out)
+
+
+def finish(out, gh, gm, ga, vec, table):
     count, width = out.shape
     share = gm.shape[0]
     ff = gm.shape[1] // 2
@@ -698,233 +909,29 @@
     tok = pl.BlockSpec((2 * TILE, width), lambda i: (i, 0))
     line = jax.ShapeDtypeStruct((width,), F32)
     shapes = [
-        jax.ShapeDtypeStruct((steps, piece), F32), line, line,
+        jax.ShapeDtypeStruct(table.shape, F32), line, line,
         jax.ShapeDtypeStruct((3, share, piece), F32), jax.ShapeDtypeStruct((piece, share), F32),
         line, line, line,
-        jax.ShapeDtypeStruct((share, ff), F32), line, jax.ShapeDtypeStruct((ff, share), F32), line,
+        jax.ShapeDtypeStruct((share, ff), F32), line, jax.ShapeDtypeStruct((share, ff), F32), line,
     ]
     return pl.pallas_call(
         finish_kernel,
         name="finish",
         grid=(count // (2 * TILE),),
-        in_specs=[tok, tok] + [fixed(x.shape) for x in (gm, ga, vec, u, ts)],
+        in_specs=[tok, tok] + [fixed(x.shape) for x in (gm, ga, vec, table)],
         out_specs=[tok, tok] + [fixed(x.shape) for x in shapes],
         out_shape=[jax.ShapeDtypeStruct(out.shape, BF16), jax.ShapeDtypeStruct(gh.shape, BF16)] + shapes,
         compiler_params=pltpu.CompilerParams(vmem_limit_bytes=LIMIT),
         cost_estimate=pl.CostEstimate(flops=1_000_000, bytes_accessed=20_000_000, transcendentals=0),
-    )(out, gh, gm, ga, vec, u, ts)
-
-
-ARRAYS = 4
-
-
-def gather_kernel(
-    wqkv, wo, wu, wd, bu, ts, wqkv_f, wo_f, wu_f, wd_f, bu_f, ts_f,
-    hold_qkv, hold_wo, hold_wu, hold_wd, hold_bu, hold_ts,
-    loc_sem, z_send, z_recv, b_send, b_recv, n_send, n_recv, t_send, t_recv,
-):
-    place = lax.axis_index("dp")
-    member = lax.axis_index("mp")
-    base = place - lax.rem(place, 8)
-    spot = place - base
-    bit0 = lax.rem(spot, 2)
-    bit1 = lax.rem(spot // 2, 2)
-    bit2 = spot // 4
-
-    def flip(where, bit, size):
-        return where + size - 2 * size * bit
-
-    near = {
-        "core": {"dp": flip(place, bit0, 1), "mp": member},
-        "x": {"dp": flip(place, bit1, 2), "mp": member},
-        "y": {"dp": flip(place, bit2, 4), "mp": member},
-    }
-    mine = spot
-    from_x = flip(spot, bit1, 2)
-    from_y = flip(spot, bit2, 4)
-    from_d = flip(from_x, bit2, 4)
-
-    def peer(turn):
-        return {"dp": place, "mp": lax.rem(member + turn, 4)}
-
-    others = [{"dp": base + lax.rem(spot + turn, 8), "mp": member} for turn in range(1, 8)]
-    greet([peer(1), peer(2), peer(3)] + others)
-
-    rows_a = wo.shape[0]
-    step_a = rows_a // 8
-    step_m = wu.shape[1 - 1] // 8
-
-    def full_at(array, shard, piece):
-        if array == 0:
-            return wqkv_f.at[:, pl.ds(shard * rows_a + piece * step_a, step_a), :]
-        if array == 1:
-            return wo_f.at[pl.ds(shard * rows_a + piece * step_a, step_a), :]
-        full = wu_f if array == 2 else wd_f
-        return full.at[shard, pl.ds(piece * step_m, step_m), :]
-
-    def own_at(array, piece):
-        if array == 0:
-            return wqkv.at[:, pl.ds(piece * step_a, step_a), :]
-        if array == 1:
-            return wo.at[pl.ds(piece * step_a, step_a), :]
-        return (wu if array == 2 else wd).at[pl.ds(piece * step_m, step_m), :]
-
-    sends = []
-    z_recvs, n_recvs = {}, {}
-    for array in range(ARRAYS):
-        for turn in (2, 1, 3):
-            copy = pltpu.make_async_remote_copy(
-                src_ref=own_at(array, spot),
-                dst_ref=full_at(array, member, spot),
-                send_sem=z_send.at[array, turn - 1],
-                recv_sem=z_recv.at[array, turn - 1],
-                device_id=peer(turn),
-                device_id_type=pl.DeviceIdType.MESH,
-            )
-            copy.start()
-            sends.append(copy)
-            z_recvs[array, turn] = copy
-        if array == 0:
-            for turn in (1, 2, 3):
-                copy = pltpu.make_async_remote_copy(
-                    src_ref=bu, dst_ref=bu_f.at[member],
-                    send_sem=b_send.at[turn - 1], recv_sem=b_recv.at[turn - 1],
-                    device_id=peer(turn), device_id_type=pl.DeviceIdType.MESH,
-                )
-                copy.start()
-                sends.append(copy)
-                n_recvs["bias", turn] = copy
-            for n in range(7):
-                copy = pltpu.make_async_remote_copy(
-                    src_ref=ts, dst_ref=ts_f.at[spot],
-                    send_sem=t_send.at[n], recv_sem=t_recv.at[n],
-                    device_id=others[n], device_id_type=pl.DeviceIdType.MESH,
-                )
-                copy.start()
-                sends.append(copy)
-                n_recvs["step", n] = copy
-
-    own_full = (
-        (wqkv, hold_qkv, wqkv_f.at[:, pl.ds(member * rows_a, rows_a), :]),
-        (wo, hold_wo, wo_f.at[pl.ds(member * rows_a, rows_a), :]),
-        (wu, hold_wu, wu_f.at[member]),
-        (wd, hold_wd, wd_f.at[member]),
-        (bu, hold_bu, bu_f.at[member]),
-        (ts, hold_ts, ts_f.at[spot]),
-    )
-    into = [pltpu.make_async_copy(src, hold, loc_sem.at[n]) for n, (src, hold, _) in enumerate(own_full)]
-    for copy in into:
-        copy.start()
-    outof = []
-    for n, (_, hold, dst) in enumerate(own_full):
-        into[n].wait()
-        copy = pltpu.make_async_copy(hold, dst, loc_sem.at[6 + n])
-        copy.start()
-        outof.append(copy)
-
-    def push(array, turn, kind, piece, target):
-        shard = lax.rem(member + 4 - turn, 4)
-        copy = pltpu.make_async_remote_copy(
-            src_ref=full_at(array, shard, piece),
-            dst_ref=full_at(array, shard, piece),
-            send_sem=n_send.at[array, turn - 1, kind],
-            recv_sem=n_recv.at[array, turn - 1, kind],
-            device_id=near[target],
-            device_id_type=pl.DeviceIdType.MESH,
-        )
-        copy.start()
-        sends.append(copy)
-        n_recvs[array, turn, kind] = copy
-
-    order = (1, 3, 2)
-
-    def stage_z(array):
-        for turn in order:
-            z_recvs[array, turn].wait_recv()
-            push(array, turn, 0, mine, "x")
-            push(array, turn, 1, mine, "y")
-            push(array, turn, 3, mine, "core")
-
-    def stage_near(array):
-        for turn in order:
-            n_recvs[array, turn, 0].wait_recv()
-            if (array + turn) % 2 == 0:
-                push(array, turn, 2, from_x, "y")
-            push(array, turn, 4, from_x, "core")
-            n_recvs[array, turn, 1].wait_recv()
-            if (array + turn) % 2 == 1:
-                push(array, turn, 2, from_y, "x")
-            push(array, turn, 5, from_y, "core")
-
-    def stage_far(array):
-        for turn in order:
-            n_recvs[array, turn, 2].wait_recv()
-            push(array, turn, 6, from_d, "core")
-
-    for step in range(ARRAYS + 2):
-        if step < ARRAYS:
-            stage_z(step)
-        if 0 <= step - 1 < ARRAYS:
-            stage_near(step - 1)
-        if 0 <= step - 2 < ARRAYS:
-            stage_far(step - 2)
-    for array in range(ARRAYS):
-        for turn in order:
-            for kind in range(3, 7):
-                n_recvs[array, turn, kind].wait_recv()
-    for turn in (1, 2, 3):
-        n_recvs["bias", turn].wait_recv()
-    for n in range(7):
-        n_recvs["step", n].wait_recv()
-    for copy in sends:
-        copy.wait_send()
-    for copy in outof:
-        copy.wait()
-
-
-def gather_weights(wqkv, wo, wu, wd, bu, ts):
-    anywhere = pl.BlockSpec(memory_space=pl.ANY)
-    rows, width = wo.shape
-    ff = wu.shape[1]
-    return pl.pallas_call(
-        gather_kernel,
-        name="gather_weights",
-        in_specs=[anywhere] * 6,
-        out_specs=[anywhere] * 6,
-        out_shape=[
-            jax.ShapeDtypeStruct((3, 4 * rows, width), BF16),
-            jax.ShapeDtypeStruct((4 * rows, width), BF16),
-            jax.ShapeDtypeStruct((4, width, ff), BF16),
-            jax.ShapeDtypeStruct((4, ff, width), BF16),
-            jax.ShapeDtypeStruct((4,) + bu.shape, F32),
-            jax.ShapeDtypeStruct((GROUP,) + ts.shape, jnp.int32),
-        ],
-        scratch_shapes=[
-            pltpu.VMEM(wqkv.shape, BF16), pltpu.VMEM(wo.shape, BF16),
-            pltpu.VMEM(wu.shape, BF16), pltpu.VMEM(wd.shape, BF16), pltpu.VMEM(bu.shape, F32),
-            pltpu.VMEM(ts.shape, jnp.int32),
-            pltpu.SemaphoreType.DMA((12,)),
-            pltpu.SemaphoreType.DMA((ARRAYS, 3)), pltpu.SemaphoreType.DMA((ARRAYS, 3)),
-            pltpu.SemaphoreType.DMA((3,)), pltpu.SemaphoreType.DMA((3,)),
-            pltpu.SemaphoreType.DMA((ARRAYS, 3, 7)), pltpu.SemaphoreType.DMA((ARRAYS, 3, 7)),
-            pltpu.SemaphoreType.DMA((7,)), pltpu.SemaphoreType.DMA((7,)),
-        ],
-        compiler_params=pltpu.CompilerParams(
-            collective_id=1, has_side_effects=True, vmem_limit_bytes=LIMIT
-        ),
-    )(wqkv, wo, wu, wd, bu, ts)
+    )(out, gh, gm, ga, vec, table)
 
 
 def local(
     hidden, timesteps, cotangent, time_table, first_gain, first_shift, qkv_weight, out_weight,
     out_bias, second_gain, second_shift, up_weight, up_bias, down_weight, down_bias,
 ):
-    count, width = hidden.shape
-    steps = time_table.shape[0]
-    local_ff = up_weight.shape[1]
-    member = lax.axis_index("mp")
-    half = lax.rem(member, 2)
-    meta = jnp.stack([half, member // 2]).astype(jnp.int32)
+    count = hidden.shape[0]
+    half = lax.rem(lax.axis_index("mp"), 2)
     units = count // LEN_A
     unit = jnp.arange(units, dtype=jnp.int32)
     within = unit % 8
@@ -935,28 +942,19 @@
     emb = jnp.take(time_table, jnp.maximum(unit_step[half], 0), axis=0).astype(F32)
     stamps = jnp.broadcast_to(unit_step.reshape(32, 1), (32, 128))
 
-    def row(v):
-        return v.reshape(1, -1)
-
-    wqkv_f, wo_f, wu_f, wd_f, bu_f, ts_f = gather_weights(
-        jnp.swapaxes(qkv_weight, 1, 2),
-        out_weight,
-        up_weight,
-        down_weight,
-        jnp.broadcast_to(row(up_bias), (8, local_ff)),
-        stamps,
-    )
-    qkv, probs, ctx, mid = attn_fwd(
-        meta, hidden, emb, row(first_gain), row(first_shift), wqkv_f, wo_f, row(out_bias)
+    wqkv_f, wo_f, wu_f, wd_f, bu_f, ts_f, qkv, probs, ctx, mid = attn_fwd(
+        hidden, emb, first_gain, first_shift, out_bias, up_bias, stamps,
+        jnp.swapaxes(qkv_weight, 1, 2), out_weight, up_weight, down_weight,
     )
     output, gmid, gw_mlp, vec_mlp, gbu = mlp(
-        mid, cotangent, wu_f, bu_f, wd_f, row(second_gain), row(second_shift), row(down_bias)
+        mid, cotangent, wu_f, bu_f, wd_f, second_gain, second_shift, down_bias
     )
-    output, grad_hidden, g_mlp, g_attn, vecs, sums = attn_bwd(
-        hidden, emb, row(first_gain), row(first_shift), wqkv_f, wo_f, qkv, probs, ctx, gmid,
-        gw_mlp, vec_mlp, gbu, output,
+    output, grad_hidden, g_mlp, g_attn, vecs, table = attn_bwd(
+        hidden, emb, first_gain, first_shift, wqkv_f, wo_f, qkv, probs, ctx, gmid,
+        gw_mlp, vec_mlp, gbu, ts_f, output, time_table.shape[0],
     )
-    outs = list(finish(output, grad_hidden, g_mlp, g_attn, vecs, sums, ts_f, steps))
+    outs = list(finish(output, grad_hidden, g_mlp, g_attn, vecs, table))
+    outs[2], outs[12] = outs[2].T, outs[12].T
     groups = lax.axis_size("dp") // GROUP
     if groups > 1:
         spots = [[g * GROUP + n for n in range(GROUP)] for g in range(groups)]

time: 287 us -> 253 us (0.88)
  Pallas kernels: 268 us -> 249 us
  local copies, waits for them, and re-layouts: 16 us -> 2.92 us
    pallas_call x2 -> x1, Pallas kernels: 94.5 us -> 78.4 us  [attn_fwd(): pl.pallas_call(attn_fwd_kernel, name='attn_fwd', grid=(steps,), in_specs=...]
    reshape x6 -> x0, local copies, waits for them, and re-layouts: 7.6 us -> none  [row(): return v.reshape(1, -1)]
    pallas_call x2 -> x0, local copies, waits for them, and re-layouts: 4.28 us -> none  [finish(): pl.pallas_call(finish_kernel, name='finish', grid=(count // (2 * TILE),),...]
where the time goes in v3:
time: 253 us
  Pallas kernels  249 us (98%)
  local copies, waits for them, and re-layouts  2.92 us (1%)
    pallas_call x1, Pallas kernels, attn_bwd(): pl.pallas_call(attn_bwd_kernel, name='attn_bwd', grid=(steps,), in_specs=...  95.2 us
    pallas_call x1, Pallas kernels, attn_fwd(): pl.pallas_call(attn_fwd_kernel, name='attn_fwd', grid=(steps,), in_specs=...  78.4 us
    pallas_call x1, Pallas kernels, mlp(): pl.pallas_call(mlp_kernel, name='mlp_both', grid=(steps,), in_specs=[tok,...  65.4 us
    pallas_call x1, Pallas kernels, finish(): pl.pallas_call(finish_kernel, name='finish', grid=(count // (2 * TILE),),...  9.61 us

profile of v3, /device:TPU:0, one launch (start us, length us, event | category | flops | bytes accessed | tf_op | source)
XLA Modules:
  0.0 253.3 jit_solution(13260513134702418347)
XLA Ops:
  0.6 0.0 copy-start
  0.7 1.5 gather_fusion
  2.2 0.1 gather.11
  2.3 0.1 broadcast_in_dim.21
  2.4 0.7 broadcast_in_dim.22.ts_ref
  3.1 0.0 copy-done
  3.1 0.6 gather_fusion.1
  3.7 0.7 select_convert_fusion.emb_ref
  4.4 78.4 %attn_fwd.1 = (bf16[3,768,768]{2,1,0:T(8,128)(2,1)}, bf16[768,768]{1,0:T(8,128)(2,1)}, bf16[4,768,768]{2,1,0:T(8,128)(2,1)}, bf16[4,768,768]{2,1,0:T(8,128)(2,1)...) custom-call(bf16[3072,768]{1,0:T(8,128)(2,1)} %hidden_ref.3, ...), custom_call_target="tpu_custom_call" | custom-call | flops 12000000000 | bytes 30000000 | tf_op jit(solution)/shard_map/attn_fwd/pallas_call | solution.py:758
  82.8 65.4 %mlp_both.1 = (bf16[3072,768]{1,0:T(8,128)(2,1)}, f32[1536,768]{1,0:T(8,128)}, bf16[2,768,1536]{2,1,0:T(8,128)(2,1)}, f32[8,768]{1,0:T(8,128)}, f32[2,8,768]{2,1,0:T(8,128)}) custom-call(f32[1536,768]{1,0:T(8,128)} %get-tuple-element.54.mid_ref, bf16[3072,768]{1,0:T(8,128)(2,1)} %gy_ref.1, bf16[4,768,768]{2,1,0:T(8,128)(2,1)} %get-tuple-element.55.wu_ref, ...), custom_call_target="tpu_custom_call" | custom-call | flops 35999997952 | bytes 30000000 | tf_op jit(solution)/shard_map/mlp_both/pallas_call | solution.py:806
  148.2 95.2 %attn_bwd.1 = (bf16[3072,768]{1,0:T(8,128)(2,1)}, bf16[3072,768]{1,0:T(8,128)(2,1)}, f32[96,1536]{1,0:T(8,128)}, f32[96,768]{1,0:T(8,128)}, f32[8,768]{1,0:T(8,128)}, /*index=5*/f32[192,1000]{1,0:T(8,128)}) custom-call(bf16[3072,768]{1,0:T(8,128)(2,1)} %hidden_ref.3, f32[16,768]{1,0:T(8,128)} %select_convert_fusion.emb_ref, ...), custom_call_target="tpu_custom_call", output_to_operand_aliasing={{0}: (14, {})} | custom-call | flops 20000000000 | bytes 40000000 | tf_op jit(solution)/shard_map/attn_bwd/pallas_call | solution.py:852
  243.5 0.0 copy-start.1
  243.5 9.6 %finish.1 = (bf16[3072,768]{1,0:T(8,128)(2,1)}, bf16[3072,768]{1,0:T(8,128)(2,1)}, f32[192,1000]{1,0:T(8,128)}, f32[768]{0:T(1024)}, f32[768]{0:T(1024)}, /*inde...) custom-call(bf16[3072,768]{1,0:T(8,128)(2,1)} %get-tuple-element.64., ...), custom_call_target="tpu_custom_call" | custom-call | flops 1000000 | bytes 20000000 | tf_op jit(solution)/shard_map/finish/pallas_call | solution.py:917
  253.1 0.0 copy-done.1
  (7 shorter events, 0.1 us)
Async XLA Ops:
  0.6 2.5 copy-start
  243.5 9.6 %copy-start.1 = (bf16[1000,768]{1,0:T(8,128)(2,1)S(1)}, bf16[1000,768]{1,0:T(8,128)(2,1)}, u32[]{:S(2)}) copy-start(bf16[1000,768]{1,0:T(8,128)(2,1)} %param.18) | copy-start | bytes 4608004

commit v4 on v3

--- a/solution.py
+++ b/solution.py
@@ -16,6 +16,7 @@
 WIN = 256
 TILE = 512
 GROUP = 8
+HALF = TILE // 2
 EPS = 1e-05
 GELU_C = 0.7978845608028654
 GELU_A = 0.044715
@@ -139,11 +140,34 @@
             device_id=target, device_id_type=pl.DeviceIdType.MESH,
         )
 
-    def z_copy(array, turn):
+    pair = member // 2
+    mate = member + 1 - 2 * half
+    beyond = 2 * member - mate
+    middle = (member == 1) | (member == 2)
+    shards = (mate, 2 - pair, 3 - 3 * pair)
+
+    def z_own(array, side):
         return remote(
             own_at(array, spot), full_at(array, member, spot),
-            z_send.at[array, turn - 1], z_recv.at[array, turn - 1], peer(turn),
+            z_send.at[array, side], z_recv.at[array, member],
+            {"dp": place, "mp": (mate, beyond)[side]},
         )
+
+    def z_on(array, turn):
+        shard = shards[turn]
+        onward = jnp.where(shard < member, member + 1, member - 1)
+        return remote(
+            full_at(array, shard, spot), full_at(array, shard, spot),
+            z_send.at[array, 2 + turn], z_recv.at[array, shard],
+            {"dp": place, "mp": onward},
+        )
+
+    def z_start(array):
+        z_own(array, 0).start()
+
+        @pl.when(middle)
+        def _():
+            z_own(array, 1).start()
 
     def bias_copy(turn):
         return remote(hold_bu, bu_f.at[member], b_send.at[turn - 1], b_recv.at[turn - 1], peer(turn))
@@ -152,20 +176,25 @@
         return remote(ts_ref, ts_f.at[spot], t_send.at[n], t_recv.at[n], others[n])
 
     def push(array, turn, kind):
-        shard = lax.rem(member + 4 - turn, 4)
+        shard = shards[turn]
         by_x = (array + turn) % 2 == 0
         piece = (spot, spot, from_x if by_x else from_y, spot, from_x, from_y, from_d)[kind]
         target = ("x", "y", "y" if by_x else "x", "core", "core", "core", "core")[kind]
         return remote(
             full_at(array, shard, piece), full_at(array, shard, piece),
-            n_send.at[array, turn - 1, kind], n_recv.at[array, turn - 1, kind], near[target],
+            n_send.at[array, turn, kind], n_recv.at[array, turn, kind], near[target],
         )
 
-    order = (1, 3, 2)
+    order = (0, 1, 2)
 
     def stage_z(array):
         for turn in order:
-            z_copy(array, turn).wait_recv()
+            z_on(array, turn).wait_recv()
+
+            @pl.when(middle)
+            def _():
+                z_on(array, turn).start()
+
             for kind in (0, 1, 3):
                 push(array, turn, kind).start()
 
@@ -215,17 +244,11 @@
     @pl.when(tile == 0)
     def _():
         hold_bu[...] = jnp.broadcast_to(bias_ref[...], hold_bu.shape)
-        greet([peer(1), peer(2), peer(3)] + others)
-        for array in range(4):
-            for turn in (2, 1, 3):
-                z_copy(array, turn).start()
         for n in range(5):
             into(n).start()
-        for n in range(GROUP - 1):
-            stamp_copy(n).start()
-        for n in range(5):
-            into(n).wait()
-            outof(n).start()
+        greet([peer(1), peer(2), peer(3)] + others)
+        for array in range(3):
+            z_start(array)
 
     stream = stream_tile(hidden_ref, emb_ref, tile)
     hat, _ = norm_stats(stream)
@@ -234,30 +257,32 @@
 
     @pl.when(tile == 0)
     def _():
+        for n in range(5):
+            into(n).wait()
+            outof(n).start()
+        stage_z(0)
+        stage_z(1)
+        z_start(3)
+        for n in range(GROUP - 1):
+            stamp_copy(n).start()
         bias_out().start()
         for turn in (1, 2, 3):
             bias_copy(turn).start()
-        stage_z(0)
-        stage_z(1)
         stage_near(0)
+        stage_near(1)
         stage_far(0)
+        stage_far(1)
+        stage_z(2)
         settle(0)
         outof(0).wait()
         load(0).start()
         load(0).wait()
 
-    @pl.when(tile == 1)
-    def _():
-        stage_z(3)
-
     for part in range(3):
         qkv_ref[part] = mm_nt(norm_v[...], wqkv_v[part]).astype(BF16)
 
     @pl.when(tile == 0)
     def _():
-        stage_near(1)
-        stage_z(2)
-        stage_far(1)
         settle(1)
         outof(1).wait()
         load(1).start()
@@ -281,38 +306,45 @@
             outs = []
             for j in range(2):
                 q1 = jnp.where(low == (j == 0), q2, jnp.zeros_like(q2))
-                scores = mm_nt(q1, k2) + same_ref[...]
-                top = jnp.max(scores, axis=-1, keepdims=True)
+                scores = mm_nt(k2, q1) + same_ref[...]
+                top = jnp.max(scores, axis=0, keepdims=True)
                 expo = jnp.exp(scores - top)
-                total = jnp.sum(expo, axis=-1, keepdims=True)
+                total = jnp.sum(expo, axis=0, keepdims=True)
                 probs = (expo * (1.0 / total)).astype(BF16)
                 probs_ref[2 * pair + j, win] = probs
-                outs.append(mm(probs, v2))
+                outs.append(mm_tn(probs, v2))
             ctx_acc[rows, cols] = jnp.where(low, outs[0], outs[1]).astype(BF16)
         if win == 0:
 
+            @pl.when(tile == 0)
+            def _():
+                stage_near(2)
+
+            @pl.when(tile == 1)
+            def _():
+                stage_far(2)
+
             @pl.when(tile == last)
             def _():
-                stage_near(3)
+                stage_far(3)
 
     @pl.when(tile == 0)
     def _():
         load(1).wait()
-
-    @pl.when(tile == 1)
-    def _():
-        stage_near(2)
-
-    @pl.when(tile == last)
-    def _():
-        stage_far(2)
 
     ctx_ref[...] = ctx_acc[...]
     mid_ref[...] += mm(ctx_acc[...], wo_v[...])
 
+    @pl.when(tile == 0)
+    def _():
+        stage_z(3)
+
+    @pl.when(tile == 1)
+    def _():
+        stage_near(3)
+
     @pl.when(tile == last)
     def _():
-        stage_far(3)
         settle(2)
         settle(3)
         for n in range(GROUP - 1):
@@ -322,8 +354,15 @@
             bias_copy(turn).wait_recv()
             bias_copy(turn).wait_send()
         for array in range(4):
-            for turn in (1, 2, 3):
-                z_copy(array, turn).wait_send()
+            z_own(array, 0).wait_send()
+
+            @pl.when(middle)
+            def _():
+                z_own(array, 1).wait_send()
+                for turn in order:
+                    z_on(array, turn).wait_send()
+
+            for turn in order:
                 for kind in range(7):
                     push(array, turn, kind).wait_send()
         for n in range(2, 5):
@@ -344,10 +383,10 @@
     pair = member // 2
     mate = mate_of(member)
     ff = wu_ref.shape[2]
-    total = out_ref.shape[0] // (2 * TILE)
+    total = out_ref.shape[0] // (2 * HALF)
 
     def rows_of(t):
-        return pl.ds(pl.multiple_of((half * total + t) * TILE, TILE), TILE)
+        return pl.ds(pl.multiple_of((half * total + t) * HALF, HALF), HALF)
 
     def local_copy(t):
         return pltpu.make_async_copy(stage.at[lax.rem(t, 2)], out_ref.at[rows_of(t)], loc_sem.at[t])
@@ -461,20 +500,27 @@
     others = [device(lax.rem(spot + turn, GROUP)) for turn in range(1, GROUP)]
     line = [{"dp": base + spot, "mp": lax.rem(member + turn, 4)} for turn in range(1, 4)]
 
-    def rows_of(t):
-        return pl.ds(pl.multiple_of((half * total + t) * TILE, TILE), TILE)
-
     def share_of(where):
         return pl.ds(pl.multiple_of(where * share, 32), share)
 
-    def out_copy(t):
-        return ahead(out_ref, rows_of(t), out_ref, out_send, out_recv, mate)
-
-    def gh_local(t):
-        return pltpu.make_async_copy(stage.at[lax.rem(t, 2)], gh_ref.at[rows_of(t)], loc_sem.at[t])
-
-    def gh_copy(t):
-        return ahead(gh_ref, rows_of(t), gh_ref, gh_send.at[t], gh_recv.at[t], mate)
+    def out_copy():
+        rows = pl.ds(pl.multiple_of((half * 2 * total + 2 * total - 1) * HALF, HALF), HALF)
+        return ahead(out_ref, rows, out_ref, out_send, out_recv, mate)
+
+    chunks = 2 * total
+
+    def gh_local(n):
+        rows = pl.ds(pl.multiple_of((half * chunks + n) * HALF, HALF), HALF)
+        return pltpu.make_async_copy(stage.at[lax.rem(n, 2)], gh_ref.at[rows], loc_sem.at[n])
+
+    def gh_copy(n):
+        rows = pl.ds(pl.multiple_of((half * chunks + n) * HALF, HALF), HALF)
+        return ahead(gh_ref, rows, gh_ref, gh_send.at[n], gh_recv.at[n], mate)
+
+    def gh_last(n):
+        quarter = HALF // 2
+        rows = pl.ds(pl.multiple_of((half * chunks + chunks - 1) * HALF + n * quarter, quarter), quarter)
+        return ahead(gh_ref, rows, gh_ref, gh_send.at[chunks - 1 + n], gh_recv.at[chunks - 1 + n], mate)
 
     def own_copy(k):
         return pltpu.make_async_copy(gwm_ref.at[:, share_of(2 * k + core), :], m_own.at[k], own_sem.at[k])
@@ -522,7 +568,7 @@
         vec_ref[...] = jnp.zeros_like(vec_ref)
         usum_ref[...] = jnp.zeros_like(usum_ref)
         greet(others + line)
-        out_copy(total - 1).start()
+        out_copy().start()
         for k in range(4):
             core_copy(0, k).start()
         for k in range(4):
@@ -530,8 +576,8 @@
 
     @pl.when(tile > 0)
     def _():
-        gh_local(tile - 1).wait()
-        gh_copy(tile - 1).start()
+        gh_local(2 * tile - 1).wait()
+        gh_copy(2 * tile - 1).start()
 
     own = pl.ds(pl.multiple_of(pair_id * part_w, 128), part_w)
     stream = stream_tile(hidden_ref, emb_ref, tile)
@@ -549,6 +595,9 @@
         rows = slice(win * WIN, (win + 1) * WIN)
         for pair in range(pairs):
             cols = slice(pair * 2 * HD, (pair + 1) * 2 * HD)
+            if win == 1 and pair == 1:
+                gh_local(2 * tile).wait()
+                gh_copy(2 * tile).start()
             q2 = qkv_ref[0, rows, cols]
             k2 = qkv_ref[1, rows, cols]
             v2 = qkv_ref[2, rows, cols]
@@ -558,55 +607,85 @@
                 gc1 = jnp.where(low == (j == 0), gc2, jnp.zeros_like(gc2))
                 probs_low = probs_ref[2 * pair + j, win]
                 probs = probs_low.astype(F32)
-                dprob = mm_nt(gc1, v2)
+                dprob = mm_nt(v2, gc1)
                 mix = probs * dprob
-                total_row = jnp.sum(mix, axis=-1, keepdims=True)
+                total_row = jnp.sum(mix, axis=0, keepdims=True)
                 grad_s = (mix - probs * total_row).astype(BF16)
-                dv.append(mm_tn(probs_low, gc2))
-                dk.append(mm_tn(grad_s, q2))
-                dq.append(mm(grad_s, k2))
+                dv.append(mm(probs_low, gc2))
+                dk.append(mm(grad_s, q2))
+                dq.append(mm_tn(grad_s, k2))
             gp_ref[0, rows, cols] = (jnp.where(low, dq[0], dq[1]) * scale).astype(BF16)
             gp_ref[1, rows, cols] = (jnp.where(low, dk[0], dk[1]) * scale).astype(BF16)
             gp_ref[2, rows, cols] = jnp.where(low, dv[0], dv[1]).astype(BF16)
 
-    @pl.when(tile == 0)
-    def _():
+        if win == 0:
+
+            @pl.when(tile == 0)
+            def _():
+                for k in range(4):
+                    own_copy(k).wait()
+                    core_copy(0, k).wait_recv()
+                    m_sum[k] = (m_own[k].astype(F32) + m_core[k].astype(F32)).astype(BF16)
+
+        else:
+            for part in range(3):
+                acc[part] += mm(n1t_ref[...], gp_ref[part, :, own])
+
+            @pl.when(tile == last)
+            def _():
+                a_src[...] = acc[...].astype(BF16)
+                for r in range(3):
+                    chip_copy(0, r).wait_recv()
+                kept_m = m_sum[chip, half].astype(F32)
+                give_m = m_sum[chip, 1 - half].astype(F32)
+                for r in range(3):
+                    kept_m = kept_m + m_chip[r, half].astype(F32)
+                    give_m = give_m + m_chip[r, 1 - half].astype(F32)
+                m_give[...] = give_m.astype(BF16)
+                gm_ref[...] = kept_m
+                for k in range(4):
+                    core_copy(1, k).start()
+
+        grad_n = mm(gp_ref[0, rows], wqkv_ref[0])
+        for part in range(1, 3):
+            grad_n = grad_n + mm(gp_ref[part, rows], wqkv_ref[part])
+        if win == 0:
+
+            @pl.when(tile == 0)
+            def _():
+                for r in range(3):
+                    chip_copy(0, r).start()
+
+        else:
+
+            @pl.when(tile == last)
+            def _():
+                give_copy(0).start()
+
+        unit_at = tile * (TILE // LEN_A) + win * (WIN // LEN_A)
+        parts = []
+        for unit in range(WIN // LEN_A):
+            at = win * WIN + unit * LEN_A
+            parts.append(hidden_ref[at : at + LEN_A, :].astype(F32) + emb_ref[pl.ds(unit_at + unit, 1), :])
+        hat, inv = norm_stats(jnp.concatenate(parts, axis=0))
+        vec_ref[0:1] += jnp.sum(grad_n * hat, axis=0, keepdims=True)
+        vec_ref[1:2] += jnp.sum(grad_n, axis=0, keepdims=True)
+        grad_in = gmid_ref[rows] + norm_back(grad_n, gain_ref[...], hat, inv)
+        stage[win] = grad_in.astype(BF16)
+        for unit in range(WIN // LEN_A):
+            usum_ref[pl.ds(unit_at + unit, 1), :] = jnp.sum(
+                grad_in[unit * LEN_A : (unit + 1) * LEN_A], axis=0, keepdims=True
+            )
+        gh_local(2 * tile + win).start()
+
+    @pl.when(tile == last)
+    def _():
+        units = usum_ref.shape[0]
         for k in range(4):
-            own_copy(k).wait()
-            core_copy(0, k).wait_recv()
-            m_sum[k] = (m_own[k].astype(F32) + m_core[k].astype(F32)).astype(BF16)
-
-    grad_n = mm(gp_ref[0], wqkv_ref[0])
-    for part in range(1, 3):
-        grad_n = grad_n + mm(gp_ref[part], wqkv_ref[part])
-    for part in range(3):
-        acc[part] += mm(n1t_ref[...], gp_ref[part, :, own])
-
-    @pl.when(tile == 0)
-    def _():
-        for r in range(3):
-            chip_copy(0, r).start()
-
-    stream = stream_tile(hidden_ref, emb_ref, tile)
-    hat, inv = norm_stats(stream)
-    vec_ref[0:1] += jnp.sum(grad_n * hat, axis=0, keepdims=True)
-    vec_ref[1:2] += jnp.sum(grad_n, axis=0, keepdims=True)
-    grad_in = gmid_ref[...] + norm_back(grad_n, gain_ref[...], hat, inv)
-    stage[lax.rem(tile, 2)] = grad_in.astype(BF16)
-    for unit in range(TILE // LEN_A):
-        usum_ref[pl.ds(tile * (TILE // LEN_A) + unit, 1), :] = jnp.sum(
-            grad_in[unit * LEN_A : (unit + 1) * LEN_A], axis=0, keepdims=True
-        )
-    gh_local(tile).start()
-
-    @pl.when(tile == last)
-    def _():
-        units = usum_ref.shape[0]
-        for group in range(2):
-            for part in range(4):
-                a_src[group, :, part * piece : (part + 1) * piece] = acc[
-                    part, :, group * piece : (group + 1) * piece
-                ].astype(BF16)
+            core_copy(1, k).wait_recv()
+            a_sum[k] = (
+                a_src[:, share_of(2 * k + core), :].astype(F32) + a_core[k].astype(F32)
+            ).astype(BF16)
         s_src[0:units, :] = usum_ref[:, own]
         for left in range(2):
             cols = slice(left * part_w, (left + 1) * part_w)
@@ -615,32 +694,14 @@
             s_src[at + 2 : at + 6, :] = vecm_ref[0:4, cols]
             s_src[at + 6 : at + 7, :] = gbu_ref[0, 0:1, cols]
             s_src[at + 7 : at + 8, :] = gbu_ref[1, 0:1, cols]
-        gh_local(tile).wait()
-        gh_copy(tile).start()
-        for k in range(4):
-            core_copy(1, k).start()
-        s_rcv[spot] = s_src[...]
+        gh_local(2 * tile + 1).wait()
         for n in range(GROUP - 1):
             small_copy(n).start()
         for r in range(3):
-            chip_copy(0, r).wait_recv()
-        kept_m = m_sum[chip, half].astype(F32)
-        give_m = m_sum[chip, 1 - half].astype(F32)
-        for r in range(3):
-            kept_m = kept_m + m_chip[r, half].astype(F32)
-            give_m = give_m + m_chip[r, 1 - half].astype(F32)
-        m_give[...] = give_m.astype(BF16)
-        gm_ref[...] = kept_m
-        for k in range(4):
-            core_copy(1, k).wait_recv()
-            a_sum[k] = (
-                a_src[:, share_of(2 * k + core), :].astype(F32) + a_core[k].astype(F32)
-            ).astype(BF16)
-        give_copy(0).start()
+            chip_copy(1, r).start()
+        s_rcv[spot] = s_src[...]
         for n in range(GROUP - 1):
             small_copy(n).wait_recv()
-        for r in range(3):
-            chip_copy(1, r).start()
         v_sum = s_rcv[0, units : units + 16, :]
         for n in range(1, GROUP):
             v_sum = v_sum + s_rcv[n, units : units + 16, :]
@@ -654,18 +715,29 @@
         for n in range(3):
             line_copy(n).start()
         u_copy().start()
+        gh_last(0).start()
         give_copy(0).wait_recv()
         gm_ref[...] += m_got[...].astype(F32)
         for n in range(3):
             line_copy(n).wait_recv()
         every = 0.5 * ((v_rcv[0] + v_rcv[1]) + (v_rcv[2] + v_rcv[3]))
         other = member + 1 - 2 * half
-        mine = v_rcv[member] + v_rcv[other]
+        both = v_rcv[member] + v_rcv[other]
         for left in range(2):
             cols = slice(left * part_w, (left + 1) * part_w)
             at = 8 * left
             vec_out[0:6, cols] = every[at : at + 6]
-            vec_out[6:7, cols] = jnp.where(half == 0, mine[at + 6 : at + 7], mine[at + 7 : at + 8])
+            vec_out[6:7, cols] = jnp.where(half == 0, both[at + 6 : at + 7], both[at + 7 : at + 8])
+        for r in range(3):
+            chip_copy(1, r).wait_recv()
+        both_a = a_sum[chip].astype(F32)
+        for r in range(3):
+            both_a = both_a + a_chip[r].astype(F32)
+        first_a, last_a = both_a[:, :, :piece], both_a[:, :, piece:]
+        a_give[...] = jnp.where(half == 0, last_a, first_a).astype(BF16)
+        ga_ref[...] = jnp.where(half == 0, first_a, last_a)
+        give_copy(1).start()
+        gh_last(1).start()
         u_copy().wait_recv()
         at = lax.broadcasted_iota(jnp.int32, (units, table_ref.shape[1]), 1)
         picks, sums = [], []
@@ -682,23 +754,16 @@
             table = table + mm_tn(first, pick)
             rest = rest - first.astype(F32)
         table_ref[...] = table
-        for r in range(3):
-            chip_copy(1, r).wait_recv()
-        kept_a = a_sum[chip, half].astype(F32)
-        give_a = a_sum[chip, 1 - half].astype(F32)
-        for r in range(3):
-            kept_a = kept_a + a_chip[r, half].astype(F32)
-            give_a = give_a + a_chip[r, 1 - half].astype(F32)
-        a_give[...] = give_a.astype(BF16)
-        ga_ref[...] = kept_a
-        give_copy(1).start()
         give_copy(1).wait_recv()
         ga_ref[...] += a_got[...].astype(F32)
-        out_copy(total - 1).wait_recv()
-        out_copy(total - 1).wait_send()
-        for t in range(total):
+        out_copy().wait_recv()
+        out_copy().wait_send()
+        for t in range(chunks - 1):
             gh_copy(t).wait_recv()
             gh_copy(t).wait_send()
+        for n in range(2):
+            gh_last(n).wait_recv()
+            gh_last(n).wait_send()
         for kind in range(2):
             for k in range(4):
                 core_copy(kind, k).wait_send()
@@ -723,13 +788,12 @@
     @pl.when(pl.program_id(0) == 0)
     def _():
         ff = up_ref.shape[1]
-        piece = qkv_ref.shape[2]
         table_ref[...] = table_in[...]
         up_ref[...] = gm_ref[:, 0:ff]
         down_ref[...] = gm_ref[:, ff : 2 * ff]
         for part in range(3):
-            qkv_ref[part] = ga_ref[:, part * piece : (part + 1) * piece]
-        wo_ref[...] = ga_ref[:, 3 * piece : 4 * piece].T
+            qkv_ref[part] = ga_ref[part]
+        wo_ref[...] = ga_ref[3].T
         for n, ref in enumerate((g1_ref, s1_ref, g2_ref, s2_ref, ob_ref, db_ref, ub_ref)):
             ref[...] = vec_ref[n]
 
@@ -787,7 +851,7 @@
             pltpu.VMEM((TILE, width), BF16),
             pltpu.VMEM(wu.shape, BF16), pltpu.VMEM(wd.shape, BF16),
             pltpu.VMEM((8, ff), F32), pltpu.VMEM(ts.shape, jnp.int32),
-            dma((16,)), dma((2,)), dma((4, 3)), dma((4, 3)), dma((3,)), dma((3,)),
+            dma((16,)), dma((2,)), dma((4, 5)), dma((4, 4)), dma((3,)), dma((3,)),
             dma((4, 3, 7)), dma((4, 3, 7)), dma((GROUP - 1,)), dma((GROUP - 1,)),
         ],
         compiler_params=pltpu.CompilerParams(
@@ -799,9 +863,9 @@
 
 def mlp(mid, gy, wu, bu, wd, gain, shift, db):
     count, width = mid.shape
-    steps = count // TILE
+    steps = count // HALF
     ff = wu.shape[2]
-    tok = pl.BlockSpec((TILE, width), lambda i: (i, 0))
+    tok = pl.BlockSpec((HALF, width), lambda i: (i, 0))
     dma = pltpu.SemaphoreType.DMA
     return pl.pallas_call(
         mlp_kernel,
@@ -809,7 +873,7 @@
         grid=(steps,),
         in_specs=[
             tok,
-            pl.BlockSpec((TILE, width), half_map(steps)),
+            pl.BlockSpec((HALF, width), half_map(steps)),
             fixed(wu.shape), fixed(bu.shape), fixed(wd.shape),
             fixed(gain.shape), fixed(shift.shape), fixed(db.shape),
         ],
@@ -819,10 +883,10 @@
         ],
         scratch_shapes=[
             pltpu.VMEM((2, width, ff), F32), pltpu.VMEM((2, width, ff), F32),
-            pltpu.VMEM((TILE, width), BF16), pltpu.VMEM((width, TILE), BF16),
-            pltpu.VMEM((width, TILE), BF16),
-            pltpu.VMEM((TILE, width), F32), pltpu.VMEM((TILE, width), F32),
-            pltpu.VMEM((2, TILE, width), BF16), dma((steps,)), dma((steps,)), dma((steps,)),
+            pltpu.VMEM((HALF, width), BF16), pltpu.VMEM((width, HALF), BF16),
+            pltpu.VMEM((width, HALF), BF16),
+            pltpu.VMEM((HALF, width), F32), pltpu.VMEM((HALF, width), F32),
+            pltpu.VMEM((2, HALF, width), BF16), dma((steps,)), dma((steps,)), dma((steps,)),
         ],
         out_shape=[
             jax.ShapeDtypeStruct((2 * count, width), BF16),
@@ -862,7 +926,7 @@
             tok, tok, anywhere, fixed(vecm.shape), fixed(gbu.shape), fixed(ts.shape), anywhere,
         ],
         out_specs=[
-            anywhere, anywhere, fixed((share, wide)), fixed((share, width)),
+            anywhere, anywhere, fixed((share, wide)), fixed((4, share, piece)),
             fixed((8, width)), fixed((piece, table_rows)),
         ],
         scratch_shapes=[
@@ -870,18 +934,18 @@
             pltpu.VMEM((3, TILE, width), BF16), pltpu.VMEM((TILE, width), BF16),
             pltpu.VMEM((width, TILE), BF16), pltpu.VMEM((width, TILE), BF16),
             pltpu.VMEM((8, width), F32), pltpu.VMEM((units, width), F32),
-            pltpu.VMEM((2, TILE, width), BF16),
+            pltpu.VMEM((2, HALF, width), BF16),
             pltpu.VMEM((4, 2, share, wide), BF16), pltpu.VMEM((4, 2, share, wide), BF16),
             pltpu.VMEM((4, 2, share, wide), BF16), pltpu.VMEM((3, 2, share, wide), BF16),
             pltpu.VMEM((share, wide), BF16), pltpu.VMEM((share, wide), BF16),
-            pltpu.VMEM((2, width, width), BF16), pltpu.VMEM((4, 2, share, width), BF16),
-            pltpu.VMEM((4, 2, share, width), BF16), pltpu.VMEM((3, 2, share, width), BF16),
-            pltpu.VMEM((share, width), BF16), pltpu.VMEM((share, width), BF16),
+            pltpu.VMEM((4, width, width // 2), BF16), pltpu.VMEM((4, 4, share, width // 2), BF16),
+            pltpu.VMEM((4, 4, share, width // 2), BF16), pltpu.VMEM((3, 4, share, width // 2), BF16),
+            pltpu.VMEM((4, share, piece), BF16), pltpu.VMEM((4, share, piece), BF16),
             pltpu.VMEM((units + 16, width // 2), F32), pltpu.VMEM((GROUP, units + 16, width // 2), F32),
             pltpu.VMEM((16, width // 2), F32), pltpu.VMEM((4, 16, width // 2), F32),
             pltpu.VMEM((GROUP, units, piece), F32), pltpu.VMEM((GROUP, units, piece), F32),
             pltpu.VMEM((GROUP, units, piece), F32),
-            dma((4,)), dma(()), dma(()), dma((steps,)), dma((steps,)), dma((steps,)),
+            dma((4,)), dma(()), dma(()), dma((2 * steps,)), dma((2 * steps + 1,)), dma((2 * steps + 1,)),
             dma((2, 4)), dma((2, 4)), dma((2, 3)), dma((2, 3)), dma((2,)), dma((2,)),
             dma((GROUP - 1,)), dma((GROUP - 1,)), dma((3,)), dma((3,)), dma(()), dma(()),
         ],
@@ -889,7 +953,7 @@
             jax.ShapeDtypeStruct((2 * count, width), BF16),
             jax.ShapeDtypeStruct((2 * count, width), BF16),
             jax.ShapeDtypeStruct((share, wide), F32),
-            jax.ShapeDtypeStruct((share, width), F32),
+            jax.ShapeDtypeStruct((4, share, piece), F32),
             jax.ShapeDtypeStruct((8, width), F32),
             jax.ShapeDtypeStruct((piece, table_rows), F32),
         ],

time: 253 us -> 239 us (0.945)
  Pallas kernels: 249 us -> 234 us
    pallas_call x1, Pallas kernels: 95.2 us -> 84.4 us  [attn_bwd(): pl.pallas_call(attn_bwd_kernel, name='attn_bwd', grid=(steps,), in_specs=...]
    pallas_call x1, Pallas kernels: 78.4 us -> 75.7 us  [attn_fwd(): pl.pallas_call(attn_fwd_kernel, name='attn_fwd', grid=(steps,), in_specs=...]
where the time goes in v4:
time: 239 us
  Pallas kernels  234 us (98%)
  local copies, waits for them, and re-layouts  2.92 us (1%)
    pallas_call x1, Pallas kernels, attn_bwd(): pl.pallas_call(attn_bwd_kernel, name='attn_bwd', grid=(steps,), in_specs=...  84.4 us
    pallas_call x1, Pallas kernels, attn_fwd(): pl.pallas_call(attn_fwd_kernel, name='attn_fwd', grid=(steps,), in_specs=...  75.7 us
    pallas_call x1, Pallas kernels, mlp(): pl.pallas_call(mlp_kernel, name='mlp_both', grid=(steps,), in_specs=[tok,...  64.5 us
    pallas_call x1, Pallas kernels, finish(): pl.pallas_call(finish_kernel, name='finish', grid=(count // (2 * TILE),),...  9.59 us

profile of v4, /device:TPU:0, one launch (start us, length us, event | category | flops | bytes accessed | tf_op | source)
XLA Modules:
  0.0 238.8 jit_solution(2525367642968522599)
XLA Ops:
  0.6 0.0 copy-start
  0.7 1.5 gather_fusion
  2.2 0.1 gather.11
  2.3 0.1 broadcast_in_dim.21
  2.4 0.7 broadcast_in_dim.22.ts_ref
  3.1 0.0 copy-done
  3.1 0.6 gather_fusion.1
  3.7 0.7 select_convert_fusion.emb_ref
  4.4 75.7 %attn_fwd.1 = (bf16[3,768,768]{2,1,0:T(8,128)(2,1)}, bf16[768,768]{1,0:T(8,128)(2,1)}, bf16[4,768,768]{2,1,0:T(8,128)(2,1)}, bf16[4,768,768]{2,1,0:T(8,128)(2,1)...) custom-call(bf16[3072,768]{1,0:T(8,128)(2,1)} %hidden_ref.3, ...), custom_call_target="tpu_custom_call" | custom-call | flops 12000000000 | bytes 30000000 | tf_op jit(solution)/shard_map/attn_fwd/pallas_call | solution.py:822
  80.1 64.5 %mlp_both.1 = (bf16[3072,768]{1,0:T(8,128)(2,1)}, f32[1536,768]{1,0:T(8,128)}, bf16[2,768,1536]{2,1,0:T(8,128)(2,1)}, f32[8,768]{1,0:T(8,128)}, f32[2,8,768]{2,1,0:T(8,128)}) custom-call(f32[1536,768]{1,0:T(8,128)} %get-tuple-element.54.mid_ref, bf16[3072,768]{1,0:T(8,128)(2,1)} %gy_ref.1, bf16[4,768,768]{2,1,0:T(8,128)(2,1)} %get-tuple-element.55.wu_ref, ...), custom_call_target="tpu_custom_call" | custom-call | flops 35999997952 | bytes 30000000 | tf_op jit(solution)/shard_map/mlp_both/pallas_call | solution.py:870
  144.6 84.4 %attn_bwd.1 = (bf16[3072,768]{1,0:T(8,128)(2,1)}, bf16[3072,768]{1,0:T(8,128)(2,1)}, f32[96,1536]{1,0:T(8,128)}, f32[4,96,192]{2,1,0:T(8,128)}, f32[8,768]{1,0:T(8,128)}, /*index=5*/f32[192,1000]{1,0:T(8,128)}) custom-call(bf16[3072,768]{1,0:T(8,128)(2,1)} %hidden_ref.3, f32[16,768]{1,0:T(8,128)} %select_convert_fusion.emb_ref, ...), custom_call_target="tpu_custom_call", output_to_operand_aliasing={{0}: (14, {})} | custom-call | flops 20000000000 | bytes 40000000 | tf_op jit(solution)/shard_map/attn_bwd/pallas_call | solution.py:916
  229.1 0.0 copy-start.1
  229.1 9.6 %finish.1 = (bf16[3072,768]{1,0:T(8,128)(2,1)}, bf16[3072,768]{1,0:T(8,128)(2,1)}, f32[192,1000]{1,0:T(8,128)}, f32[768]{0:T(1024)}, f32[768]{0:T(1024)}, /*inde...) custom-call(bf16[3072,768]{1,0:T(8,128)(2,1)} %get-tuple-element.64., ...), custom_call_target="tpu_custom_call" | custom-call | flops 1000000 | bytes 20000000 | tf_op jit(solution)/shard_map/finish/pallas_call | solution.py:981
  238.7 0.0 copy-done.1
  (7 shorter events, 0.1 us)
Async XLA Ops:
  0.6 2.5 %copy-start = (bf16[1000,768]{1,0:T(8,128)(2,1)S(1)}, bf16[1000,768]{1,0:T(8,128)(2,1)}, u32[]{:S(2)}) copy-start(bf16[1000,768]{1,0:T(8,128)(2,1)} %param.18) | copy-start | bytes 4608004
  229.1 9.6 %copy-start.1 = (bf16[1000,768]{1,0:T(8,128)(2,1)S(1)}, bf16[1000,768]{1,0:T(8,128)(2,1)}, u32[]{:S(2)}) copy-start(bf16[1000,768]{1,0:T(8,128)(2,1)} %param.18) | copy-start | bytes 4608004

commit v5 on v4

--- a/solution.py
+++ b/solution.py
@@ -187,13 +187,21 @@
 
     order = (0, 1, 2)
 
+    def onward(array, turns):
+        @pl.when(middle)
+        def _():
+            for turn in turns:
+                z_on(array, turn).wait_recv()
+                z_on(array, turn).start()
+
     def stage_z(array):
         for turn in order:
-            z_on(array, turn).wait_recv()
-
-            @pl.when(middle)
+            if array < 2:
+                onward(array, (turn,))
+
+            @pl.when(jnp.logical_not(middle))
             def _():
-                z_on(array, turn).start()
+                z_on(array, turn).wait_recv()
 
             for kind in (0, 1, 3):
                 push(array, turn, kind).start()
@@ -268,10 +276,13 @@
         bias_out().start()
         for turn in (1, 2, 3):
             bias_copy(turn).start()
+        onward(2, (0, 1))
         stage_near(0)
         stage_near(1)
+        onward(2, (2,))
         stage_far(0)
         stage_far(1)
+        onward(3, (0, 1))
         stage_z(2)
         settle(0)
         outof(0).wait()
@@ -283,6 +294,7 @@
 
     @pl.when(tile == 0)
     def _():
+        onward(3, (2,))
         settle(1)
         outof(1).wait()
         load(1).start()
@@ -420,11 +432,10 @@
         pre = mm(n2_ref[...], wu_ref[group]) + bu_ref[group, 0:1]
         grad_act = mm_nt(gy_ref[...], wd_ref[group])
         square = pre * pre
-        bend = jnp.tanh(pre * (GELU_C + (GELU_C * GELU_A) * square))
-        half_in = 0.5 * pre
-        up = 1.0 + bend
-        act = (half_in * up).astype(BF16)
-        slope = 0.5 * up + half_in * (1.0 - bend * bend) * (GELU_C + (3.0 * GELU_C * GELU_A) * square)
+        gate = 0.5 * jnp.tanh(pre * (GELU_C + (GELU_C * GELU_A) * square)) + 0.5
+        value = pre * gate
+        act = value.astype(BF16)
+        slope = gate + value * (1.0 - gate) * (2.0 * GELU_C + (6.0 * GELU_C * GELU_A) * square)
         grad_f = grad_act * slope
         grad_pre = grad_f.astype(BF16)
         mlp_ref[...] += mm(act, wd_ref[group])

time: 239 us -> 236 us (0.987)
  Pallas kernels: 234 us -> 231 us
where the time goes in v5:
time: 236 us
  Pallas kernels  231 us (98%)
  local copies, waits for them, and re-layouts  2.92 us (1%)
    pallas_call x1, Pallas kernels, attn_bwd(): pl.pallas_call(attn_bwd_kernel, name='attn_bwd', grid=(steps,), in_specs=...  83.9 us
    pallas_call x1, Pallas kernels, attn_fwd(): pl.pallas_call(attn_fwd_kernel, name='attn_fwd', grid=(steps,), in_specs=...  73.5 us
    pallas_call x1, Pallas kernels, mlp(): pl.pallas_call(mlp_kernel, name='mlp_both', grid=(steps,), in_specs=[tok,...  64.1 us
    pallas_call x1, Pallas kernels, finish(): pl.pallas_call(finish_kernel, name='finish', grid=(count // (2 * TILE),),...  9.59 us

profile of v5, /device:TPU:0, one launch (start us, length us, event | category | flops | bytes accessed | tf_op | source)
XLA Modules:
  0.0 235.7 jit_solution(1911861081505195936)
XLA Ops:
  0.6 0.0 copy-start
  0.7 1.5 gather_fusion
  2.2 0.1 gather.11
  2.3 0.1 broadcast_in_dim.21
  2.4 0.7 broadcast_in_dim.22.ts_ref
  3.1 0.0 copy-done
  3.1 0.6 gather_fusion.1
  3.7 0.7 select_convert_fusion.emb_ref
  4.4 73.5 %attn_fwd.1 = (bf16[3,768,768]{2,1,0:T(8,128)(2,1)}, bf16[768,768]{1,0:T(8,128)(2,1)}, bf16[4,768,768]{2,1,0:T(8,128)(2,1)}, bf16[4,768,768]{2,1,0:T(8,128)(2,1)...) custom-call(bf16[3072,768]{1,0:T(8,128)(2,1)} %hidden_ref.3, ...), custom_call_target="tpu_custom_call" | custom-call | flops 12000000000 | bytes 30000000 | tf_op jit(solution)/shard_map/attn_fwd/pallas_call | solution.py:833
  77.9 64.1 %mlp_both.1 = (bf16[3072,768]{1,0:T(8,128)(2,1)}, f32[1536,768]{1,0:T(8,128)}, bf16[2,768,1536]{2,1,0:T(8,128)(2,1)}, f32[8,768]{1,0:T(8,128)}, f32[2,8,768]{2,1,0:T(8,128)}) custom-call(f32[1536,768]{1,0:T(8,128)} %get-tuple-element.54.mid_ref, bf16[3072,768]{1,0:T(8,128)(2,1)} %gy_ref.1, bf16[4,768,768]{2,1,0:T(8,128)(2,1)} %get-tuple-element.55.wu_ref, ...), custom_call_target="tpu_custom_call" | custom-call | flops 35999997952 | bytes 30000000 | tf_op jit(solution)/shard_map/mlp_both/pallas_call | solution.py:881
  142.0 83.9 %attn_bwd.1 = (bf16[3072,768]{1,0:T(8,128)(2,1)}, bf16[3072,768]{1,0:T(8,128)(2,1)}, f32[96,1536]{1,0:T(8,128)}, f32[4,96,192]{2,1,0:T(8,128)}, f32[8,768]{1,0:T(8,128)}, /*index=5*/f32[192,1000]{1,0:T(8,128)}) custom-call(bf16[3072,768]{1,0:T(8,128)(2,1)} %hidden_ref.3, f32[16,768]{1,0:T(8,128)} %select_convert_fusion.emb_ref, ...), custom_call_target="tpu_custom_call", output_to_operand_aliasing={{0}: (14, {})} | custom-call | flops 20000000000 | bytes 40000000 | tf_op jit(solution)/shard_map/attn_bwd/pallas_call | solution.py:927
  225.9 0.0 copy-start.1
  225.9 9.6 %finish.1 = (bf16[3072,768]{1,0:T(8,128)(2,1)}, bf16[3072,768]{1,0:T(8,128)(2,1)}, f32[192,1000]{1,0:T(8,128)}, f32[768]{0:T(1024)}, f32[768]{0:T(1024)}, /*inde...) custom-call(bf16[3072,768]{1,0:T(8,128)(2,1)} %get-tuple-element.64., ...), custom_call_target="tpu_custom_call" | custom-call | flops 1000000 | bytes 20000000 | tf_op jit(solution)/shard_map/finish/pallas_call | solution.py:992
  235.5 0.0 copy-done.1
  (7 shorter events, 0.1 us)
Async XLA Ops:
  0.6 2.5 %copy-start = (bf16[1000,768]{1,0:T(8,128)(2,1)S(1)}, bf16[1000,768]{1,0:T(8,128)(2,1)}, u32[]{:S(2)}) copy-start(bf16[1000,768]{1,0:T(8,128)(2,1)} %param.18) | copy-start | bytes 4608004
  225.9 9.6 %copy-start.1 = (bf16[1000,768]{1,0:T(8,128)(2,1)S(1)}, bf16[1000,768]{1,0:T(8,128)(2,1)}, u32[]{:S(2)}) copy-start(bf16[1000,768]{1,0:T(8,128)(2,1)} %param.18) | copy-start | bytes 4608004
